TPU v7x, 32 devices: a whole 2x2x4 slice. The times are simulated.
32 devices in a mesh: seq: 32 (over z, y, x, core).
Axes of the slice: x: 2, y: 2, z: 4, core: 2. Of those that a mesh axis runs over, the one named last changes fastest.
Arguments:
- x_first: float32 [8192, 1024], P('seq'), may hold values from -6 to 6
- x_second: float32 [8192, 1024], P('seq'), may hold values from -6 to 6
- w_qk: float32 [1024, 1024], P('seq'), may hold values from -3 to 3
- w_value: float32 [1024, 1024], P('seq'), may hold values from -0.1875 to 0.1875
- w_out: float32 [1024, 1024], P('seq'), may hold values from -0.75 to 0.75
- gain_attn: float32 [1024], P('seq'), may hold values from 0.5 to 1.5
- bias_attn: float32 [1024], P('seq'), may hold values from -3 to 3
- gain_ffn: float32 [1024], P('seq'), may hold values from 0.5 to 1.5
- bias_ffn: float32 [1024], P('seq'), may hold values from -3 to 3
- w_up: float32 [1024, 4096], P('seq'), may hold values from -0.1875 to 0.1875
- bias_up: float32 [4096], P('seq'), may hold values from -3 to 3
- w_down: float32 [4096, 1024], P('seq'), may hold values from -0.09375 to 0.09375
- bias_down: float32 [1024], P('seq'), may hold values from -3 to 3
- sort_order: int32 [4, 8192], P(None, 'seq'), may hold values from 0 to 8191, as said below
- inverse: int32 [4, 8192], P(None, 'seq'), may hold values from 0 to 8191, as said below
- lengths: int32 [2], replicated, may hold values from 1 to 6144, 8192 in all
- dy_first: float32 [8192, 1024], P('seq'), may hold values from -6 to 6
- dy_second: float32 [8192, 1024], P('seq'), may hold values from -6 to 6
Outputs:
- y_first: float32 [8192, 1024], P('seq')
- y_second: float32 [8192, 1024], P('seq')
- dx_first: float32 [8192, 1024], P('seq')
- dx_second: float32 [8192, 1024], P('seq')
- grad_qk: float32 [1024, 1024], P('seq')
- grad_value: float32 [1024, 1024], P('seq')
- grad_out: float32 [1024, 1024], P('seq')
- grad_gain_attn: float32 [1024], P('seq')
- grad_bias_attn: float32 [1024], P('seq')
- grad_gain_ffn: float32 [1024], P('seq')
- grad_bias_ffn: float32 [1024], P('seq')
- grad_up: float32 [1024, 4096], P('seq')
- grad_bias_up: float32 [4096], P('seq')
- grad_down: float32 [4096, 1024], P('seq')
- grad_bias_down: float32 [1024], P('seq')
Inputs may be any that keep to these rules, and one draw needn't show every extreme that they name: Row r lists the tokens in the order in which hash round r sorts them: sorted position p holds token sort_order[r, p], each row is a permutation of the 8192 tokens. Of the 256 tokens of one device, at most 16 fall into the sorted positions from k * 256 to (k + 1) * 256 - 1 of any one device k, and this most is reached in every round. inverse[r, sort_order[r, p]] = p for every round r and position p. The lengths sum to 8192; the longest is at most 6144.
All inputs are finite; a program needn't handle non-finite values.
Results may differ from a plain program's by a relative error of at most 0.014.
The roundings to bfloat16 on the way count: a program that leaves them out, or rounds other values in their place, can miss the bound.
Values may be sent and summed in bfloat16 or wider, within the bound.
No kernel may reach another device: no remote copies, remote signals or barrier semaphores. Data moves between devices by JAX's collectives and lax.ppermute only.
A program may use at most 256 MiB of HBM per device.

v0:
```python
from functools import partial
import math

import jax
import jax.numpy as jnp
from jax import lax
from jax.sharding import PartitionSpec as P

HEADS = 8
HEAD_DIM = 128
SPAN = 64
ROUNDS = 4


EPSILON = 1e-05


def shifted(x, axis, by):
    size = lax.axis_size(axis)
    return lax.ppermute(x, axis, [(i, (i + by) % size) for i in range(size)])


def as_sent(x):
    return jax.tree.map(lambda a: a.astype(jnp.bfloat16) if a.dtype == jnp.float32 else a, x)


def layer_norm(inputs, norm_gain, norm_shift):
    centered = inputs - jnp.mean(inputs, axis=-1, keepdims=True)
    inv_std = lax.rsqrt(jnp.mean(centered * centered, axis=-1, keepdims=True) + EPSILON)
    normed = centered * inv_std
    return (normed * norm_gain + norm_shift, normed, inv_std)


def norm_back(grad_rows, normed, inv_std, norm_gain):
    grad_hat = grad_rows * norm_gain
    return inv_std * (
        grad_hat
        - jnp.mean(grad_hat, axis=-1, keepdims=True)
        - normed * jnp.mean(grad_hat * normed, axis=-1, keepdims=True)
    )


def linear(matrix_a, matrix_b):
    return jnp.dot(matrix_a, matrix_b, preferred_element_type=jnp.float32)


def inner_rows(matrix_a, matrix_b):
    return lax.dot_general(
        matrix_a, matrix_b, (((0,), (0,)), ((), ())), preferred_element_type=jnp.float32
    )


def outer_cols(matrix_a, matrix_b):
    return lax.dot_general(
        matrix_a, matrix_b, (((1,), (1,)), ((), ())), preferred_element_type=jnp.float32
    )


def segment_of(token_ids, doc_ends):
    return jnp.sum((token_ids[:, None] >= doc_ends[None, :]).astype(jnp.int32), axis=1)


def send_slots(target, tokens, devices, capacity):
    device = target // tokens
    onehot = (device[:, None] == jnp.arange(devices, dtype=jnp.int32)[None, :]).astype(jnp.int32)
    rank_in = jnp.sum(jnp.cumsum(onehot, axis=0) * onehot, axis=1) - 1
    return device * capacity + rank_in


def recv_slots(source_ids, tokens, capacity):
    device = source_ids // tokens
    earlier = (device[:, None] == device[None, :]) & (source_ids[None, :] < source_ids[:, None])
    return device * capacity + jnp.sum(earlier.astype(jnp.int32), axis=1)


def packed(inputs, slot_ids, devices, capacity):
    filled = (
        jnp.zeros((devices * capacity,) + inputs.shape[1:], inputs.dtype).at[slot_ids].set(inputs)
    )
    return filled.reshape((devices, capacity) + inputs.shape[1:])


def unpacked(received, slot_ids):
    return received.reshape((-1,) + received.shape[2:])[slot_ids]


def spanned(inputs, before):
    blocks = inputs.shape[0] // SPAN
    current = inputs.reshape((blocks, SPAN) + inputs.shape[1:])
    earlier = jnp.concatenate([before[None], current[:-1]], axis=0)
    return (current, jnp.concatenate([earlier, current], axis=1))


def arrange(got_qk, got_value, recv_slot):
    sorted_qk = unpacked(got_qk, recv_slot)
    sorted_value = unpacked(got_value, recv_slot)
    last_block = jnp.stack([sorted_qk[-SPAN:], sorted_value[-SPAN:]])
    return (sorted_qk, sorted_value, last_block)


def score_parts(sorted_rows, query_ids, before_ids, doc_ends):
    sorted_qk, sorted_value, before_qk, before_value = sorted_rows
    current, key_rows = spanned(sorted_qk, before_qk)
    _, value_keys = spanned(sorted_value, before_value)
    current_ids, key_ids = spanned(query_ids, before_ids)
    current_seg, key_seg = spanned(
        segment_of(query_ids, doc_ends), segment_of(before_ids, doc_ends)
    )
    blocks = current.shape[0]
    q_heads = current.reshape(blocks, SPAN, HEADS, HEAD_DIM)
    k_heads = key_rows.reshape(blocks, 2 * SPAN, HEADS, HEAD_DIM)
    v_heads = value_keys.reshape(blocks, 2 * SPAN, HEADS, HEAD_DIM)
    raw_dots = jnp.einsum("gihd,gjhd->ghij", q_heads, k_heads, preferred_element_type=jnp.float32)
    k_float = k_heads.astype(jnp.float32)
    key_norm = lax.rsqrt(jnp.sum(k_float * k_float, axis=-1))
    factor = jnp.transpose(key_norm, (0, 2, 1))[:, :, None, :] / math.sqrt(HEAD_DIM)
    allowed = (
        (key_ids[:, None, :] <= current_ids[:, :, None])
        & (key_seg[:, None, :] == current_seg[:, :, None])
    )[:, None]
    itself = (key_ids[:, None, :] == current_ids[:, :, None])[:, None]
    scores = jnp.where(itself, -100000.0, jnp.where(allowed, raw_dots * factor, -1000000000.0))
    log_total = jax.nn.logsumexp(scores, axis=-1)
    attn_probs = jnp.exp(scores - log_total[..., None])
    kept_mask = allowed & jnp.logical_not(itself)
    return (
        q_heads,
        k_heads,
        v_heads,
        k_float,
        key_norm,
        factor,
        kept_mask,
        raw_dots,
        attn_probs,
        log_total,
    )


def attend_out(pieces):
    (
        q_heads,
        k_heads,
        v_heads,
        k_float,
        key_norm,
        factor,
        kept_mask,
        raw_dots,
        attn_probs,
        log_total,
    ) = pieces
    blocks = q_heads.shape[0]
    out_heads = jnp.einsum(
        "ghij,gjhd->gihd",
        attn_probs.astype(jnp.bfloat16),
        v_heads,
        preferred_element_type=jnp.float32,
    )
    return (
        out_heads.reshape(blocks * SPAN, -1),
        jnp.transpose(log_total, (0, 2, 1)).reshape(blocks * SPAN, HEADS),
    )


def attend_back(pieces, grad_rows, grad_total):
    (
        q_heads,
        k_heads,
        v_heads,
        k_float,
        key_norm,
        factor,
        kept_mask,
        raw_dots,
        attn_probs,
        log_total,
    ) = pieces
    blocks = q_heads.shape[0]
    grad_heads = grad_rows.astype(jnp.bfloat16).reshape(blocks, SPAN, HEADS, HEAD_DIM)
    grad_lse = jnp.transpose(grad_total.reshape(blocks, SPAN, HEADS), (0, 2, 1))
    grad_prob = jnp.einsum(
        "gihd,gjhd->ghij", grad_heads, v_heads, preferred_element_type=jnp.float32
    )
    grad_val = jnp.einsum(
        "ghij,gihd->gjhd",
        attn_probs.astype(jnp.bfloat16),
        grad_heads,
        preferred_element_type=jnp.float32,
    )
    row_dot = jnp.sum(attn_probs * grad_prob, axis=-1, keepdims=True)
    grad_score = jnp.where(kept_mask, attn_probs * (grad_prob - row_dot + grad_lse[..., None]), 0.0)
    grad_raw = (grad_score * factor).astype(jnp.bfloat16)
    grad_norm = jnp.transpose(jnp.sum(grad_score * raw_dots, axis=2), (0, 2, 1)) / math.sqrt(
        HEAD_DIM
    )
    norm_cube = key_norm * key_norm * key_norm
    grad_query = jnp.einsum(
        "ghij,gjhd->gihd", grad_raw, k_heads, preferred_element_type=jnp.float32
    )
    grad_key = (
        jnp.einsum("ghij,gihd->gjhd", grad_raw, q_heads, preferred_element_type=jnp.float32)
        - (grad_norm * norm_cube)[..., None] * k_float
    )
    return (
        grad_query.reshape(blocks, SPAN, -1),
        grad_key.reshape(blocks, 2 * SPAN, -1),
        grad_val.reshape(blocks, 2 * SPAN, -1),
    )


def shards(
    x_first,
    x_second,
    w_qk,
    w_value,
    w_out,
    gain_attn,
    bias_attn,
    gain_ffn,
    bias_ffn,
    w_up,
    bias_up,
    w_down,
    bias_down,
    sort_order,
    inverse,
    lengths,
    dy_first,
    dy_second,
):
    devices = lax.axis_size("seq")
    tokens = x_first.shape[0]
    capacity = 2 * tokens // devices
    gathered = (
        lax.all_gather(w_qk.astype(jnp.bfloat16), "seq", axis=0, tiled=True),
        lax.all_gather(w_value.astype(jnp.bfloat16), "seq", axis=0, tiled=True),
        lax.all_gather(w_out.astype(jnp.bfloat16), "seq", axis=0, tiled=True),
        lax.all_gather(gain_attn.astype(jnp.bfloat16), "seq", axis=0, tiled=True),
        lax.all_gather(bias_attn.astype(jnp.bfloat16), "seq", axis=0, tiled=True),
        lax.all_gather(gain_ffn.astype(jnp.bfloat16), "seq", axis=0, tiled=True),
        lax.all_gather(bias_ffn.astype(jnp.bfloat16), "seq", axis=0, tiled=True),
        lax.all_gather(w_up.astype(jnp.bfloat16), "seq", axis=0, tiled=True),
        lax.all_gather(bias_up.astype(jnp.bfloat16), "seq", axis=0, tiled=True),
        lax.all_gather(w_down.astype(jnp.bfloat16), "seq", axis=0, tiled=True),
        lax.all_gather(bias_down.astype(jnp.bfloat16), "seq", axis=0, tiled=True),
    )
    m_qk, m_value, m_out, g_attn, b_attn, g_ffn, b_ffn, m_up, b_up, m_down, b_down = gathered
    gain_one = g_attn.astype(jnp.float32)
    gain_two = g_ffn.astype(jnp.float32)
    doc_ends = jnp.cumsum(lengths)
    send_list = [send_slots(inverse[turn], tokens, devices, capacity) for turn in range(ROUNDS)]
    recv_list = [recv_slots(sort_order[turn], tokens, capacity) for turn in range(ROUNDS)]
    before_ids = shifted(sort_order[:, tokens - SPAN :], "seq", 1)
    normed_one, hat_one, inv_one = layer_norm(x_second, gain_one, b_attn.astype(jnp.float32))
    normed_one = normed_one.astype(jnp.bfloat16)
    qk_rows = linear(normed_one, m_qk).astype(jnp.bfloat16)
    value_rows = linear(normed_one, m_value).astype(jnp.bfloat16)
    stashed = []
    round_outs = []
    round_lse = []
    for turn in range(ROUNDS):
        got_qk, got_value = (
            lax.all_to_all(
                packed(qk_rows, send_list[turn], devices, capacity),
                "seq",
                split_axis=0,
                concat_axis=0,
                tiled=True,
            ),
            lax.all_to_all(
                packed(value_rows, send_list[turn], devices, capacity),
                "seq",
                split_axis=0,
                concat_axis=0,
                tiled=True,
            ),
        )
        sorted_qk, sorted_value, last_block = arrange(got_qk, got_value, recv_list[turn])
        before_block = shifted(last_block, "seq", 1)
        sorted_rows = (sorted_qk, sorted_value, before_block[0], before_block[1])
        pieces = score_parts(sorted_rows, sort_order[turn], before_ids[turn], doc_ends)
        out_sorted, lse_sorted = attend_out(pieces)
        back_out, back_lse = (
            lax.all_to_all(
                packed(out_sorted, recv_list[turn], devices, capacity),
                "seq",
                split_axis=0,
                concat_axis=0,
                tiled=True,
            ),
            lax.all_to_all(
                packed(lse_sorted, recv_list[turn], devices, capacity),
                "seq",
                split_axis=0,
                concat_axis=0,
                tiled=True,
            ),
        )
        round_outs.append(unpacked(back_out, send_list[turn]))
        round_lse.append(unpacked(back_lse, send_list[turn]))
        stashed.append(sorted_rows)
    lse_all = jnp.stack(round_lse)
    out_all = jnp.stack(round_outs).reshape(ROUNDS, tokens, HEADS, HEAD_DIM)
    merge = jnp.exp(lse_all - jax.nn.logsumexp(lse_all, axis=0))
    mixed = jnp.sum(merge[..., None] * out_all, axis=0).reshape(tokens, -1).astype(jnp.bfloat16)
    y_first = x_first + linear(mixed, m_out)
    normed_two, hat_two, inv_two = layer_norm(y_first, gain_two, b_ffn.astype(jnp.float32))
    normed_two = normed_two.astype(jnp.bfloat16)
    pre_up = linear(normed_two, m_up) + b_up.astype(jnp.float32)
    hidden, gelu_back = jax.vjp(partial(jax.nn.gelu, approximate=True), pre_up)
    hidden = hidden.astype(jnp.bfloat16)
    y_second = x_second + (linear(hidden, m_down) + b_down.astype(jnp.float32))
    grad_f = dy_second.astype(jnp.bfloat16)
    grad_down = inner_rows(hidden, grad_f)
    grad_bias_down = jnp.sum(grad_f.astype(jnp.float32), axis=0)
    grad_pre = gelu_back(outer_cols(grad_f, m_down))[0].astype(jnp.bfloat16)
    grad_up = inner_rows(normed_two, grad_pre)
    grad_bias_up = jnp.sum(grad_pre.astype(jnp.float32), axis=0)
    grad_two = outer_cols(grad_pre, m_up)
    grad_gain_ffn = jnp.sum(grad_two * hat_two, axis=0)
    grad_bias_ffn = jnp.sum(grad_two, axis=0)
    dx_first = dy_first + norm_back(grad_two, hat_two, inv_two, gain_two)
    grad_attn = dx_first.astype(jnp.bfloat16)
    grad_out = inner_rows(mixed, grad_attn)
    grad_mixed = outer_cols(grad_attn, m_out).reshape(tokens, HEADS, HEAD_DIM)
    along = jnp.sum(grad_mixed[None] * out_all, axis=-1)
    grad_lse_all = merge * (along - jnp.sum(merge * along, axis=0, keepdims=True))
    grad_qk_sum = jnp.zeros((tokens, HEADS * HEAD_DIM), jnp.float32)
    grad_value_sum = jnp.zeros((tokens, HEADS * HEAD_DIM), jnp.float32)
    for turn in range(ROUNDS):
        grad_round = (merge[turn][..., None] * grad_mixed).reshape(tokens, -1)
        got_out, got_lse = (
            lax.all_to_all(
                packed(grad_round, send_list[turn], devices, capacity),
                "seq",
                split_axis=0,
                concat_axis=0,
                tiled=True,
            ),
            lax.all_to_all(
                packed(grad_lse_all[turn], send_list[turn], devices, capacity),
                "seq",
                split_axis=0,
                concat_axis=0,
                tiled=True,
            ),
        )
        sorted_grad_out = unpacked(got_out, recv_list[turn])
        sorted_grad_lse = unpacked(got_lse, recv_list[turn])
        sorted_rows = stashed[turn]
        pieces = score_parts(sorted_rows, sort_order[turn], before_ids[turn], doc_ends)
        grad_query, grad_key, grad_val = attend_back(pieces, sorted_grad_out, sorted_grad_lse)
        spill = shifted(
            jnp.stack([grad_key[0, :SPAN], grad_val[0, :SPAN]]).astype(jnp.bfloat16), "seq", -1
        ).astype(jnp.float32)
        key_add = jnp.concatenate([grad_key[1:, :SPAN], spill[0][None]], axis=0)
        value_add = jnp.concatenate([grad_val[1:, :SPAN], spill[1][None]], axis=0)
        sorted_grad_qk = (grad_query + grad_key[:, SPAN:] + key_add).reshape(tokens, -1)
        sorted_grad_value = (grad_val[:, SPAN:] + value_add).reshape(tokens, -1)
        back_qk, back_value = (
            lax.all_to_all(
                as_sent(packed(sorted_grad_qk, recv_list[turn], devices, capacity)),
                "seq",
                split_axis=0,
                concat_axis=0,
                tiled=True,
            ),
            lax.all_to_all(
                as_sent(packed(sorted_grad_value, recv_list[turn], devices, capacity)),
                "seq",
                split_axis=0,
                concat_axis=0,
                tiled=True,
            ),
        )
        grad_qk_sum = grad_qk_sum + unpacked(back_qk, send_list[turn])
        grad_value_sum = grad_value_sum + unpacked(back_value, send_list[turn])
    grad_qk_rows = grad_qk_sum.astype(jnp.bfloat16)
    grad_value_rows = grad_value_sum.astype(jnp.bfloat16)
    grad_qk = inner_rows(normed_one, grad_qk_rows)
    grad_value = inner_rows(normed_one, grad_value_rows)
    grad_one = outer_cols(grad_qk_rows, m_qk) + outer_cols(grad_value_rows, m_value)
    grad_gain_attn = jnp.sum(grad_one * hat_one, axis=0)
    grad_bias_attn = jnp.sum(grad_one, axis=0)
    dx_second = dy_second + norm_back(grad_one, hat_one, inv_one, gain_one)
    s_qk, s_value, s_out, s_gattn, s_battn, s_gffn, s_bffn, s_up, s_bup, s_down, s_bdown = (
        lax.psum_scatter(grad_qk, "seq", scatter_dimension=0, tiled=True),
        lax.psum_scatter(grad_value, "seq", scatter_dimension=0, tiled=True),
        lax.psum_scatter(grad_out, "seq", scatter_dimension=0, tiled=True),
        lax.psum_scatter(grad_gain_attn, "seq", scatter_dimension=0, tiled=True),
        lax.psum_scatter(grad_bias_attn, "seq", scatter_dimension=0, tiled=True),
        lax.psum_scatter(grad_gain_ffn, "seq", scatter_dimension=0, tiled=True),
        lax.psum_scatter(grad_bias_ffn, "seq", scatter_dimension=0, tiled=True),
        lax.psum_scatter(grad_up, "seq", scatter_dimension=0, tiled=True),
        lax.psum_scatter(grad_bias_up, "seq", scatter_dimension=0, tiled=True),
        lax.psum_scatter(grad_down, "seq", scatter_dimension=0, tiled=True),
        lax.psum_scatter(grad_bias_down, "seq", scatter_dimension=0, tiled=True),
    )
    return (
        y_first,
        y_second,
        dx_first,
        dx_second,
        s_qk,
        s_value,
        s_out,
        s_gattn,
        s_battn,
        s_gffn,
        s_bffn,
        s_up,
        s_bup,
        s_down,
        s_bdown,
    )


def solution(mesh):
    in_specs = (
        P("seq", None),
        P("seq", None),
        P("seq", None),
        P("seq", None),
        P("seq", None),
        P("seq"),
        P("seq"),
        P("seq"),
        P("seq"),
        P("seq", None),
        P("seq"),
        P("seq", None),
        P("seq"),
        P(None, "seq"),
        P(None, "seq"),
        P(),
        P("seq", None),
        P("seq", None),
    )
    out_specs = (
        P("seq", None),
        P("seq", None),
        P("seq", None),
        P("seq", None),
        P("seq", None),
        P("seq", None),
        P("seq", None),
        P("seq"),
        P("seq"),
        P("seq"),
        P("seq"),
        P("seq", None),
        P("seq"),
        P("seq", None),
        P("seq"),
    )
    return jax.shard_map(shards, mesh=mesh, in_specs=in_specs, out_specs=out_specs, check_vma=False)
```

profile of v0, /device:TPU:0, one launch (start us, length us, event | category | flops | bytes accessed | tf_op | source)
XLA Modules:
  0.0 1978.4 jit_solution(8456141559756890319)
XLA Ops:
  19.5 42.7 %all-reduce.12 = (bf16[1024]{0:T(1024)(128)(2,1)S(1)}, bf16[1024]{0:T(1024)(128)(2,1)S(1)}, bf16[1024]{0:T(1024)(128)(2,1)}, bf16[1024]{0:T(1024)(128)(2,1)}, bf16[1024]{0:T(1024)(128)(2,1)}) all-reduce(bf16[1024]{0:T(1024)(128)(2,1)S(1)} %dynamic-update-slice.1, ...), channel_id=1, replica_groups=mesh['seq'=32] {'seq'}, use_global_device_ids=true, to_apply=%add.1 | all-reduce | flops 5120 | bytes 20480
  79.5 53.8 %all-gather.7.cloned.1.call-done = bf16[1024,1024]{1,0:T(8,128)(2,1)} async-done(((bf16[32,1024]{1,0:T(8,128)(2,1)}), bf16[1024,1024]{1,0:T(8,128)(2,1)}) %all-gather.7.cloned.1.call-update) | async-done | bytes 2097168 | tf_op jit(solution)/shard_map/all_gather | solution.py:236
  144.9 23.1 %all-to-all-done = bf16[32,16,1024]{2,1,0:T(8,128)(2,1)S(1)} async-done(((bf16[32,16,1024]{2,1,0:T(8,128)(2,1)}), bf16[32,16,1024]{2,1,0:T(8,128)(2,1)S(1)}, u32[]{:S(2)}, u32[]{:S(2)}) %all-to-all-start) | async-done | bytes 1048608 | tf_op jit(solution)/shard_map/all_to_all | solution.py:264
  174.8 23.1 %all-to-all-done.4 = bf16[32,16,1024]{2,1,0:T(8,128)(2,1)S(1)} async-done(((bf16[32,16,1024]{2,1,0:T(8,128)(2,1)}), bf16[32,16,1024]{2,1,0:T(8,128)(2,1)S(1)}, u32[]{:S(2)}, u32[]{:S(2)}) %all-to-all-start.4) | async-done | bytes 1048608 | tf_op jit(solution)/shard_map/all_to_all | solution.py:271
  205.5 23.7 %all-to-all-done.3 = bf16[32,16,1024]{2,1,0:T(8,128)(2,1)} async-done(((bf16[32,16,1024]{2,1,0:T(8,128)(2,1)}), bf16[32,16,1024]{2,1,0:T(8,128)(2,1)}, u32[]{:S(2)}, u32[]{:S(2)}) %all-to-all-start.3) | async-done | bytes 1048608 | tf_op jit(solution)/shard_map/all_to_all | solution.py:264
  236.1 30.7 %all-to-all-done.7 = bf16[32,16,1024]{2,1,0:T(8,128)(2,1)} async-done(((bf16[32,16,1024]{2,1,0:T(8,128)(2,1)}), bf16[32,16,1024]{2,1,0:T(8,128)(2,1)}, u32[]{:S(2)}, u32[]{:S(2)}) %all-to-all-start.7) | async-done | bytes 1048608 | tf_op jit(solution)/shard_map/all_to_all | solution.py:271
  277.1 25.2 %all-to-all-done.6 = bf16[32,16,1024]{2,1,0:T(8,128)(2,1)} async-done(((bf16[32,16,1024]{2,1,0:T(8,128)(2,1)}), bf16[32,16,1024]{2,1,0:T(8,128)(2,1)}, u32[]{:S(2)}, u32[]{:S(2)}) %all-to-all-start.6) | async-done | bytes 1048608 | tf_op jit(solution)/shard_map/all_to_all | solution.py:264
  312.5 29.3 %all-to-all-done.10 = bf16[32,16,1024]{2,1,0:T(8,128)(2,1)} async-done(((bf16[32,16,1024]{2,1,0:T(8,128)(2,1)}), bf16[32,16,1024]{2,1,0:T(8,128)(2,1)}, u32[]{:S(2)}, u32[]{:S(2)}) %all-to-all-start.10) | async-done | bytes 1048608 | tf_op jit(solution)/shard_map/all_to_all | solution.py:271
  371.9 22.0 %all-to-all-done.9 = bf16[32,16,1024]{2,1,0:T(8,128)(2,1)} async-done(((bf16[32,16,1024]{2,1,0:T(8,128)(2,1)}), bf16[32,16,1024]{2,1,0:T(8,128)(2,1)}, u32[]{:S(2)}, u32[]{:S(2)}) %all-to-all-start.9) | async-done | bytes 1048608 | tf_op jit(solution)/shard_map/all_to_all | solution.py:264
  478.3 58.3 %all-to-all-done.12 = f32[32,16,1024]{2,1,0:T(8,128)S(1)} async-done(((f32[32,16,1024]{2,1,0:T(8,128)}), f32[32,16,1024]{2,1,0:T(8,128)S(1)}, u32[]{:S(2)}, u32[]{:S(2)}) %all-to-all-start.12) | async-done | bytes 2097184 | tf_op jit(solution)/shard_map/all_to_all | solution.py:285
  546.8 59.6 %all-to-all-done.13 = f32[32,16,1024]{2,1,0:T(8,128)} async-done(((f32[32,16,1024]{2,1,0:T(8,128)}), f32[32,16,1024]{2,1,0:T(8,128)}, u32[]{:S(2)}, u32[]{:S(2)}) %all-to-all-start.13) | async-done | bytes 2097184 | tf_op jit(solution)/shard_map/all_to_all | solution.py:285
  616.1 42.9 %all-to-all-done.14 = f32[32,16,1024]{2,1,0:T(8,128)} async-done(((f32[32,16,1024]{2,1,0:T(8,128)}), f32[32,16,1024]{2,1,0:T(8,128)}, u32[]{:S(2)}, u32[]{:S(2)}) %all-to-all-start.14) | async-done | bytes 2097184 | tf_op jit(solution)/shard_map/all_to_all | solution.py:285
  663.2 69.3 %all-gather = bf16[32,1,128]{2,1,0:T(2,128)(2,1)S(1)} all-gather(bf16[1,1,128]{2,1,0:T(2,128)(2,1)S(1)} %convert_bitcast_fusion.4), channel_id=1, replica_groups=mesh['seq'=32] {'seq'}, dimensions={0}, use_global_device_ids=true | all-gather | bytes 8448 | tf_op jit(solution)/shard_map/all_gather | solution.py:244
  776.6 12.1 convert_reduce_fusion
  852.3 42.9 %all-to-all-done.25 = f32[32,16,1024]{2,1,0:T(8,128)S(1)} async-done(((f32[32,16,1024]{2,1,0:T(8,128)}), f32[32,16,1024]{2,1,0:T(8,128)S(1)}, u32[]{:S(2)}, u32[]{:S(2)}) %all-to-all-start.25) | async-done | bytes 2097184 | tf_op jit(solution)/shard_map/all_to_all | solution.py:334
  906.5 42.9 %all-to-all-done.22 = f32[32,16,1024]{2,1,0:T(8,128)S(1)} async-done(((f32[32,16,1024]{2,1,0:T(8,128)}), f32[32,16,1024]{2,1,0:T(8,128)S(1)}, u32[]{:S(2)}, u32[]{:S(2)}) %all-to-all-start.22) | async-done | bytes 2097184 | tf_op jit(solution)/shard_map/all_to_all | solution.py:334
  960.8 42.9 %all-to-all-done.19 = f32[32,16,1024]{2,1,0:T(8,128)S(1)} async-done(((f32[32,16,1024]{2,1,0:T(8,128)}), f32[32,16,1024]{2,1,0:T(8,128)S(1)}, u32[]{:S(2)}, u32[]{:S(2)}) %all-to-all-start.19) | async-done | bytes 2097184 | tf_op jit(solution)/shard_map/all_to_all | solution.py:334
  1353.7 11.7 all-to-all-done.30
  1407.6 25.6 %all-to-all-done.28 = bf16[32,16,1024]{2,1,0:T(8,128)(2,1)} async-done(((bf16[32,16,1024]{2,1,0:T(8,128)(2,1)}), bf16[32,16,1024]{2,1,0:T(8,128)(2,1)}, u32[]{:S(2)}, u32[]{:S(2)}) %all-to-all-start.28) | async-done | bytes 1048608 | tf_op jit(solution)/shard_map/all_to_all | solution.py:369
  1452.4 10.8 fusion.197
  1477.1 38.7 %all-reduce.11 = (f32[1024]{0:T(1024)S(1)}, f32[1024]{0:T(1024)S(1)}, f32[1024]{0:T(1024)S(1)}, f32[1024]{0:T(1024)S(1)}, f32[4096]{0:T(1024)S(1)}, /*index=5*/f32[1024]{0:T(1024)S(1)}) all-reduce(f32[1024]{0:T(1024)S(1)} %get-tuple-element.17, f32[1024]{0:T(1024)S(1)} %get-tuple-element.22, ...), channel_id=5, replica_groups=mesh['seq'=32] {'seq'}, use_global_device_ids=true, to_apply=%region_93.94.clone | all-reduce | flops 9216 | bytes 73728
  1519.3 82.8 %reduce-scatter.8.cloned.1.call-done = f32[32,1024]{1,0:T(8,128)} async-done(((f32[1024,1024]{1,0:T(8,128)}), f32[32,1024]{1,0:T(8,128)}) %reduce-scatter.8.cloned.1.call-update) | async-done | bytes 131088 | tf_op jit(solution)/shard_map/reduce_scatter | solution.py:389
  1602.1 181.6 %reduce-scatter.12.cloned.1.call-done = f32[32,4096]{1,0:T(8,128)} async-done(((f32[1024,4096]{1,0:T(8,128)}), f32[32,4096]{1,0:T(8,128)}) %reduce-scatter.12.cloned.1.call-update) | async-done | bytes 524304 | tf_op jit(solution)/shard_map/reduce_scatter | solution.py:395
  1783.8 187.4 %reduce-scatter.14.cloned.1.call-done = f32[128,1024]{1,0:T(8,128)} async-done(((f32[4096,1024]{1,0:T(8,128)}), f32[128,1024]{1,0:T(8,128)}) %reduce-scatter.14.cloned.1.call-update) | async-done | bytes 524304 | tf_op jit(solution)/shard_map/reduce_scatter | solution.py:397
  (1116 shorter events, 776.2 us)
Async XLA Ops:
  7.2 63.8 %all-gather.9.cloned.1.call-start = ((), (), s32[]{:S(2)}) async-start(), calls=%async_computation.38 | async-start | bytes 2162688 | tf_op jit(solution)/shard_map/all_gather | solution.py:237
  8.9 124.4 %all-gather.7.cloned.1.call-start = ((), (), s32[]{:S(2)}) async-start(), calls=%async_computation.37 | async-start | bytes 2162688 | tf_op jit(solution)/shard_map/all_gather | solution.py:236
  76.0 62.3 %all-to-all-start.1 = ((bf16[32,16,1024]{2,1,0:T(8,128)(2,1)}), bf16[32,16,1024]{2,1,0:T(8,128)(2,1)S(1)}, u32[]{:S(2)}, u32[]{:S(2)}) async-start(bf16[32,16,1024]{2,1,0:T(8,128)(2,1)} %bitcast.18), calls=%async_computation.1 | async-start | bytes 2097152 | tf_op jit(solution)/shard_map/all_to_all | solution.py:271
  201.6 563.2 %all-gather.11.cloned.1.call-start = ((), (), s32[]{:S(2)}) async-start(), calls=%async_computation.39 | async-start | bytes 2162688 | tf_op jit(solution)/shard_map/all_gather | solution.py:238
  270.6 498.0 %all-gather.13.cloned.1.call-start = ((), (), s32[]{:S(2)}) async-start(), calls=%async_computation.40 | async-start | bytes 8650752 | tf_op jit(solution)/shard_map/all_gather | solution.py:243
  341.8 52.1 %all-to-all-start.9 = ((bf16[32,16,1024]{2,1,0:T(8,128)(2,1)}), bf16[32,16,1024]{2,1,0:T(8,128)(2,1)}, u32[]{:S(2)}, u32[]{:S(2)}) async-start(bf16[32,16,1024]{2,1,0:T(8,128)(2,1)} %bitcast.720), calls=%async_computation.9 | async-start | bytes 2097152 | tf_op jit(solution)/shard_map/all_to_all | solution.py:264
  354.7 45.7 %collective-permute-start.1 = (bf16[2,64,1024]{2,1,0:T(8,128)(2,1)}, bf16[2,64,1024]{2,1,0:T(8,128)(2,1)}, u32[]{:S(2)}, u32[]{:S(2)}) collective-permute-start(bf16[2,64,1024]{2,1,0:T(8,128)(2,1)} %pad_maximum_fusion.16), channel_id=1, source_target_pairs={{0,1},{1,2},{2,3},{3,4},{4,5},{5,6},{6,7},{7,8},{8,9},{9,10},{10,1... | collective-permute-start | bytes 786440 | tf_op jit(solution)/shard_map/ppermute | solution.py:20
  466.9 69.6 %all-to-all-start.12 = ((f32[32,16,1024]{2,1,0:T(8,128)}), f32[32,16,1024]{2,1,0:T(8,128)S(1)}, u32[]{:S(2)}, u32[]{:S(2)}) async-start(f32[32,16,1024]{2,1,0:T(8,128)} %bitcast.668), calls=%async_computation.12 | async-start | bytes 4194304 | tf_op jit(solution)/shard_map/all_to_all | solution.py:285
  470.9 305.6 %all-gather.15.cloned.1.call-start = ((), (), s32[]{:S(2)}) async-start(), calls=%async_computation.41 | async-start | bytes 8650752 | tf_op jit(solution)/shard_map/all_gather | solution.py:245
  536.5 69.9 %all-to-all-start.13 = ((f32[32,16,1024]{2,1,0:T(8,128)}), f32[32,16,1024]{2,1,0:T(8,128)}, u32[]{:S(2)}, u32[]{:S(2)}) async-start(f32[32,16,1024]{2,1,0:T(8,128)} %bitcast.669), calls=%async_computation.13 | async-start | bytes 4194304 | tf_op jit(solution)/shard_map/all_to_all | solution.py:285
  606.4 52.6 %all-to-all-start.14 = ((f32[32,16,1024]{2,1,0:T(8,128)}), f32[32,16,1024]{2,1,0:T(8,128)}, u32[]{:S(2)}, u32[]{:S(2)}) async-start(f32[32,16,1024]{2,1,0:T(8,128)} %bitcast.670), calls=%async_computation.14 | async-start | bytes 4194304 | tf_op jit(solution)/shard_map/all_to_all | solution.py:285
  659.0 96.8 %all-to-all-start.15 = ((f32[32,16,1024]{2,1,0:T(8,128)}), f32[32,16,1024]{2,1,0:T(8,128)}, u32[]{:S(2)}, u32[]{:S(2)}) async-start(f32[32,16,1024]{2,1,0:T(8,128)} %bitcast.667), calls=%async_computation.15 | async-start | bytes 4194304 | tf_op jit(solution)/shard_map/all_to_all | solution.py:285
  843.3 51.9 %all-to-all-start.25 = ((f32[32,16,1024]{2,1,0:T(8,128)}), f32[32,16,1024]{2,1,0:T(8,128)S(1)}, u32[]{:S(2)}, u32[]{:S(2)}) async-start(f32[32,16,1024]{2,1,0:T(8,128)} %bitcast.672), calls=%async_computation.25 | async-start | bytes 4194304 | tf_op jit(solution)/shard_map/all_to_all | solution.py:334
  896.5 52.9 %all-to-all-start.22 = ((f32[32,16,1024]{2,1,0:T(8,128)}), f32[32,16,1024]{2,1,0:T(8,128)S(1)}, u32[]{:S(2)}, u32[]{:S(2)}) async-start(f32[32,16,1024]{2,1,0:T(8,128)} %bitcast.673), calls=%async_computation.22 | async-start | bytes 4194304 | tf_op jit(solution)/shard_map/all_to_all | solution.py:334
  950.8 52.9 %all-to-all-start.19 = ((f32[32,16,1024]{2,1,0:T(8,128)}), f32[32,16,1024]{2,1,0:T(8,128)S(1)}, u32[]{:S(2)}, u32[]{:S(2)}) async-start(f32[32,16,1024]{2,1,0:T(8,128)} %bitcast.671), calls=%async_computation.19 | async-start | bytes 4194304 | tf_op jit(solution)/shard_map/all_to_all | solution.py:334
  1005.0 83.8 %all-to-all-start.16 = ((f32[32,16,1024]{2,1,0:T(8,128)}), f32[32,16,1024]{2,1,0:T(8,128)S(1)}, u32[]{:S(2)}, u32[]{:S(2)}) async-start(f32[32,16,1024]{2,1,0:T(8,128)} %bitcast.666), calls=%async_computation.16 | async-start | bytes 4194304 | tf_op jit(solution)/shard_map/all_to_all | solution.py:334
  1009.1 510.3 %reduce-scatter.10.cloned.1.call-start = ((), (), s32[]{:S(2)}) async-start(), calls=%async_computation.44 | async-start | bytes 4325376 | tf_op jit(solution)/shard_map/reduce_scatter | solution.py:390
  1090.2 55.6 %all-to-all-start.27 = ((bf16[32,16,1024]{2,1,0:T(8,128)(2,1)}), bf16[32,16,1024]{2,1,0:T(8,128)(2,1)S(1)}, u32[]{:S(2)}, u32[]{:S(2)}) async-start(bf16[32,16,1024]{2,1,0:T(8,128)(2,1)} %bitcast.704), calls=%async_computation.27 | async-start | bytes 2097152 | tf_op jit(solution)/shard_map/all_to_all | solution.py:362
  1145.8 64.4 %all-to-all-start.24 = ((bf16[32,16,1024]{2,1,0:T(8,128)(2,1)}), bf16[32,16,1024]{2,1,0:T(8,128)(2,1)S(1)}, u32[]{:S(2)}, u32[]{:S(2)}) async-start(bf16[32,16,1024]{2,1,0:T(8,128)(2,1)} %bitcast.705), calls=%async_computation.24 | async-start | bytes 2097152 | tf_op jit(solution)/shard_map/all_to_all | solution.py:362
  1210.2 58.3 %all-to-all-start.21 = ((bf16[32,16,1024]{2,1,0:T(8,128)(2,1)}), bf16[32,16,1024]{2,1,0:T(8,128)(2,1)S(1)}, u32[]{:S(2)}, u32[]{:S(2)}) async-start(bf16[32,16,1024]{2,1,0:T(8,128)(2,1)} %bitcast.706), calls=%async_computation.21 | async-start | bytes 2097152 | tf_op jit(solution)/shard_map/all_to_all | solution.py:362
  1303.5 215.9 %reduce-scatter.6.cloned.1.call-start = ((), (), s32[]{:S(2)}) async-start(), calls=%async_computation.42 | async-start | bytes 4325376 | tf_op jit(solution)/shard_map/reduce_scatter | solution.py:388
  1403.2 198.9 %reduce-scatter.8.cloned.1.call-start = ((), (), s32[]{:S(2)}) async-start(), calls=%async_computation.43 | async-start | bytes 4325376 | tf_op jit(solution)/shard_map/reduce_scatter | solution.py:389
  1440.0 343.7 %reduce-scatter.12.cloned.1.call-start = ((), (), s32[]{:S(2)}) async-start(), calls=%async_computation.45 | async-start | bytes 17301504 | tf_op jit(solution)/shard_map/reduce_scatter | solution.py:395
  1451.1 520.0 %reduce-scatter.14.cloned.1.call-start = ((), (), s32[]{:S(2)}) async-start(), calls=%async_computation.46 | async-start | bytes 17301504 | tf_op jit(solution)/shard_map/reduce_scatter | solution.py:397
  (291 other events, 3657.0 us)
Sparse Core Ops, SparseCore 0:
  11.5 59.4 all-gather.8
  74.4 58.8 all-gather.6
  205.3 60.3 all-gather.10
  274.0 111.8 all-gather.12
  474.3 115.0 all-gather.14
  1013.7 149.6 reduce-scatter.9
  1310.8 150.5 reduce-scatter.5
  1464.2 137.8 reduce-scatter.7
  1605.0 178.7 reduce-scatter.11
  1786.5 184.6 reduce-scatter.13
where the time goes:
time: 1990 us; the launch traced here: 1980 us
  waiting for transfers between devices  1060 us (53%)
  local copies, waits for them, and re-layouts  354 us (18%)
  blocking collectives  151 us (8%)
  starting transfers between devices  143 us (7%)
  other arithmetic  136 us (7%)
  matrix products  111 us (6%)
    reduce_scatter x1, waiting for transfers between devices, shards(): lax.psum_scatter(grad_down, 'seq', scatter_dimension=0, tiled=True)  187 us
    reduce_scatter x1, waiting for transfers between devices, shards(): lax.psum_scatter(grad_up, 'seq', scatter_dimension=0, tiled=True)  182 us
    all_to_all x4, waiting for transfers between devices, shards(): lax.all_to_all(packed(out_sorted, recv_list[turn], devices, capacity), 's...  161 us
    all_to_all x4, waiting for transfers between devices, shards(): lax.all_to_all(packed(grad_round, send_list[turn], devices, capacity), 's...  129 us
    unnamed x624, local copies, waits for them, and re-layouts  123 us
    all_to_all x4, waiting for transfers between devices, shards(): lax.all_to_all(packed(qk_rows, send_list[turn], devices, capacity), 'seq'...  94 us
    all_to_all x4, waiting for transfers between devices, shards(): lax.all_to_all(packed(value_rows, send_list[turn], devices, capacity), 's...  83.1 us
    reduce_scatter x1, waiting for transfers between devices, shards(): lax.psum_scatter(grad_value, 'seq', scatter_dimension=0, tiled=True)  82.8 us
  transfers between devices with their start and end apart: 51, of which 31 were waited for; matrix products, arithmetic and copies ran while one was open for 27% of the time, Pallas kernels for 0%

commit v1 on v0

--- a/solution.py
+++ b/solution.py
@@ -4,6 +4,8 @@
 import jax
 import jax.numpy as jnp
 from jax import lax
+from jax.experimental import pallas as pl
+from jax.experimental.pallas import tpu as pltpu
 from jax.sharding import PartitionSpec as P
 
 HEADS = 8
@@ -11,8 +13,10 @@
 SPAN = 64
 ROUNDS = 4
 
-
 EPSILON = 1e-05
+SCALE = 1.0 / math.sqrt(HEAD_DIM)
+BF = jnp.bfloat16
+F32 = jnp.float32
 
 
 def shifted(x, axis, by):
@@ -416,6 +420,500 @@
     )
 
 
+CAP_ROWS = 16
+PARTS = 8
+
+
+def dot_nn(a, b):
+    return lax.dot_general(a, b, (((1,), (0,)), ((), ())), preferred_element_type=F32)
+
+
+def dot_nt(a, b):
+    return lax.dot_general(a, b, (((1,), (1,)), ((), ())), preferred_element_type=F32)
+
+
+def dot_tn(a, b):
+    return lax.dot_general(a, b, (((0,), (0,)), ((), ())), preferred_element_type=F32)
+
+
+def hot_rows(slot_row, slots):
+    ids = lax.broadcasted_iota(jnp.int32, (slots, slot_row.shape[1]), 0).astype(F32)
+    return jnp.where(ids == slot_row, 1.0, 0.0).astype(BF)
+
+
+def hot_cols(slot_col, slots):
+    ids = lax.broadcasted_iota(jnp.int32, (slot_col.shape[0], slots), 1).astype(F32)
+    return jnp.where(ids == slot_col, 1.0, 0.0).astype(BF)
+
+
+def key_norm(keys):
+    wide = keys.astype(F32)
+    square = wide * wide
+    high = square.astype(BF)
+    low = (square - high.astype(F32)).astype(BF)
+    ones = jnp.ones((8, keys.shape[1]), BF)
+    return lax.rsqrt((dot_nt(ones, high) + dot_nt(ones, low))[0:1])
+
+
+def span_scores(queries, keys, key_ids, query_ids, query_starts):
+    raw = dot_nt(queries, keys)
+    norm = key_norm(keys)
+    factor = norm * SCALE
+    kept = (key_ids < query_ids) & (key_ids >= query_starts)
+    score = jnp.where(
+        key_ids == query_ids, -100000.0, jnp.where(kept, raw * factor, -1000000000.0)
+    )
+    top = jnp.max(score, axis=1, keepdims=True)
+    weight = jnp.exp(score - top)
+    total = jnp.sum(weight, axis=1, keepdims=True)
+    return raw, norm, factor, kept, weight, top, total
+
+
+def three_parts(wide):
+    high = wide.astype(BF).astype(F32)
+    rest = wide - high
+    mid = rest.astype(BF).astype(F32)
+    return high, mid, rest - mid
+
+
+def forward_kernel(place, x_0, x_1, x_2, x_3, info, key_ids, out, kept_rows, lanes, heads_out):
+    blocks, tokens = info.shape[0], info.shape[2]
+    slots = blocks * CAP_ROWS
+    width = x_0.shape[1]
+    spans = tokens // SPAN
+    turn = place[0]
+    rounds = ROUNDS
+
+    for offset, rows in enumerate((x_0, x_1, x_2, x_3)):
+
+        def pack(group, carry, offset=offset, rows=rows):
+            source = group * rounds + lax.bitwise_xor(turn, offset)
+            hot = hot_rows(info[source, 3:4, :], slots)
+            start = pl.multiple_of(group * tokens, tokens)
+            part = dot_nn(hot, rows[pl.ds(start, tokens), :]).astype(BF)
+            lanes[:, pl.ds(source, 1)] = part.reshape(blocks, 1, CAP_ROWS, width)
+            return carry
+
+        lax.fori_loop(0, blocks // rounds, pack, 0)
+
+    def place_rows(block, carry):
+        cols = jnp.transpose(info[block])
+        hot = hot_cols(cols[:, 2:3], slots)
+        part = dot_nn(hot, lanes[block].reshape(slots, width)).astype(BF)
+        start = pl.multiple_of(SPAN + block * tokens, SPAN)
+        kept_rows[pl.ds(start, tokens), :] = part
+        return carry
+
+    lax.fori_loop(0, blocks, place_rows, 0)
+    kept_rows[0:SPAN, :] = kept_rows[blocks * tokens : blocks * tokens + SPAN, :]
+
+    def attend(block, carry):
+        cols = jnp.transpose(info[block])
+        lane = lax.broadcasted_iota(jnp.int32, (SPAN, width - HEAD_DIM), 1)
+        pieces = []
+        for part in range(spans):
+            span = block * spans + part
+            start = pl.multiple_of(span * SPAN, SPAN)
+            rows = kept_rows[pl.ds(start, 2 * SPAN), :]
+            queries = rows[SPAN:, :HEAD_DIM]
+            ids = cols[part * SPAN : (part + 1) * SPAN]
+            raw, norm, factor, kept, weight, top, total = span_scores(
+                queries, rows[:, :HEAD_DIM], key_ids[pl.ds(span, 1), :], ids[:, 0:1], ids[:, 1:2]
+            )
+            probs = (weight * (1.0 / total)).astype(BF)
+            mixed = dot_nn(probs, rows[:, HEAD_DIM:]).astype(BF)
+            high, mid, low = three_parts(top + jnp.log(total))
+            extra = jnp.where(
+                lane == 0, high, jnp.where(lane == 1, mid, jnp.where(lane == 2, low, 0.0))
+            ).astype(BF)
+            pieces.append(jnp.concatenate([mixed, extra], axis=1))
+        heads_out[block] = jnp.concatenate(pieces, axis=0)
+        return carry
+
+    lax.fori_loop(0, blocks, attend, 0)
+
+    def unplace(block, carry):
+        hot = hot_rows(info[block, 2:3, :], slots)
+        part = dot_nn(hot, heads_out[block]).astype(BF)
+        lanes[:, pl.ds(block, 1)] = part.reshape(blocks, 1, CAP_ROWS, width)
+        return carry
+
+    lax.fori_loop(0, blocks, unplace, 0)
+
+    def unpack(source, carry):
+        cols = jnp.transpose(info[source])
+        hot = hot_cols(cols[:, 3:4], slots)
+        part = dot_nn(hot, lanes[source].reshape(slots, width))
+        out[source, 0:tokens, :] = part[:, :HEAD_DIM].astype(BF)
+        flat = jnp.transpose(part[:, HEAD_DIM:])[0:PARTS, :].astype(BF)
+        for piece in range(tokens // HEAD_DIM):
+            first = tokens + piece * PARTS
+            out[source, first : first + PARTS, :] = flat[
+                :, piece * HEAD_DIM : (piece + 1) * HEAD_DIM
+            ]
+        return carry
+
+    lax.fori_loop(0, blocks, unpack, 0)
+
+
+def backward_kernel(grads, kept_rows, info, key_ids, out, lanes, sums):
+    blocks, tokens = info.shape[0], info.shape[2]
+    slots = blocks * CAP_ROWS
+    width = kept_rows.shape[1]
+    spans = tokens // SPAN
+
+    def pack(source, carry):
+        hot = hot_rows(info[source, 3:4, :], slots)
+        flat = jnp.concatenate(
+            [
+                grads[source, tokens + piece * PARTS : tokens + (piece + 1) * PARTS, :].astype(F32)
+                for piece in range(tokens // HEAD_DIM)
+            ],
+            axis=1,
+        )
+        tall = jnp.concatenate([flat, jnp.zeros((HEAD_DIM - PARTS, tokens), F32)], axis=0)
+        rows = jnp.concatenate(
+            [grads[source, 0:tokens, :], jnp.transpose(tall).astype(BF)], axis=1
+        )
+        part = dot_nn(hot, rows).astype(BF)
+        lanes[:, pl.ds(source, 1)] = part.reshape(blocks, 1, CAP_ROWS, width)
+        return carry
+
+    lax.fori_loop(0, blocks, pack, 0)
+    sums[0:SPAN, :] = jnp.zeros((SPAN, width), F32)
+
+    def attend(block, carry):
+        cols = jnp.transpose(info[block])
+        hot = hot_cols(cols[:, 2:3], slots)
+        part_grads = dot_nn(hot, lanes[block].reshape(slots, width))
+        grad_rows = part_grads[:, :HEAD_DIM].astype(BF)
+        grad_lse = (
+            part_grads[:, HEAD_DIM : HEAD_DIM + 1]
+            + part_grads[:, HEAD_DIM + 1 : HEAD_DIM + 2]
+            + part_grads[:, HEAD_DIM + 2 : HEAD_DIM + 3]
+        )
+        held = []
+        slopes = []
+        for part in range(spans):
+            span = block * spans + part
+            start = pl.multiple_of(span * SPAN, SPAN)
+            rows = kept_rows[pl.ds(start, 2 * SPAN), :]
+            keys = rows[:, :HEAD_DIM]
+            queries = rows[SPAN:, :HEAD_DIM]
+            here = slice(part * SPAN, (part + 1) * SPAN)
+            ids = cols[here]
+            raw, norm, factor, kept, weight, top, total = span_scores(
+                queries, keys, key_ids[pl.ds(span, 1), :], ids[:, 0:1], ids[:, 1:2]
+            )
+            probs = weight * (1.0 / total)
+            grad_out = grad_rows[here]
+            grad_prob = dot_nt(grad_out, rows[:, HEAD_DIM:])
+            row_dot = jnp.sum(probs * grad_prob, axis=1, keepdims=True)
+            grad_score = jnp.where(kept, probs * (grad_prob - row_dot + grad_lse[here]), 0.0)
+            grad_raw = (grad_score * factor).astype(BF)
+            slopes.append(
+                jnp.sum(grad_score * raw, axis=0, keepdims=True) * SCALE * norm * norm * norm
+            )
+            grad_query = dot_nn(grad_raw, keys)
+            grad_key = dot_tn(grad_raw, queries)
+            grad_val = dot_tn(probs.astype(BF), grad_out)
+            held.append((start, keys, grad_query, grad_key, grad_val))
+        slopes.append(jnp.zeros((8 - spans, 2 * SPAN), F32))
+        slope_cols = jnp.transpose(jnp.concatenate(slopes, axis=0))
+        for part in range(spans):
+            start, keys, grad_query, grad_key, grad_val = held[part]
+            grad_key = grad_key - slope_cols[:, part : part + 1] * keys.astype(F32)
+            sums[pl.ds(start, SPAN), :] += jnp.concatenate(
+                [grad_key[:SPAN], grad_val[:SPAN]], axis=1
+            )
+            after = pl.multiple_of(start + SPAN, SPAN)
+            sums[pl.ds(after, SPAN), :] = jnp.concatenate(
+                [grad_query + grad_key[SPAN:], grad_val[SPAN:]], axis=1
+            )
+        return carry
+
+    lax.fori_loop(0, blocks, attend, 0)
+    sums[blocks * tokens : blocks * tokens + SPAN, :] += sums[0:SPAN, :]
+
+    def unplace(block, carry):
+        hot = hot_rows(info[block, 2:3, :], slots)
+        start = pl.multiple_of(SPAN + block * tokens, SPAN)
+        part = dot_nn(hot, sums[pl.ds(start, tokens), :].astype(BF)).astype(BF)
+        lanes[:, pl.ds(block, 1)] = part.reshape(blocks, 1, CAP_ROWS, width)
+        return carry
+
+    lax.fori_loop(0, blocks, unplace, 0)
+
+    def unpack(source, carry):
+        cols = jnp.transpose(info[source])
+        hot = hot_cols(cols[:, 3:4], slots)
+        out[source] = dot_nn(hot, lanes[source].reshape(slots, width)).astype(BF)
+        return carry
+
+    lax.fori_loop(0, blocks, unpack, 0)
+
+
+def in_vmem(count):
+    return [pl.BlockSpec(memory_space=pltpu.VMEM)] * count
+
+
+def run_forward(turn, rows, info, key_ids):
+    blocks, _, tokens = info.shape
+    width = rows[0].shape[1]
+    positions = blocks * tokens
+    extra = PARTS * tokens // HEAD_DIM
+    return pl.pallas_call(
+        forward_kernel,
+        out_shape=(
+            jax.ShapeDtypeStruct((blocks, tokens + extra, HEAD_DIM), BF),
+            jax.ShapeDtypeStruct((SPAN + positions, width), BF),
+        ),
+        in_specs=[pl.BlockSpec(memory_space=pltpu.SMEM)] + in_vmem(6),
+        out_specs=tuple(in_vmem(2)),
+        scratch_shapes=[
+            pltpu.VMEM((blocks, blocks, CAP_ROWS, width), BF),
+            pltpu.VMEM((blocks, tokens, width), BF),
+        ],
+        compiler_params=pltpu.CompilerParams(vmem_limit_bytes=48 << 20),
+        cost_estimate=pl.CostEstimate(
+            flops=20 * 10**9, bytes_accessed=12 * 10**6, transcendentals=10**6
+        ),
+        name="hash_forward",
+    )(turn, *rows, info, key_ids)
+
+
+def run_backward(grads, kept_rows, info, key_ids):
+    blocks, _, tokens = info.shape
+    width = kept_rows.shape[1]
+    positions = blocks * tokens
+    return pl.pallas_call(
+        backward_kernel,
+        out_shape=jax.ShapeDtypeStruct((blocks, tokens, width), BF),
+        in_specs=in_vmem(4),
+        out_specs=in_vmem(1)[0],
+        scratch_shapes=[
+            pltpu.VMEM((blocks, blocks, CAP_ROWS, width), BF),
+            pltpu.VMEM((SPAN + positions, width), F32),
+        ],
+        compiler_params=pltpu.CompilerParams(vmem_limit_bytes=48 << 20),
+        cost_estimate=pl.CostEstimate(
+            flops=20 * 10**9, bytes_accessed=12 * 10**6, transcendentals=10**6
+        ),
+        name="hash_backward",
+    )(grads, kept_rows, info, key_ids)
+
+
+def peers(mask):
+    size = HEADS * ROUNDS
+    return [(i, i ^ mask) for i in range(size)]
+
+
+def swap(x, mask):
+    return lax.ppermute(x, "seq", peers(mask))
+
+
+def columns():
+    return [[head * ROUNDS + turn for head in range(HEADS)] for turn in range(ROUNDS)]
+
+
+def exchange(x, groups=None):
+    return lax.all_to_all(
+        x, "seq", split_axis=0, concat_axis=0, tiled=True, axis_index_groups=groups
+    )
+
+
+def rounded(x):
+    return lax.reduce_precision(x, 8, 7)
+
+
+def split_three(wide):
+    high = rounded(wide)
+    rest = wide - high
+    mid = rounded(rest)
+    return jnp.stack([high, mid, rest - mid])
+
+
+def slots_sent(target, tokens, capacity):
+    device = target // tokens
+    early = jnp.arange(tokens)[None, :] < jnp.arange(tokens)[:, None]
+    same = (device[:, None] == device[None, :]) & early
+    return device * capacity + jnp.sum(same.astype(jnp.int32), axis=1)
+
+
+def start_of(token_ids, doc_ends):
+    ends = doc_ends[None, :]
+    return jnp.max(jnp.where(ends <= token_ids[:, None], ends, 0), axis=1)
+
+
+def shards_fast(
+    x_first,
+    x_second,
+    w_qk,
+    w_value,
+    w_out,
+    gain_attn,
+    bias_attn,
+    gain_ffn,
+    bias_ffn,
+    w_up,
+    bias_up,
+    w_down,
+    bias_down,
+    sort_order,
+    inverse,
+    lengths,
+    dy_first,
+    dy_second,
+):
+    devices = lax.axis_size("seq")
+    tokens, features = x_first.shape
+    capacity = 2 * tokens // devices
+    shard = features // devices
+    place = lax.axis_index("seq")
+    doc_ends = jnp.cumsum(lengths)
+
+    per_round = []
+    vectors = rounded(
+        jnp.concatenate([gain_attn, bias_attn, gain_ffn, bias_ffn, bias_up, bias_down])
+    )
+    vectors = jnp.pad(vectors, (0, 2 * tokens - vectors.shape[0])).reshape(2, tokens)
+    for turn in range(ROUNDS):
+        ids = sort_order[turn]
+        rows = jnp.stack(
+            [
+                ids,
+                start_of(ids, doc_ends),
+                recv_slots(ids, tokens, capacity),
+                slots_sent(inverse[turn], tokens, capacity),
+            ]
+        ).astype(F32)
+        per_round.append(jnp.concatenate([rows, vectors, jnp.zeros((2, tokens), F32)]))
+    info = jnp.tile(jnp.stack(per_round), (HEADS, 1, 1))
+    info = exchange(info)
+    got = info[:, 4:6].reshape(devices, 2 * tokens)
+
+    def vector(first, size):
+        return got[:, first : first + size].reshape(devices * size)
+
+    gain_one, shift_one = vector(0, shard), vector(shard, shard)
+    gain_two, shift_two = vector(2 * shard, shard), vector(3 * shard, shard)
+    wide = bias_up.shape[0]
+    b_up = vector(4 * shard, wide)
+    b_down = vector(4 * shard + wide, shard)
+    spans = info[:, 0].reshape(devices * tokens // SPAN, SPAN)
+    key_ids = jnp.concatenate([jnp.roll(spans, 1, axis=0), spans], axis=1)
+
+    pair = jnp.stack(
+        [w_qk.reshape(shard, HEADS, HEAD_DIM), w_value.reshape(shard, HEADS, HEAD_DIM)], axis=2
+    ).reshape(shard, 2 * features)
+    m_attn = lax.all_gather(
+        jnp.concatenate([pair, w_out], axis=1).astype(BF), "seq", axis=0, tiled=True
+    )
+    m_pair, m_out = m_attn[:, : 2 * features], m_attn[:, 2 * features :]
+    m_up = lax.all_gather(w_up.astype(BF), "seq", axis=0, tiled=True)
+    m_down = lax.all_gather(w_down.astype(BF), "seq", axis=0, tiled=True)
+
+    normed_one, hat_one, inv_one = layer_norm(x_second, gain_one, shift_one)
+    normed_one = normed_one.astype(BF)
+    rows = linear(normed_one, m_pair).astype(BF)
+    rows = jnp.transpose(rows.reshape(tokens, HEADS, 2 * HEAD_DIM), (1, 0, 2))
+    own = exchange(rows, columns()).reshape(HEADS * tokens, 2 * HEAD_DIM)
+    side = swap(own, 2)
+    all_rows = (own, swap(own, 1), side, swap(side, 1))
+    turn = (place % ROUNDS).astype(jnp.int32).reshape(1)
+    sent, kept_rows = run_forward(turn, all_rows, info, key_ids)
+    back = exchange(sent).reshape(HEADS, ROUNDS, -1, HEAD_DIM)
+    out_all = jnp.transpose(back[:, :, :tokens], (1, 2, 0, 3)).astype(F32)
+    pieces = back[:, :, tokens:].reshape(HEADS, ROUNDS, -1, PARTS, HEAD_DIM)[:, :, :, :3]
+    lse_all = jnp.sum(pieces.astype(F32), axis=3).reshape(HEADS, ROUNDS, tokens)
+    lse_all = jnp.transpose(lse_all, (1, 2, 0))
+
+    merge = jnp.exp(lse_all - jax.nn.logsumexp(lse_all, axis=0))
+    mixed = jnp.sum(merge[..., None] * out_all, axis=0).reshape(tokens, -1).astype(BF)
+    y_first = x_first + linear(mixed, m_out)
+    normed_two, hat_two, inv_two = layer_norm(y_first, gain_two, shift_two)
+    normed_two = normed_two.astype(BF)
+    pre_up = linear(normed_two, m_up) + b_up
+    hidden, gelu_back = jax.vjp(partial(jax.nn.gelu, approximate=True), pre_up)
+    hidden = hidden.astype(BF)
+    y_second = x_second + (linear(hidden, m_down) + b_down)
+    grad_f = dy_second.astype(BF)
+    grad_down = inner_rows(hidden, grad_f)
+    grad_bias_down = jnp.sum(grad_f.astype(F32), axis=0)
+    grad_pre = gelu_back(outer_cols(grad_f, m_down))[0].astype(BF)
+    grad_up = inner_rows(normed_two, grad_pre)
+    grad_bias_up = jnp.sum(grad_pre.astype(F32), axis=0)
+    grad_two = outer_cols(grad_pre, m_up)
+    grad_gain_ffn = jnp.sum(grad_two * hat_two, axis=0)
+    grad_bias_ffn = jnp.sum(grad_two, axis=0)
+    dx_first = dy_first + norm_back(grad_two, hat_two, inv_two, gain_two)
+    grad_attn = dx_first.astype(BF)
+    grad_out = inner_rows(mixed, grad_attn)
+    grad_mixed = outer_cols(grad_attn, m_out).reshape(tokens, HEADS, HEAD_DIM)
+    along = jnp.sum(grad_mixed[None] * out_all, axis=-1)
+    grad_lse_all = merge * (along - jnp.sum(merge * along, axis=0, keepdims=True))
+
+    grad_round = (merge[..., None] * grad_mixed[None]).astype(BF)
+    grad_round = jnp.transpose(grad_round, (2, 0, 1, 3)).reshape(devices, tokens, HEAD_DIM)
+    parts = split_three(jnp.transpose(grad_lse_all, (2, 0, 1)).reshape(devices, tokens))
+    parts = jnp.pad(parts, ((0, PARTS - 3), (0, 0), (0, 0)))
+    parts = jnp.transpose(parts.reshape(PARTS, devices, -1, HEAD_DIM), (1, 2, 0, 3))
+    parts = parts.reshape(devices, -1, HEAD_DIM).astype(BF)
+    got_grads = exchange(jnp.concatenate([grad_round, parts], axis=1))
+    grad_rows = exchange(run_backward(got_grads, kept_rows, info, key_ids))
+    grad_rows = grad_rows.reshape(HEADS, ROUNDS, tokens, 2 * HEAD_DIM)
+    grad_rows = jnp.sum(grad_rows.astype(F32), axis=1).astype(BF)
+    grad_rows = jnp.transpose(grad_rows, (1, 0, 2)).reshape(tokens, 2 * features)
+
+    grad_pair = inner_rows(normed_one, grad_rows)
+    grad_one = outer_cols(grad_rows, m_pair)
+    grad_gain_attn = jnp.sum(grad_one * hat_one, axis=0)
+    grad_bias_attn = jnp.sum(grad_one, axis=0)
+    dx_second = dy_second + norm_back(grad_one, hat_one, inv_one, gain_one)
+
+    def scatter(x):
+        return lax.psum_scatter(x.astype(BF), "seq", scatter_dimension=0, tiled=True).astype(F32)
+
+    s_pair = scatter(grad_pair).reshape(shard, HEADS, 2, HEAD_DIM)
+    s_qk = s_pair[:, :, 0].reshape(shard, features)
+    s_value = s_pair[:, :, 1].reshape(shard, features)
+    s_out = scatter(grad_out)
+    s_up = scatter(grad_up)
+    s_down = scatter(grad_down)
+    small = jnp.concatenate(
+        [
+            grad_gain_attn.reshape(devices, -1),
+            grad_bias_attn.reshape(devices, -1),
+            grad_gain_ffn.reshape(devices, -1),
+            grad_bias_ffn.reshape(devices, -1),
+            grad_bias_up.reshape(devices, -1),
+            grad_bias_down.reshape(devices, -1),
+        ],
+        axis=1,
+    )
+    small = jnp.sum(exchange(small[:, None]), axis=(0, 1))
+    s_gattn, s_battn, s_gffn, s_bffn = (small[i * shard : (i + 1) * shard] for i in range(4))
+    s_bup = small[4 * shard : 4 * shard + wide]
+    s_bdown = small[4 * shard + wide :]
+    return (
+        y_first,
+        y_second,
+        dx_first,
+        dx_second,
+        s_qk,
+        s_value,
+        s_out,
+        s_gattn,
+        s_battn,
+        s_gffn,
+        s_bffn,
+        s_up,
+        s_bup,
+        s_down,
+        s_bdown,
+    )
+
+
 def solution(mesh):
     in_specs = (
         P("seq", None),
@@ -454,4 +952,5 @@
         P("seq", None),
         P("seq"),
     )
-    return jax.shard_map(shards, mesh=mesh, in_specs=in_specs, out_specs=out_specs, check_vma=False)
+    fast = mesh.shape["seq"] == HEADS * ROUNDS
+    return jax.shard_map(shards_fast if fast else shards, mesh=mesh, in_specs=in_specs, out_specs=out_specs, check_vma=False)

time: 1990 us -> 961 us (0.48)
  waiting for transfers between devices: 1060 us -> 396 us
  local copies, waits for them, and re-layouts: 354 us -> 14.9 us
  Pallas kernels: 0 us -> 202 us
  starting transfers between devices: 143 us -> 16.8 us
  other arithmetic: 136 us -> 25.8 us
  blocking collectives: 151 us -> 223 us
  matrix products: 111 us -> 65.6 us
    all_to_all x32 -> x3, waiting for transfers between devices: 549 us -> 62.3 us  [exchange(): lax.all_to_all(x, 'seq', split_axis=0, concat_axis=0, tiled=True, axis_in...]
    all_to_all x0 -> x3, blocking collectives: none -> 223 us  [exchange(): lax.all_to_all(x, 'seq', split_axis=0, concat_axis=0, tiled=True, axis_in...]
    pallas_call x0 -> x2, Pallas kernels: none -> 202 us  [the longest x1 115 us: run_backward(): pl.pallas_call(backward_kernel, out_shape=jax.ShapeDtypeStruct((blocks, t...]
    reduce_scatter x5 -> x4, waiting for transfers between devices: 452 us -> 250 us  [scatter(): lax.psum_scatter(x.astype(BF), 'seq', scatter_dimension=0, tiled=True)]
    unnamed x624 -> x78, local copies, waits for them, and re-layouts: 123 us -> 4.28 us
    all_to_all x32 -> x3, starting transfers between devices: 118 us -> 16.1 us  [exchange(): lax.all_to_all(x, 'seq', split_axis=0, concat_axis=0, tiled=True, axis_in...]
    unnamed x2 -> x0, blocking collectives: 81.4 us -> none
    scatter x28 -> x0, local copies, waits for them, and re-layouts: 75.4 us -> none  [packed(): jnp.zeros((devices * capacity,) + inputs.shape[1:], inputs.dtype)]
  transfers between devices with their start and end apart: 51 -> 13, of which waited for: 31 -> 7; matrix products, arithmetic and copies ran while one was open for 27% -> 8% of each run, Pallas kernels for 0% -> 21%
where the time goes in v1:
time: 961 us; the launch traced here: 960 us
  waiting for transfers between devices  396 us (41%)
  blocking collectives  223 us (23%)
  Pallas kernels  202 us (21%)
  matrix products  65.6 us (7%)
  other arithmetic  25.8 us (3%)
  starting transfers between devices  16.8 us (2%)
  between operations  15 us (2%)
  local copies, waits for them, and re-layouts  14.9 us (2%)
    reduce_scatter x4, waiting for transfers between devices, scatter(): lax.psum_scatter(x.astype(BF), 'seq', scatter_dimension=0, tiled=True)  250 us
    all_to_all x3, blocking collectives, exchange(): lax.all_to_all(x, 'seq', split_axis=0, concat_axis=0, tiled=True, axis_in...  223 us
    pallas_call x1, Pallas kernels, run_backward(): pl.pallas_call(backward_kernel, out_shape=jax.ShapeDtypeStruct((blocks, t...  115 us
    pallas_call x1, Pallas kernels, run_forward(): pl.pallas_call(forward_kernel, out_shape=(jax.ShapeDtypeStruct((blocks, t...  87 us
    all_to_all x3, waiting for transfers between devices, exchange(): lax.all_to_all(x, 'seq', split_axis=0, concat_axis=0, tiled=True, axis_in...  62.3 us
    all_gather x1, waiting for transfers between devices, shards_fast(): lax.all_gather(jnp.concatenate([pair, w_out], axis=1).astype(BF), 'seq',...  44.8 us
    ppermute x3, waiting for transfers between devices, swap(): return lax.ppermute(x, 'seq', peers(mask))  38.9 us
    dot_general x4, matrix products, linear(): return jnp.dot(matrix_a, matrix_b, preferred_element_type=jnp.float32)  22.3 us
  transfers between devices with their start and end apart: 13, of which 7 were waited for; matrix products, arithmetic and copies ran while one was open for 8% of the time, Pallas kernels for 21%

profile of v1, /device:TPU:0, one launch (start us, length us, event | category | flops | bytes accessed | tf_op | source)
XLA Modules:
  0.0 959.6 jit_solution(625095877609711762)
XLA Ops:
  18.4 7.3 all-to-all-start
  26.1 12.9 %all-to-all-done.info = f32[32,8,256]{2,1,0:T(8,128)S(1)} async-done(((f32[32,8,256]{2,1,0:T(8,128)}), f32[32,8,256]{2,1,0:T(8,128)S(1)}, u32[]{:S(2)}, u32[]{:S(2)}) %all-to-all-start) | async-done | bytes 262176 | tf_op jit(solution)/shard_map/all_to_all | solution.py:720
  40.5 44.8 %all-gather.4.cloned.1.call-done = bf16[1024,3072]{1,0:T(8,128)(2,1)} async-done(((bf16[32,3072]{1,0:T(8,128)(2,1)}), bf16[1024,3072]{1,0:T(8,128)(2,1)}) %all-gather.4.cloned.1.call-update) | async-done | bytes 6291472 | tf_op jit(solution)/shard_map/all_gather | solution.py:809
  85.3 3.5 fusion.14
  89.0 42.5 %all_to_all.30 = bf16[8,256,256]{2,1,0:T(8,128)(2,1)S(1)} all-to-all(bf16[8,256,256]{2,1,0:T(8,128)(2,1)S(1)} %bitcast.140), channel_id=1, replica_groups={{0,4,8,12,16,20,24,28},{1,5,9,13,17,21,25,29},{2,6,10,14,18,22,26,30},{..., dimensions={0} | all-to-all | bytes 2097152 | tf_op jit(solution)/shard_map/all_to_all | solution.py:720
  131.5 35.9 %collective-permute-done.1.x_2 = bf16[2048,256]{1,0:T(8,128)(2,1)S(1)} collective-permute-done((bf16[2048,256]{1,0:T(8,128)(2,1)S(1)}, bf16[2048,256]{1,0:T(8,128)(2,1)S(1)}, u32[]{:S(2)}, u32[]{:S(2)}) %collective-permute-start.1) | collective-permute-done | bytes 1048608 | tf_op jit(solution)/shard_map/ppermute | solution.py:712
  170.7 87.0 %hash_forward.1 = (bf16[32,272,128]{2,1,0:T(8,128)(2,1)}, bf16[8256,256]{1,0:T(8,128)(2,1)}) custom-call(s32[1]{0:T(128)} %bitcast.place, bf16[2048,256]{1,0:T(8,128)(2,1)S(1)} %bitcast.133, bf16[2048,256]{1,0:T(8,128)(2,1)S(1)} %collective-permute-done.x_1, bf16[2048,256]{1,0:T(8,128)(2,1)S(1)} %collective-permute-done.1.x_2, ...), custom_call_target="tpu_custom_call" | custom-call | flops 20000000000 | bytes 12000000 | tf_op jit(solution)/shard_map/hash_forward/pallas_call | solution.py:665
  257.7 3.7 all-to-all-start.2
  263.7 49.4 %all-to-all-done.2 = bf16[32,272,128]{2,1,0:T(8,128)(2,1)} async-done(((bf16[32,272,128]{2,1,0:T(8,128)(2,1)}), bf16[32,272,128]{2,1,0:T(8,128)(2,1)}, u32[]{:S(2)}, u32[]{:S(2)}) %all-to-all-start.2) | async-done | bytes 2228256 | tf_op jit(solution)/shard_map/all_to_all | solution.py:720
  314.9 3.4 fusion.8
  321.3 7.9 convolution_add_fusion
  329.2 12.1 %convert_reduce_fusion = (f32[4096]{0:T(1024)}, bf16[256,4096]{1,0:T(8,128)(2,1)S(1)}) fusion(f32[256,4096]{1,0:T(8,128)} %convolution_add_fusion, bf16[4096,1024]{1,0:T(8,128)(2,1)} %all-gather.8.cloned.1.call-done, f32[256,1024]{1,0:T(8,128)S(1)} %copy-done.6), kind=kOutput, calls=%fused_computation.19 | convolution fusion | flops 2170810368 | bytes 15745024 | tf_op jit(solution)/shard_map/dot_general | solution.py:58
  341.3 3.2 multiply_reduce_fusion
  347.2 8.8 convolution_convert_fusion
  356.7 7.5 convolution_convert_fusion.1
  371.9 61.1 %all_to_all.31.grads = bf16[32,272,128]{2,1,0:T(8,128)(2,1)S(1)} all-to-all(bf16[32,272,128]{2,1,0:T(8,128)(2,1)S(1)} %pad_maximum_fusion), channel_id=1, replica_groups=mesh['seq'=32] {'seq'}, dimensions={0} | all-to-all | bytes 4456448 | tf_op jit(solution)/shard_map/all_to_all | solution.py:720
  433.0 115.4 %hash_backward.1 = bf16[32,256,256]{2,1,0:T(8,128)(2,1)} custom-call(bf16[32,272,128]{2,1,0:T(8,128)(2,1)S(1)} %all_to_all.31.grads, bf16[8256,256]{1,0:T(8,128)(2,1)} %get-tuple-element.18.kept_rows, f32[32,8,256]{2,1,0:T(8,128)S(1)} %all-to-all-done.info, f32[128,128]{1,0:T(8,128)S(1)} %pad_maximum_fusion.3.key_ids), custom_call_target="tpu_custom_call" | custom-call | flops 20000000000 | bytes 12000000 | tf_op jit(solution)/shard_map/hash_backward/pallas_call | solution.py:689
  548.4 119.1 %all_to_all.32 = bf16[32,256,256]{2,1,0:T(8,128)(2,1)S(1)} all-to-all(bf16[32,256,256]{2,1,0:T(8,128)(2,1)} %hash_backward.1), channel_id=1, replica_groups=mesh['seq'=32] {'seq'}, dimensions={0} | all-to-all | bytes 8388608 | tf_op jit(solution)/shard_map/all_to_all | solution.py:720
  668.7 3.5 convolution_convert_fusion.2
  673.2 3.9 multiply_reduce_fusion.1
  679.4 5.1 all-to-all-start.5
  684.6 8.5 fusion.24
  697.5 113.0 %reduce-scatter.9.cloned.1.call-done = bf16[32,4096]{1,0:T(8,128)(2,1)} async-done(((bf16[1024,4096]{1,0:T(8,128)(2,1)}), bf16[32,4096]{1,0:T(8,128)(2,1)}) %reduce-scatter.9.cloned.1.call-update) | async-done | bytes 262160 | tf_op jit(solution)/shard_map/reduce_scatter | solution.py:875
  812.3 137.2 %reduce-scatter.5.cloned.1.call-done = bf16[32,2048]{1,0:T(8,128)(2,1)} async-done(((bf16[1024,2048]{1,0:T(8,128)(2,1)}), bf16[32,2048]{1,0:T(8,128)(2,1)}) %reduce-scatter.5.cloned.1.call-update) | async-done | bytes 131088 | tf_op jit(solution)/shard_map/reduce_scatter | solution.py:875
  (220 shorter events, 47.9 us)
Async XLA Ops:
  7.2 8.0 copy-start.25
  7.3 8.1 copy-start.26
  7.3 8.2 copy-start.36
  7.3 18.4 %copy-start = (f32[256,1024]{1,0:T(8,128)S(1)}, f32[256,1024]{1,0:T(8,128)}, u32[]{:S(2)}) copy-start(f32[256,1024]{1,0:T(8,128)} %param.19) | copy-start | bytes 3145732
  7.3 78.0 %all-gather.4.cloned.1.call-start = ((), (), s32[]{:S(2)}) async-start(), calls=%async_computation.10 | async-start | bytes 6488064 | tf_op jit(solution)/shard_map/all_gather | solution.py:809
  11.4 309.9 %all-gather.6.cloned.1.call-start = ((), (), s32[]{:S(2)}) async-start(), calls=%async_computation.11 | async-start | bytes 8650752 | tf_op jit(solution)/shard_map/all_gather | solution.py:813
  13.2 315.9 %all-gather.8.cloned.1.call-start = ((), (), s32[]{:S(2)}) async-start(), calls=%async_computation.12 | async-start | bytes 8650752 | tf_op jit(solution)/shard_map/all_gather | solution.py:814
  18.4 20.6 %all-to-all-start = ((f32[32,8,256]{2,1,0:T(8,128)}), f32[32,8,256]{2,1,0:T(8,128)S(1)}, u32[]{:S(2)}, u32[]{:S(2)}) async-start(f32[32,8,256]{2,1,0:T(8,128)} %bitcast.35), calls=%async_computation | async-start | bytes 524288 | tf_op jit(solution)/shard_map/all_to_all | solution.py:720
  25.8 63.0 %copy-start.20 = (f32[256]{0:T(256)}, f32[256]{0:T(256)S(1)}, u32[]{:S(2)}) copy-start(f32[256]{0:T(256)S(1)} %broadcast_multiply_fusion.5) | copy-start | bytes 3076
  26.1 62.8 %copy-start.22 = (f32[256]{0:T(256)}, f32[256]{0:T(256)S(1)}, u32[]{:S(2)}) copy-start(f32[256]{0:T(256)S(1)} %add_rsqrt_fusion.1) | copy-start | bytes 3076
  40.5 48.4 %copy-start.10 = (f32[1024]{0:T(1024)}, f32[1024]{0:T(1024)S(1)}, u32[]{:S(2)}) copy-start(f32[1024]{0:T(1024)S(1)} %add.199) | copy-start | bytes 12292
  131.5 35.9 %collective-permute-start.1 = (bf16[2048,256]{1,0:T(8,128)(2,1)S(1)}, bf16[2048,256]{1,0:T(8,128)(2,1)S(1)}, u32[]{:S(2)}, u32[]{:S(2)}) collective-permute-start(bf16[2048,256]{1,0:T(8,128)(2,1)S(1)} %bitcast.131), channel_id=1, source_target_pairs={{0,2},{1,3},{2,0},{3,1},{4,6},{5,7},{6,4},{7,5},{8,10},{9,11},{10,... | collective-permute-start | bytes 3145736 | tf_op jit(solution)/shard_map/ppermute | solution.py:712
  131.5 36.2 %collective-permute-start = (bf16[2048,256]{1,0:T(8,128)(2,1)S(1)}, bf16[2048,256]{1,0:T(8,128)(2,1)S(1)}, u32[]{:S(2)}, u32[]{:S(2)}) collective-permute-start(bf16[2048,256]{1,0:T(8,128)(2,1)S(1)} %bitcast.132), channel_id=1, source_target_pairs={{0,1},{1,0},{2,3},{3,2},{4,5},{5,4},{6,7},{7,6},{8,9},{9,8},{10,11... | collective-permute-start | bytes 3145736 | tf_op jit(solution)/shard_map/ppermute | solution.py:712
  167.4 3.3 collective-permute-start.2
  257.7 60.8 %copy-start.5 = (f32[256,1024]{1,0:T(8,128)S(1)}, f32[256,1024]{1,0:T(8,128)}, u32[]{:S(2)}) copy-start(f32[256,1024]{1,0:T(8,128)} %param.18) | copy-start | bytes 3145732
  257.7 55.4 %all-to-all-start.2 = ((bf16[32,272,128]{2,1,0:T(8,128)(2,1)}), bf16[32,272,128]{2,1,0:T(8,128)(2,1)}, u32[]{:S(2)}, u32[]{:S(2)}) async-start(bf16[32,272,128]{2,1,0:T(8,128)(2,1)} %get-tuple-element.17), calls=%async_computation.2 | async-start | bytes 4456448 | tf_op jit(solution)/shard_map/all_to_all | solution.py:720
  261.4 431.6 %reduce-scatter.7.cloned.1.call-start = ((), (), s32[]{:S(2)}) async-start(), calls=%async_computation.14 | async-start | bytes 2162688 | tf_op jit(solution)/shard_map/reduce_scatter | solution.py:875
  321.0 35.1 %copy-start.2 = (f32[256,1024]{1,0:T(8,128)}, f32[256,1024]{1,0:T(8,128)S(1)}, u32[]{:S(2)}) copy-start(f32[256,1024]{1,0:T(8,128)S(1)} %get-tuple-element.69) | copy-start | bytes 3145732
  329.2 12.1 %copy-start.35 = (bf16[1024,4096]{1,0:T(8,128)(2,1)S(1)}, bf16[1024,4096]{1,0:T(8,128)(2,1)}, u32[]{:S(2)}) copy-start(bf16[1024,4096]{1,0:T(8,128)(2,1)} %all-gather.6.cloned.1.call-done) | copy-start | bytes 25165828
  344.8 19.4 %copy-start.3 = (f32[256,1024]{1,0:T(8,128)}, f32[256,1024]{1,0:T(8,128)S(1)}, u32[]{:S(2)}) copy-start(f32[256,1024]{1,0:T(8,128)S(1)} %multiply_add_fusion.1) | copy-start | bytes 3145732
  346.9 348.8 %reduce-scatter.11.cloned.1.call-start = ((), (), s32[]{:S(2)}) async-start(), calls=%async_computation.16 | async-start | bytes 8650752 | tf_op jit(solution)/shard_map/reduce_scatter | solution.py:875
  356.0 454.4 %reduce-scatter.9.cloned.1.call-start = ((), (), s32[]{:S(2)}) async-start(), calls=%async_computation.15 | async-start | bytes 8650752 | tf_op jit(solution)/shard_map/reduce_scatter | solution.py:875
  364.2 585.3 %reduce-scatter.5.cloned.1.call-start = ((), (), s32[]{:S(2)}) async-start(), calls=%async_computation.13 | async-start | bytes 4325376 | tf_op jit(solution)/shard_map/reduce_scatter | solution.py:875
  679.4 15.1 %all-to-all-start.5 = ((f32[32,1,288]{2,1,0:T(1,128)}), f32[32,1,288]{2,1,0:T(1,128)S(1)}, u32[]{:S(2)}, u32[]{:S(2)}) async-start(f32[32,1,288]{2,1,0:T(1,128)} %broadcast_in_dim.31), calls=%async_computation.7 | async-start | bytes 98304 | tf_op jit(solution)/shard_map/all_to_all | solution.py:720
  (26 other events, 93.5 us)
Sparse Core Ops, SparseCore 0:
  11.6 73.7 all-gather.3
  88.8 91.0 all-gather.5
  183.2 77.4 all-gather.7
  347.0 139.1 reduce-scatter.6
  488.5 169.2 reduce-scatter.10
  660.0 150.4 reduce-scatter.8
  812.8 136.5 reduce-scatter.4

commit v2 on v1

--- a/solution.py
+++ b/solution.py
@@ -455,9 +455,7 @@
     return lax.rsqrt((dot_nt(ones, high) + dot_nt(ones, low))[0:1])
 
 
-def span_scores(queries, keys, key_ids, query_ids, query_starts):
-    raw = dot_nt(queries, keys)
-    norm = key_norm(keys)
+def span_softmax(raw, norm, key_ids, query_ids, query_starts):
     factor = norm * SCALE
     kept = (key_ids < query_ids) & (key_ids >= query_starts)
     score = jnp.where(
@@ -466,7 +464,7 @@
     top = jnp.max(score, axis=1, keepdims=True)
     weight = jnp.exp(score - top)
     total = jnp.sum(weight, axis=1, keepdims=True)
-    return raw, norm, factor, kept, weight, top, total
+    return factor, kept, weight, top, total
 
 
 def three_parts(wide):
@@ -494,7 +492,7 @@
             lanes[:, pl.ds(source, 1)] = part.reshape(blocks, 1, CAP_ROWS, width)
             return carry
 
-        lax.fori_loop(0, blocks // rounds, pack, 0)
+        lax.fori_loop(0, blocks // rounds, pack, 0, unroll=4)
 
     def place_rows(block, carry):
         cols = jnp.transpose(info[block])
@@ -504,30 +502,36 @@
         kept_rows[pl.ds(start, tokens), :] = part
         return carry
 
-    lax.fori_loop(0, blocks, place_rows, 0)
+    lax.fori_loop(0, blocks, place_rows, 0, unroll=4)
     kept_rows[0:SPAN, :] = kept_rows[blocks * tokens : blocks * tokens + SPAN, :]
 
     def attend(block, carry):
         cols = jnp.transpose(info[block])
         lane = lax.broadcasted_iota(jnp.int32, (SPAN, width - HEAD_DIM), 1)
-        pieces = []
+        first = []
         for part in range(spans):
             span = block * spans + part
             start = pl.multiple_of(span * SPAN, SPAN)
             rows = kept_rows[pl.ds(start, 2 * SPAN), :]
-            queries = rows[SPAN:, :HEAD_DIM]
+            keys = rows[:, :HEAD_DIM]
+            first.append((rows, dot_nt(rows[SPAN:, :HEAD_DIM], keys), key_norm(keys)))
+        second = []
+        for part in range(spans):
+            rows, raw, norm = first[part]
             ids = cols[part * SPAN : (part + 1) * SPAN]
-            raw, norm, factor, kept, weight, top, total = span_scores(
-                queries, rows[:, :HEAD_DIM], key_ids[pl.ds(span, 1), :], ids[:, 0:1], ids[:, 1:2]
+            factor, kept, weight, top, total = span_softmax(
+                raw, norm, key_ids[pl.ds(block * spans + part, 1), :], ids[:, 0:1], ids[:, 1:2]
             )
-            probs = (weight * (1.0 / total)).astype(BF)
-            mixed = dot_nn(probs, rows[:, HEAD_DIM:]).astype(BF)
             high, mid, low = three_parts(top + jnp.log(total))
             extra = jnp.where(
                 lane == 0, high, jnp.where(lane == 1, mid, jnp.where(lane == 2, low, 0.0))
             ).astype(BF)
-            pieces.append(jnp.concatenate([mixed, extra], axis=1))
-        heads_out[block] = jnp.concatenate(pieces, axis=0)
+            second.append(((weight * (1.0 / total)).astype(BF), extra))
+        for part in range(spans):
+            probs, extra = second[part]
+            here = slice(part * SPAN, (part + 1) * SPAN)
+            heads_out[block, here, :HEAD_DIM] = dot_nn(probs, first[part][0][:, HEAD_DIM:]).astype(BF)
+            heads_out[block, here, HEAD_DIM:] = extra
         return carry
 
     lax.fori_loop(0, blocks, attend, 0)
@@ -538,7 +542,7 @@
         lanes[:, pl.ds(block, 1)] = part.reshape(blocks, 1, CAP_ROWS, width)
         return carry
 
-    lax.fori_loop(0, blocks, unplace, 0)
+    lax.fori_loop(0, blocks, unplace, 0, unroll=4)
 
     def unpack(source, carry):
         cols = jnp.transpose(info[source])
@@ -553,10 +557,10 @@
             ]
         return carry
 
-    lax.fori_loop(0, blocks, unpack, 0)
-
-
-def backward_kernel(grads, kept_rows, info, key_ids, out, lanes, sums):
+    lax.fori_loop(0, blocks, unpack, 0, unroll=4)
+
+
+def backward_kernel(place, grads, kept_rows, info, key_ids, out_0, out_1, out_2, out_3, lanes, sums):
     blocks, tokens = info.shape[0], info.shape[2]
     slots = blocks * CAP_ROWS
     width = kept_rows.shape[1]
@@ -579,7 +583,7 @@
         lanes[:, pl.ds(source, 1)] = part.reshape(blocks, 1, CAP_ROWS, width)
         return carry
 
-    lax.fori_loop(0, blocks, pack, 0)
+    lax.fori_loop(0, blocks, pack, 0, unroll=4)
     sums[0:SPAN, :] = jnp.zeros((SPAN, width), F32)
 
     def attend(block, carry):
@@ -592,32 +596,46 @@
             + part_grads[:, HEAD_DIM + 1 : HEAD_DIM + 2]
             + part_grads[:, HEAD_DIM + 2 : HEAD_DIM + 3]
         )
-        held = []
-        slopes = []
+        first = []
         for part in range(spans):
             span = block * spans + part
             start = pl.multiple_of(span * SPAN, SPAN)
             rows = kept_rows[pl.ds(start, 2 * SPAN), :]
             keys = rows[:, :HEAD_DIM]
             queries = rows[SPAN:, :HEAD_DIM]
+            grad_out = grad_rows[part * SPAN : (part + 1) * SPAN]
+            raw = dot_nt(queries, keys)
+            grad_prob = dot_nt(grad_out, rows[:, HEAD_DIM:])
+            first.append((start, keys, queries, grad_out, raw, grad_prob, key_norm(keys)))
+        second = []
+        slopes = []
+        for part in range(spans):
+            start, keys, queries, grad_out, raw, grad_prob, norm = first[part]
             here = slice(part * SPAN, (part + 1) * SPAN)
             ids = cols[here]
-            raw, norm, factor, kept, weight, top, total = span_scores(
-                queries, keys, key_ids[pl.ds(span, 1), :], ids[:, 0:1], ids[:, 1:2]
+            factor, kept, weight, top, total = span_softmax(
+                raw, norm, key_ids[pl.ds(block * spans + part, 1), :], ids[:, 0:1], ids[:, 1:2]
             )
             probs = weight * (1.0 / total)
-            grad_out = grad_rows[here]
-            grad_prob = dot_nt(grad_out, rows[:, HEAD_DIM:])
             row_dot = jnp.sum(probs * grad_prob, axis=1, keepdims=True)
             grad_score = jnp.where(kept, probs * (grad_prob - row_dot + grad_lse[here]), 0.0)
-            grad_raw = (grad_score * factor).astype(BF)
             slopes.append(
                 jnp.sum(grad_score * raw, axis=0, keepdims=True) * SCALE * norm * norm * norm
             )
-            grad_query = dot_nn(grad_raw, keys)
-            grad_key = dot_tn(grad_raw, queries)
-            grad_val = dot_tn(probs.astype(BF), grad_out)
-            held.append((start, keys, grad_query, grad_key, grad_val))
+            second.append(((grad_score * factor).astype(BF), probs.astype(BF)))
+        held = []
+        for part in range(spans):
+            start, keys, queries, grad_out = first[part][:4]
+            grad_raw, probs = second[part]
+            held.append(
+                (
+                    start,
+                    keys,
+                    dot_nn(grad_raw, keys),
+                    dot_tn(grad_raw, queries),
+                    dot_tn(probs, grad_out),
+                )
+            )
         slopes.append(jnp.zeros((8 - spans, 2 * SPAN), F32))
         slope_cols = jnp.transpose(jnp.concatenate(slopes, axis=0))
         for part in range(spans):
@@ -642,15 +660,20 @@
         lanes[:, pl.ds(block, 1)] = part.reshape(blocks, 1, CAP_ROWS, width)
         return carry
 
-    lax.fori_loop(0, blocks, unplace, 0)
-
-    def unpack(source, carry):
-        cols = jnp.transpose(info[source])
-        hot = hot_cols(cols[:, 3:4], slots)
-        out[source] = dot_nn(hot, lanes[source].reshape(slots, width)).astype(BF)
-        return carry
-
-    lax.fori_loop(0, blocks, unpack, 0)
+    lax.fori_loop(0, blocks, unplace, 0, unroll=4)
+
+    for offset, out in enumerate((out_0, out_1, out_2, out_3)):
+
+        def unpack(group, carry, offset=offset, out=out):
+            source = group * ROUNDS + lax.bitwise_xor(place[0], offset)
+            cols = jnp.transpose(info[source])
+            hot = hot_cols(cols[:, 3:4], slots)
+            start = pl.multiple_of(group * tokens, tokens)
+            part = dot_nn(hot, lanes[source].reshape(slots, width))
+            out[pl.ds(start, tokens), :] = part.astype(BF)
+            return carry
+
+        lax.fori_loop(0, blocks // ROUNDS, unpack, 0, unroll=4)
 
 
 def in_vmem(count):
@@ -682,15 +705,15 @@
     )(turn, *rows, info, key_ids)
 
 
-def run_backward(grads, kept_rows, info, key_ids):
+def run_backward(turn, grads, kept_rows, info, key_ids):
     blocks, _, tokens = info.shape
     width = kept_rows.shape[1]
     positions = blocks * tokens
     return pl.pallas_call(
         backward_kernel,
-        out_shape=jax.ShapeDtypeStruct((blocks, tokens, width), BF),
-        in_specs=in_vmem(4),
-        out_specs=in_vmem(1)[0],
+        out_shape=(jax.ShapeDtypeStruct((positions // ROUNDS, width), BF),) * ROUNDS,
+        in_specs=[pl.BlockSpec(memory_space=pltpu.SMEM)] + in_vmem(4),
+        out_specs=tuple(in_vmem(ROUNDS)),
         scratch_shapes=[
             pltpu.VMEM((blocks, blocks, CAP_ROWS, width), BF),
             pltpu.VMEM((SPAN + positions, width), F32),
@@ -700,7 +723,7 @@
             flops=20 * 10**9, bytes_accessed=12 * 10**6, transcendentals=10**6
         ),
         name="hash_backward",
-    )(grads, kept_rows, info, key_ids)
+    )(turn, grads, kept_rows, info, key_ids)
 
 
 def peers(mask):
@@ -714,6 +737,21 @@
 
 def columns():
     return [[head * ROUNDS + turn for head in range(HEADS)] for turn in range(ROUNDS)]
+
+
+def rows_of():
+    return [[head * ROUNDS + turn for turn in range(ROUNDS)] for head in range(HEADS)]
+
+
+def gather_group(x):
+    side = swap(x, 2)
+    return (x, swap(x, 1), side, swap(side, 1))
+
+
+def sum_group(parts):
+    near = parts[0] + swap(parts[1].astype(BF), 1).astype(F32)
+    far = parts[2] + swap(parts[3].astype(BF), 1).astype(F32)
+    return near + swap(far.astype(BF), 2).astype(F32)
 
 
 def exchange(x, groups=None):
@@ -806,20 +844,33 @@
     pair = jnp.stack(
         [w_qk.reshape(shard, HEADS, HEAD_DIM), w_value.reshape(shard, HEADS, HEAD_DIM)], axis=2
     ).reshape(shard, 2 * features)
-    m_attn = lax.all_gather(
-        jnp.concatenate([pair, w_out], axis=1).astype(BF), "seq", axis=0, tiled=True
-    )
-    m_pair, m_out = m_attn[:, : 2 * features], m_attn[:, 2 * features :]
-    m_up = lax.all_gather(w_up.astype(BF), "seq", axis=0, tiled=True)
-    m_down = lax.all_gather(w_down.astype(BF), "seq", axis=0, tiled=True)
+    m_pair = lax.all_gather(pair.astype(BF), "seq", axis=0, tiled=True)
+    m_out = lax.all_gather(w_out.astype(BF), "seq", axis=0, tiled=True)
+    up_cols = jnp.transpose(
+        w_up.astype(BF).reshape(shard, HEADS, ROUNDS, wide), (2, 0, 1, 3)
+    ).reshape(ROUNDS, shard, HEADS * wide)
+    up_cols = exchange(up_cols, rows_of()).reshape(ROUNDS * shard, HEADS * wide)
+    m_ffn = lax.all_gather(
+        jnp.concatenate([up_cols, w_down.astype(BF)], axis=1),
+        "seq",
+        axis=0,
+        tiled=True,
+        axis_index_groups=columns(),
+    )
+    m_up, m_down = m_ffn[:, : HEADS * wide], m_ffn[:, HEADS * wide :]
+    b_up = lax.dynamic_index_in_dim(
+        b_up.reshape(HEADS, ROUNDS, wide), place % ROUNDS, axis=1, keepdims=False
+    ).reshape(HEADS * wide)
 
     normed_one, hat_one, inv_one = layer_norm(x_second, gain_one, shift_one)
     normed_one = normed_one.astype(BF)
     rows = linear(normed_one, m_pair).astype(BF)
     rows = jnp.transpose(rows.reshape(tokens, HEADS, 2 * HEAD_DIM), (1, 0, 2))
     own = exchange(rows, columns()).reshape(HEADS * tokens, 2 * HEAD_DIM)
-    side = swap(own, 2)
-    all_rows = (own, swap(own, 1), side, swap(side, 1))
+    all_rows = gather_group(own)
+    normed_col = lax.all_gather(
+        normed_one, "seq", axis=0, tiled=True, axis_index_groups=columns()
+    )
     turn = (place % ROUNDS).astype(jnp.int32).reshape(1)
     sent, kept_rows = run_forward(turn, all_rows, info, key_ids)
     back = exchange(sent).reshape(HEADS, ROUNDS, -1, HEAD_DIM)
@@ -833,22 +884,42 @@
     y_first = x_first + linear(mixed, m_out)
     normed_two, hat_two, inv_two = layer_norm(y_first, gain_two, shift_two)
     normed_two = normed_two.astype(BF)
-    pre_up = linear(normed_two, m_up) + b_up
+    grad_f = dy_second.astype(BF)
+    grad_f_all = jnp.concatenate(gather_group(grad_f))
+    normed_all = jnp.concatenate(gather_group(normed_two))
+    pre_up = linear(normed_all, m_up) + b_up
     hidden, gelu_back = jax.vjp(partial(jax.nn.gelu, approximate=True), pre_up)
     hidden = hidden.astype(BF)
-    y_second = x_second + (linear(hidden, m_down) + b_down)
-    grad_f = dy_second.astype(BF)
-    grad_down = inner_rows(hidden, grad_f)
+    branch = sum_group(linear(hidden, m_down).reshape(ROUNDS, tokens, features))
+    y_second = x_second + (branch + b_down)
+    grad_down = inner_rows(hidden, grad_f_all)
     grad_bias_down = jnp.sum(grad_f.astype(F32), axis=0)
-    grad_pre = gelu_back(outer_cols(grad_f, m_down))[0].astype(BF)
-    grad_up = inner_rows(normed_two, grad_pre)
+    grad_pre = gelu_back(outer_cols(grad_f_all, m_down))[0].astype(BF)
+    grad_up = inner_rows(normed_all, grad_pre)
     grad_bias_up = jnp.sum(grad_pre.astype(F32), axis=0)
-    grad_two = outer_cols(grad_pre, m_up)
+    grad_two = sum_group(outer_cols(grad_pre, m_up).reshape(ROUNDS, tokens, features))
     grad_gain_ffn = jnp.sum(grad_two * hat_two, axis=0)
     grad_bias_ffn = jnp.sum(grad_two, axis=0)
     dx_first = dy_first + norm_back(grad_two, hat_two, inv_two, gain_two)
     grad_attn = dx_first.astype(BF)
     grad_out = inner_rows(mixed, grad_attn)
+    fourth = features // ROUNDS
+    grad_out = sum_group(
+        [
+            lax.dynamic_slice_in_dim(grad_out, ((place % ROUNDS) ^ near) * fourth, fourth, axis=1)
+            for near in range(ROUNDS)
+        ]
+    )
+    merged = jnp.concatenate([x.astype(BF) for x in (grad_up, grad_out, grad_down)], axis=1)
+    merged = lax.psum_scatter(
+        merged, "seq", scatter_dimension=0, tiled=True, axis_index_groups=columns()
+    )
+    half = HEADS * wide
+    s_down = merged[:, half + fourth :].astype(F32)
+    merged = exchange(merged[:, : half + fourth].reshape(ROUNDS, shard, -1), rows_of())
+    s_up = jnp.transpose(merged[:, :, :half].reshape(ROUNDS, shard, HEADS, wide), (1, 2, 0, 3))
+    s_up = s_up.reshape(shard, ROUNDS * half).astype(F32)
+    s_out = jnp.transpose(merged[:, :, half:], (1, 0, 2)).reshape(shard, features).astype(F32)
     grad_mixed = outer_cols(grad_attn, m_out).reshape(tokens, HEADS, HEAD_DIM)
     along = jnp.sum(grad_mixed[None] * out_all, axis=-1)
     grad_lse_all = merge * (along - jnp.sum(merge * along, axis=0, keepdims=True))
@@ -860,26 +931,26 @@
     parts = jnp.transpose(parts.reshape(PARTS, devices, -1, HEAD_DIM), (1, 2, 0, 3))
     parts = parts.reshape(devices, -1, HEAD_DIM).astype(BF)
     got_grads = exchange(jnp.concatenate([grad_round, parts], axis=1))
-    grad_rows = exchange(run_backward(got_grads, kept_rows, info, key_ids))
-    grad_rows = grad_rows.reshape(HEADS, ROUNDS, tokens, 2 * HEAD_DIM)
-    grad_rows = jnp.sum(grad_rows.astype(F32), axis=1).astype(BF)
+    grad_head = run_backward(turn, got_grads, kept_rows, info, key_ids)
+    grad_head = sum_group([x.astype(F32) for x in grad_head]).astype(BF)
+    grad_rows = exchange(grad_head.reshape(HEADS, tokens, 2 * HEAD_DIM), columns())
     grad_rows = jnp.transpose(grad_rows, (1, 0, 2)).reshape(tokens, 2 * features)
 
-    grad_pair = inner_rows(normed_one, grad_rows)
+    s_pair = exchange(
+        inner_rows(normed_col, grad_head).astype(BF).reshape(devices, shard, 2 * HEAD_DIM)
+    )
+    s_pair = jnp.sum(
+        s_pair.reshape(HEADS, ROUNDS, shard, 2, HEAD_DIM).astype(F32), axis=1
+    ).transpose(2, 1, 0, 3)
+    s_qk = s_pair[0].reshape(shard, features)
+    s_value = s_pair[1].reshape(shard, features)
     grad_one = outer_cols(grad_rows, m_pair)
     grad_gain_attn = jnp.sum(grad_one * hat_one, axis=0)
     grad_bias_attn = jnp.sum(grad_one, axis=0)
     dx_second = dy_second + norm_back(grad_one, hat_one, inv_one, gain_one)
 
-    def scatter(x):
-        return lax.psum_scatter(x.astype(BF), "seq", scatter_dimension=0, tiled=True).astype(F32)
-
-    s_pair = scatter(grad_pair).reshape(shard, HEADS, 2, HEAD_DIM)
-    s_qk = s_pair[:, :, 0].reshape(shard, features)
-    s_value = s_pair[:, :, 1].reshape(shard, features)
-    s_out = scatter(grad_out)
-    s_up = scatter(grad_up)
-    s_down = scatter(grad_down)
+    is_mine = (jnp.arange(ROUNDS) == place % ROUNDS).astype(F32)
+    grad_bias_up = grad_bias_up.reshape(HEADS, 1, wide) * is_mine[None, :, None]
     small = jnp.concatenate(
         [
             grad_gain_attn.reshape(devices, -1),

time: 961 us -> 635 us (0.66)
  blocking collectives: 223 us -> 30 us
  waiting for transfers between devices: 396 us -> 296 us
  Pallas kernels: 202 us -> 105 us
  starting transfers between devices: 16.8 us -> 52.3 us
  local copies, waits for them, and re-layouts: 14.9 us -> 38.6 us
  matrix products: 65.6 us -> 47.8 us
  other arithmetic: 25.8 us -> 41.8 us
    reduce_scatter x4 -> x1, waiting for transfers between devices: 250 us -> 0.02 us  [shards_fast(): lax.psum_scatter(merged, 'seq', scatter_dimension=0, tiled=True, axis_ind...]
    all_to_all x3 -> x1, blocking collectives: 223 us -> 30 us  [exchange(): lax.all_to_all(x, 'seq', split_axis=0, concat_axis=0, tiled=True, axis_in...]
    all_to_all x3 -> x8, waiting for transfers between devices: 62.3 us -> 160 us  [exchange(): lax.all_to_all(x, 'seq', split_axis=0, concat_axis=0, tiled=True, axis_in...]
    pallas_call x1, Pallas kernels: 115 us -> 58.9 us  [run_backward(): pl.pallas_call(backward_kernel, out_shape=(jax.ShapeDtypeStruct((position...]
    ppermute x3 -> x21, waiting for transfers between devices: 38.9 us -> 94.9 us  [swap(): return lax.ppermute(x, 'seq', peers(mask))]
    pallas_call x1, Pallas kernels: 87 us -> 45.7 us  [run_forward(): pl.pallas_call(forward_kernel, out_shape=(jax.ShapeDtypeStruct((blocks, t...]
    all_to_all x3 -> x8, starting transfers between devices: 16.1 us -> 40 us  [exchange(): lax.all_to_all(x, 'seq', split_axis=0, concat_axis=0, tiled=True, axis_in...]
    ppermute x3 -> x21, starting transfers between devices: 0.01 us -> 11.5 us  [swap(): return lax.ppermute(x, 'seq', peers(mask))]
  transfers between devices with their start and end apart: 13 -> 34, of which waited for: 7 -> 17; matrix products, arithmetic and copies ran while one was open for 8% -> 17% of each run, Pallas kernels for 21% -> 17%
where the time goes in v2:
time: 635 us; the launch traced here: 626 us
  waiting for transfers between devices  296 us (47%)
  Pallas kernels  105 us (17%)
  starting transfers between devices  52.3 us (8%)
  matrix products  47.8 us (8%)
  other arithmetic  41.8 us (7%)
  local copies, waits for them, and re-layouts  38.6 us (6%)
  blocking collectives  30 us (5%)
  between operations  15.2 us (2%)
    all_to_all x8, waiting for transfers between devices, exchange(): lax.all_to_all(x, 'seq', split_axis=0, concat_axis=0, tiled=True, axis_in...  160 us
    ppermute x21, waiting for transfers between devices, swap(): return lax.ppermute(x, 'seq', peers(mask))  94.9 us
    pallas_call x1, Pallas kernels, run_backward(): pl.pallas_call(backward_kernel, out_shape=(jax.ShapeDtypeStruct((position...  58.9 us
    pallas_call x1, Pallas kernels, run_forward(): pl.pallas_call(forward_kernel, out_shape=(jax.ShapeDtypeStruct((blocks, t...  45.7 us
    all_gather x1, waiting for transfers between devices, shards_fast(): m_pair = lax.all_gather(pair.astype(BF), 'seq', axis=0, tiled=True)  40.2 us
    all_to_all x8, starting transfers between devices, exchange(): lax.all_to_all(x, 'seq', split_axis=0, concat_axis=0, tiled=True, axis_in...  40 us
    all_to_all x1, blocking collectives, exchange(): lax.all_to_all(x, 'seq', split_axis=0, concat_axis=0, tiled=True, axis_in...  30 us
    dot_general x4, matrix products, linear(): return jnp.dot(matrix_a, matrix_b, preferred_element_type=jnp.float32)  18.5 us
  transfers between devices with their start and end apart: 34, of which 17 were waited for; matrix products, arithmetic and copies ran while one was open for 17% of the time, Pallas kernels for 17%

profile of v2, /device:TPU:0, one launch (start us, length us, event | category | flops | bytes accessed | tf_op | source)
XLA Modules:
  0.0 626.0 jit_solution(8542500303906843240)
XLA Ops:
  15.8 7.3 %all-to-all-start = ((f32[32,8,256]{2,1,0:T(8,128)}), f32[32,8,256]{2,1,0:T(8,128)S(1)}, u32[]{:S(2)}, u32[]{:S(2)}) async-start(f32[32,8,256]{2,1,0:T(8,128)} %bitcast.35), calls=%async_computation | async-start | bytes 524288 | tf_op jit(solution)/shard_map/all_to_all | solution.py:758
  24.8 11.1 %all-to-all-done.info = f32[32,8,256]{2,1,0:T(8,128)S(1)} async-done(((f32[32,8,256]{2,1,0:T(8,128)}), f32[32,8,256]{2,1,0:T(8,128)S(1)}, u32[]{:S(2)}, u32[]{:S(2)}) %all-to-all-start) | async-done | bytes 262176 | tf_op jit(solution)/shard_map/all_to_all | solution.py:758
  37.6 40.2 %all-gather.5.cloned.1.call-done = bf16[1024,2048]{1,0:T(8,128)(2,1)} async-done(((bf16[32,2048]{1,0:T(8,128)(2,1)}), bf16[1024,2048]{1,0:T(8,128)(2,1)}) %all-gather.5.cloned.1.call-update) | async-done | bytes 4194320 | tf_op jit(solution)/shard_map/all_gather | solution.py:847
  81.4 30.0 %all_to_all.45 = bf16[8,256,256]{2,1,0:T(8,128)(2,1)S(1)} all-to-all(bf16[8,256,256]{2,1,0:T(8,128)(2,1)S(1)} %bitcast.162), channel_id=1, replica_groups={{0,4,8,12,16,20,24,28},{1,5,9,13,17,21,25,29},{2,6,10,14,18,22,26,30},{..., dimensions={0} | all-to-all | bytes 2097152 | tf_op jit(solution)/shard_map/all_to_all | solution.py:758
  112.7 23.1 %collective-permute-done.1.x_2 = bf16[2048,256]{1,0:T(8,128)(2,1)S(1)} collective-permute-done((bf16[2048,256]{1,0:T(8,128)(2,1)S(1)}, bf16[2048,256]{1,0:T(8,128)(2,1)S(1)}, u32[]{:S(2)}, u32[]{:S(2)}) %collective-permute-start.1) | collective-permute-done | bytes 1048608 | tf_op jit(solution)/shard_map/ppermute | solution.py:735
  147.2 45.7 %hash_forward.1 = (bf16[32,272,128]{2,1,0:T(8,128)(2,1)}, bf16[8256,256]{1,0:T(8,128)(2,1)}) custom-call(s32[1]{0:T(128)} %bitcast.place, bf16[2048,256]{1,0:T(8,128)(2,1)S(1)} %bitcast.158, bf16[2048,256]{1,0:T(8,128)(2,1)S(1)} %collective-permute-done.x_1, bf16[2048,256]{1,0:T(8,128)(2,1)S(1)} %collective-permute-done.1.x_2, ...), custom_call_target="tpu_custom_call" | custom-call | flops 20000000000 | bytes 12000000 | tf_op jit(solution)/shard_map/hash_forward/pallas_call | solution.py:688
  192.9 5.3 all-to-all-start.2
  200.4 74.9 %all-to-all-done.2 = bf16[32,272,128]{2,1,0:T(8,128)(2,1)} async-done(((bf16[32,272,128]{2,1,0:T(8,128)(2,1)}), bf16[32,272,128]{2,1,0:T(8,128)(2,1)}, u32[]{:S(2)}, u32[]{:S(2)}) %all-to-all-start.2) | async-done | bytes 2228256 | tf_op jit(solution)/shard_map/all_to_all | solution.py:758
  288.2 12.4 %collective-permute-done.4 = bf16[256,1024]{1,0:T(8,128)(2,1)} collective-permute-done((bf16[256,1024]{1,0:T(8,128)(2,1)}, bf16[256,1024]{1,0:T(8,128)(2,1)}, u32[]{:S(2)}, u32[]{:S(2)}) %collective-permute-start.4) | collective-permute-done | bytes 524320 | tf_op jit(solution)/shard_map/ppermute | solution.py:735
  301.9 6.1 collective-permute-done.10
  308.1 4.6 fusion.18
  312.8 8.2 %convert_reduce_fusion = (f32[1024]{0:T(1024)}, bf16[1024,1024]{1,0:T(8,128)(2,1)S(1)}) fusion(f32[1024,1024]{1,0:T(8,128)S(1)} %fusion.18, f32[1024]{0:T(1024)S(1)} %bitcast.218, bf16[1024,2048]{1,0:T(8,128)(2,1)S(1)} %copy-done.34, bf16[256,1024]{1,0:T(8,128)(2,1)} %collective-permute-done.11, bf16[256,1024]{1,0:T(8,128)(2,1)} %collective-permute-done.10, ...), kind=kOutput, calls=%fused_computation.16 | convolution fusion | flops 2179988480 | bytes 10493952 | tf_op jit(solution)/shard_map/dot_general | solution.py:58
  331.6 8.5 %collective-permute-done.14 = bf16[256,1024]{1,0:T(8,128)(2,1)} collective-permute-done((bf16[256,1024]{1,0:T(8,128)(2,1)S(1)}, bf16[256,1024]{1,0:T(8,128)(2,1)}, u32[]{:S(2)}, u32[]{:S(2)}) %collective-permute-start.14) | collective-permute-done | bytes 524320 | tf_op jit(solution)/shard_map/ppermute | solution.py:735
  357.4 8.5 %all-to-all-start.4 = ((bf16[32,272,128]{2,1,0:T(8,128)(2,1)}), bf16[32,272,128]{2,1,0:T(8,128)(2,1)}, u32[]{:S(2)}, u32[]{:S(2)}) async-start(bf16[32,272,128]{2,1,0:T(8,128)(2,1)} %pad_maximum_fusion.1), calls=%async_computation.4 | async-start | bytes 4456448 | tf_op jit(solution)/shard_map/all_to_all | solution.py:758
  378.7 16.3 %collective-permute-done.20 = bf16[1024,256]{0,1:T(8,128)(2,1)S(1)} collective-permute-done((bf16[1024,256]{0,1:T(8,128)(2,1)S(1)}, bf16[1024,256]{0,1:T(8,128)(2,1)S(1)}, u32[]{:S(2)}, u32[]{:S(2)}) %collective-permute-start.20) | collective-permute-done | bytes 524320 | tf_op jit(solution)/shard_map/ppermute | solution.py:735
  398.0 6.7 %copy.105 = bf16[1024,2304]{1,0:T(8,128)(2,1)} copy(bf16[1024,2304]{0,1:T(8,128)(2,1)} %pad_maximum_fusion) | data formatting | bytes 9437184
  404.7 43.9 %all-to-all-done.4.grads = bf16[32,272,128]{2,1,0:T(8,128)(2,1)} async-done(((bf16[32,272,128]{2,1,0:T(8,128)(2,1)}), bf16[32,272,128]{2,1,0:T(8,128)(2,1)}, u32[]{:S(2)}, u32[]{:S(2)}) %all-to-all-start.4) | async-done | bytes 2228256 | tf_op jit(solution)/shard_map/all_to_all | solution.py:758
  448.6 58.9 %hash_backward.1 = (bf16[2048,256]{1,0:T(8,128)(2,1)S(1)}, bf16[2048,256]{1,0:T(8,128)(2,1)S(1)}, bf16[2048,256]{1,0:T(8,128)(2,1)S(1)}, bf16[2048,256]{1,0:T(8,128)(2,1)S(1)}) custom-call(s32[1]{0:T(128)} %bitcast.place, bf16[32,272,128]{2,1,0:T(8,128)(2,1)} %all-to-all-done.4.grads, bf16[8256,256]{1,0:T(8,128)(2,1)} %get-tuple-element.22.kept_rows, ...), custom_call_target="tpu_custom_call" | custom-call | flops 20000000000 | bytes 12000000 | tf_op jit(solution)/shard_map/hash_backward/pallas_call | solution.py:712
  512.0 23.8 %collective-permute-done.17 = bf16[2048,256]{1,0:T(8,128)(2,1)S(1)} collective-permute-done((bf16[2048,256]{1,0:T(8,128)(2,1)S(1)}, bf16[2048,256]{1,0:T(8,128)(2,1)S(1)}, u32[]{:S(2)}, u32[]{:S(2)}) %collective-permute-start.17) | collective-permute-done | bytes 1048608 | tf_op jit(solution)/shard_map/ppermute | solution.py:735
  545.0 14.2 %all-to-all-done.6 = bf16[32,32,256]{2,1,0:T(8,128)(2,1)S(1)} async-done(((bf16[32,32,256]{2,1,0:T(8,128)(2,1)}), bf16[32,32,256]{2,1,0:T(8,128)(2,1)S(1)}, u32[]{:S(2)}, u32[]{:S(2)}) %all-to-all-start.6) | async-done | bytes 524320 | tf_op jit(solution)/shard_map/all_to_all | solution.py:758
  563.8 7.7 %fusion.72 = (bf16[1024,1024]{1,0:T(8,128)(2,1)S(1)}, f32[1024,1024]{1,0:T(8,128)}) fusion(bf16[1024,2048]{1,0:T(8,128)(2,1)} %all-gather.9.cloned.1.call-done, f32[1024,1024]{1,0:T(8,128)} %copy-done.39, f32[1024]{0:T(1024)S(1)} %bitcast.220), kind=kOutput, calls=%fused_computation.243 | convolution fusion | flops 2159017984 | bytes 12587008 | tf_op jit(solution)/shard_map/dot_general | solution.py:48
  579.8 10.1 %all-to-all-done.5 = bf16[8,256,256]{1,2,0:T(8,128)(2,1)} async-done(((bf16[8,256,256]{1,2,0:T(8,128)(2,1)}), bf16[8,256,256]{1,2,0:T(8,128)(2,1)}, u32[]{:S(2)}, u32[]{:S(2)}) %all-to-all-start.5) | async-done | bytes 1048608 | tf_op jit(solution)/shard_map/all_to_all | solution.py:758
  589.9 5.0 multiply_reduce_fusion.1
  601.2 5.6 all-to-all-done.8
  (304 shorter events, 132.8 us)
Async XLA Ops:
  7.2 70.6 %all-gather.5.cloned.1.call-start = ((), (), s32[]{:S(2)}) async-start(), calls=%async_computation.10 | async-start | bytes 4325376 | tf_op jit(solution)/shard_map/all_gather | solution.py:847
  15.8 20.1 %all-to-all-start = ((f32[32,8,256]{2,1,0:T(8,128)}), f32[32,8,256]{2,1,0:T(8,128)S(1)}, u32[]{:S(2)}, u32[]{:S(2)}) async-start(f32[32,8,256]{2,1,0:T(8,128)} %bitcast.35), calls=%async_computation | async-start | bytes 524288 | tf_op jit(solution)/shard_map/all_to_all | solution.py:758
  23.1 258.3 %all-gather.7.cloned.1.call-start = ((), (), s32[]{:S(2)}) async-start(), calls=%async_computation.11 | async-start | bytes 2162688 | tf_op jit(solution)/shard_map/all_gather | solution.py:848
  111.4 24.4 %collective-permute-start.1 = (bf16[2048,256]{1,0:T(8,128)(2,1)S(1)}, bf16[2048,256]{1,0:T(8,128)(2,1)S(1)}, u32[]{:S(2)}, u32[]{:S(2)}) collective-permute-start(bf16[2048,256]{1,0:T(8,128)(2,1)S(1)} %bitcast.156), channel_id=1, source_target_pairs={{0,2},{1,3},{2,0},{3,1},{4,6},{5,7},{6,4},{7,5},{8,10},{9,11},{10,... | collective-permute-start | bytes 3145736 | tf_op jit(solution)/shard_map/ppermute | solution.py:735
  112.6 34.5 %collective-permute-start = (bf16[2048,256]{1,0:T(8,128)(2,1)S(1)}, bf16[2048,256]{1,0:T(8,128)(2,1)S(1)}, u32[]{:S(2)}, u32[]{:S(2)}) collective-permute-start(bf16[2048,256]{1,0:T(8,128)(2,1)S(1)} %bitcast.157), channel_id=1, source_target_pairs={{0,1},{1,0},{2,3},{3,2},{4,5},{5,4},{6,7},{7,6},{8,9},{9,8},{10,11... | collective-permute-start | bytes 3145736 | tf_op jit(solution)/shard_map/ppermute | solution.py:735
  135.8 11.4 %collective-permute-start.2 = (bf16[2048,256]{1,0:T(8,128)(2,1)S(1)}, bf16[2048,256]{1,0:T(8,128)(2,1)}, u32[]{:S(2)}, u32[]{:S(2)}) collective-permute-start(bf16[2048,256]{1,0:T(8,128)(2,1)S(1)} %collective-permute-done.1.x_2), channel_id=1, source_target_pairs={{0,1},{1,0},{2,3},{3,2},{4,5},{5,4},{6,7},{7,6},{8,9},{9,8},{10,11... | collective-permute-start | bytes 3145736 | tf_op jit(solution)/shard_map/ppermute | solution.py:735
  142.8 50.0 %all-to-all-start.3 = ((bf16[4,32,1024]{2,1,0:T(8,128)(2,1)}), bf16[4,32,1024]{2,1,0:T(8,128)(2,1)}, u32[]{:S(2)}, u32[]{:S(2)}) async-start(bf16[4,32,1024]{2,1,0:T(8,128)(2,1)} %reshape.520), calls=%async_computation.3 | async-start | bytes 524288 | tf_op jit(solution)/shard_map/all_to_all | solution.py:758
  192.9 82.5 %all-to-all-start.2 = ((bf16[32,272,128]{2,1,0:T(8,128)(2,1)}), bf16[32,272,128]{2,1,0:T(8,128)(2,1)}, u32[]{:S(2)}, u32[]{:S(2)}) async-start(bf16[32,272,128]{2,1,0:T(8,128)(2,1)} %get-tuple-element.21), calls=%async_computation.2 | async-start | bytes 4456448 | tf_op jit(solution)/shard_map/all_to_all | solution.py:758
  198.1 109.9 %all-gather.9.cloned.1.call-start = ((), (), s32[]{:S(2)}) async-start(), calls=%async_computation.12 | async-start | bytes 4718592 | tf_op jit(solution)/shard_map/all_gather | solution.py:853
  200.0 336.2 %all-gather.11.cloned.1.call-start = ((), (), s32[]{:S(2)}) async-start(), calls=%async_computation.13 | async-start | bytes 4718592 | tf_op jit(solution)/shard_map/all_gather | solution.py:871
  285.5 15.2 %collective-permute-start.4 = (bf16[256,1024]{1,0:T(8,128)(2,1)}, bf16[256,1024]{1,0:T(8,128)(2,1)}, u32[]{:S(2)}, u32[]{:S(2)}) collective-permute-start(bf16[256,1024]{1,0:T(8,128)(2,1)} %add_convert_fusion.4), channel_id=1, source_target_pairs={{0,2},{1,3},{2,0},{3,1},{4,6},{5,7},{6,4},{7,5},{8,10},{9,11},{10,... | collective-permute-start | bytes 1572872 | tf_op jit(solution)/shard_map/ppermute | solution.py:735
  287.9 20.1 %collective-permute-start.10 = (bf16[256,1024]{1,0:T(8,128)(2,1)S(1)}, bf16[256,1024]{1,0:T(8,128)(2,1)}, u32[]{:S(2)}, u32[]{:S(2)}) collective-permute-start(bf16[256,1024]{1,0:T(8,128)(2,1)S(1)} %get-tuple-element.130), channel_id=1, source_target_pairs={{0,2},{1,3},{2,0},{3,1},{4,6},{5,7},{6,4},{7,5},{8,10},{9,11},{10,... | collective-permute-start | bytes 1572872 | tf_op jit(solution)/shard_map/ppermute | solution.py:735
  288.2 19.8 %collective-permute-start.3 = (bf16[256,1024]{1,0:T(8,128)(2,1)}, bf16[256,1024]{1,0:T(8,128)(2,1)S(1)}, u32[]{:S(2)}, u32[]{:S(2)}) collective-permute-start(bf16[256,1024]{1,0:T(8,128)(2,1)} %add_convert_fusion.4), channel_id=1, source_target_pairs={{0,1},{1,0},{2,3},{3,2},{4,5},{5,4},{6,7},{7,6},{8,9},{9,8},{10,11... | collective-permute-start | bytes 1572872 | tf_op jit(solution)/shard_map/ppermute | solution.py:735
  300.7 12.1 %collective-permute-start.9 = (bf16[256,1024]{1,0:T(8,128)(2,1)S(1)}, bf16[256,1024]{1,0:T(8,128)(2,1)}, u32[]{:S(2)}, u32[]{:S(2)}) collective-permute-start(bf16[256,1024]{1,0:T(8,128)(2,1)S(1)} %get-tuple-element.130), channel_id=1, source_target_pairs={{0,1},{1,0},{2,3},{3,2},{4,5},{5,4},{6,7},{7,6},{8,9},{9,8},{10,11... | collective-permute-start | bytes 1572872 | tf_op jit(solution)/shard_map/ppermute | solution.py:735
  325.7 14.4 %collective-permute-start.14 = (bf16[256,1024]{1,0:T(8,128)(2,1)S(1)}, bf16[256,1024]{1,0:T(8,128)(2,1)}, u32[]{:S(2)}, u32[]{:S(2)}) collective-permute-start(bf16[256,1024]{1,0:T(8,128)(2,1)S(1)} %fusion.20), channel_id=1, source_target_pairs={{0,2},{1,3},{2,0},{3,1},{4,6},{5,7},{6,4},{7,5},{8,10},{9,11},{10,... | collective-permute-start | bytes 1572872 | tf_op jit(solution)/shard_map/ppermute | solution.py:735
  357.4 91.2 %all-to-all-start.4 = ((bf16[32,272,128]{2,1,0:T(8,128)(2,1)}), bf16[32,272,128]{2,1,0:T(8,128)(2,1)}, u32[]{:S(2)}, u32[]{:S(2)}) async-start(bf16[32,272,128]{2,1,0:T(8,128)(2,1)} %pad_maximum_fusion.1), calls=%async_computation.4 | async-start | bytes 4456448 | tf_op jit(solution)/shard_map/all_to_all | solution.py:758
  365.9 233.5 %reduce-scatter.4.cloned.1.call-start = ((), (), s32[]{:S(2)}) async-start(), calls=%async_computation.14 | async-start | bytes 5308416 | tf_op jit(solution)/shard_map/reduce_scatter | solution.py:914
  373.2 21.8 %collective-permute-start.20 = (bf16[1024,256]{0,1:T(8,128)(2,1)S(1)}, bf16[1024,256]{0,1:T(8,128)(2,1)S(1)}, u32[]{:S(2)}, u32[]{:S(2)}) collective-permute-start(bf16[1024,256]{0,1:T(8,128)(2,1)S(1)} %add_convert_fusion.3), channel_id=1, source_target_pairs={{0,2},{1,3},{2,0},{3,1},{4,6},{5,7},{6,4},{7,5},{8,10},{9,11},{10,... | collective-permute-start | bytes 1572872 | tf_op jit(solution)/shard_map/ppermute | solution.py:735
  510.5 25.3 %collective-permute-start.17 = (bf16[2048,256]{1,0:T(8,128)(2,1)S(1)}, bf16[2048,256]{1,0:T(8,128)(2,1)S(1)}, u32[]{:S(2)}, u32[]{:S(2)}) collective-permute-start(bf16[2048,256]{1,0:T(8,128)(2,1)S(1)} %add_convert_fusion.1), channel_id=1, source_target_pairs={{0,2},{1,3},{2,0},{3,1},{4,6},{5,7},{6,4},{7,5},{8,10},{9,11},{10,... | collective-permute-start | bytes 3145736 | tf_op jit(solution)/shard_map/ppermute | solution.py:735
  540.5 18.8 %all-to-all-start.6 = ((bf16[32,32,256]{2,1,0:T(8,128)(2,1)}), bf16[32,32,256]{2,1,0:T(8,128)(2,1)S(1)}, u32[]{:S(2)}, u32[]{:S(2)}) async-start(bf16[32,32,256]{2,1,0:T(8,128)(2,1)} %bitcast.58), calls=%async_computation.6 | async-start | bytes 1048576 | tf_op jit(solution)/shard_map/all_to_all | solution.py:758
  559.3 30.6 %all-to-all-start.5 = ((bf16[8,256,256]{1,2,0:T(8,128)(2,1)}), bf16[8,256,256]{1,2,0:T(8,128)(2,1)}, u32[]{:S(2)}, u32[]{:S(2)}) async-start(bf16[8,256,256]{1,2,0:T(8,128)(2,1)} %copy.98), calls=%async_computation.5 | async-start | bytes 2097152 | tf_op jit(solution)/shard_map/all_to_all | solution.py:758
  571.9 38.4 %collective-permute-start.6 = (bf16[256,1024]{1,0:T(8,128)(2,1)S(1)}, bf16[256,1024]{1,0:T(8,128)(2,1)}, u32[]{:S(2)}, u32[]{:S(2)}) collective-permute-start(bf16[256,1024]{1,0:T(8,128)(2,1)S(1)} %get-tuple-element.136), channel_id=1, source_target_pairs={{0,1},{1,0},{2,3},{3,2},{4,5},{5,4},{6,7},{7,6},{8,9},{9,8},{10,11... | collective-permute-start | bytes 1572872 | tf_op jit(solution)/shard_map/ppermute | solution.py:735
  575.7 34.6 %collective-permute-start.8 = (bf16[256,1024]{1,0:T(8,128)(2,1)}, bf16[256,1024]{1,0:T(8,128)(2,1)}, u32[]{:S(2)}, u32[]{:S(2)}) collective-permute-start(bf16[256,1024]{1,0:T(8,128)(2,1)} %fusion.22), channel_id=1, source_target_pairs={{0,2},{1,3},{2,0},{3,1},{4,6},{5,7},{6,4},{7,5},{8,10},{9,11},{10,... | collective-permute-start | bytes 1572872 | tf_op jit(solution)/shard_map/ppermute | solution.py:735
  595.8 10.9 %all-to-all-start.8 = ((f32[32,1,288]{2,1,0:T(1,128)}), f32[32,1,288]{2,1,0:T(1,128)S(1)}, u32[]{:S(2)}, u32[]{:S(2)}) async-start(f32[32,1,288]{2,1,0:T(1,128)} %broadcast_in_dim.31), calls=%async_computation.8 | async-start | bytes 98304 | tf_op jit(solution)/shard_map/all_to_all | solution.py:758
  (52 other events, 756.0 us)
Sparse Core Ops, SparseCore 0:
  11.5 66.3 all-gather.4
  112.7 55.4 all-gather.6
  201.6 99.6 all-gather.8
  327.6 113.1 all-gather.10
  444.3 94.2 reduce-scatter.3

commit v3 on v2

--- a/solution.py
+++ b/solution.py
@@ -474,7 +474,22 @@
     return high, mid, rest - mid
 
 
-def forward_kernel(place, x_0, x_1, x_2, x_3, info, key_ids, out, kept_rows, lanes, heads_out):
+def forward_kernel(
+    place,
+    x_0,
+    x_1,
+    x_2,
+    x_3,
+    info,
+    key_ids,
+    out_0,
+    out_1,
+    out_2,
+    out_3,
+    kept_rows,
+    lanes,
+    heads_out,
+):
     blocks, tokens = info.shape[0], info.shape[2]
     slots = blocks * CAP_ROWS
     width = x_0.shape[1]
@@ -544,58 +559,138 @@
 
     lax.fori_loop(0, blocks, unplace, 0, unroll=4)
 
-    def unpack(source, carry):
-        cols = jnp.transpose(info[source])
-        hot = hot_cols(cols[:, 3:4], slots)
-        part = dot_nn(hot, lanes[source].reshape(slots, width))
-        out[source, 0:tokens, :] = part[:, :HEAD_DIM].astype(BF)
-        flat = jnp.transpose(part[:, HEAD_DIM:])[0:PARTS, :].astype(BF)
-        for piece in range(tokens // HEAD_DIM):
-            first = tokens + piece * PARTS
-            out[source, first : first + PARTS, :] = flat[
-                :, piece * HEAD_DIM : (piece + 1) * HEAD_DIM
-            ]
-        return carry
-
-    lax.fori_loop(0, blocks, unpack, 0, unroll=4)
-
-
-def backward_kernel(place, grads, kept_rows, info, key_ids, out_0, out_1, out_2, out_3, lanes, sums):
+    for offset, out in enumerate((out_0, out_1, out_2, out_3)):
+
+        def unpack(group, carry, offset=offset, out=out):
+            source = group * rounds + lax.bitwise_xor(turn, offset)
+            cols = jnp.transpose(info[source])
+            hot = hot_cols(cols[:, 3:4], slots)
+            part = dot_nn(hot, lanes[source].reshape(slots, width))
+            out[group, 0:tokens, :] = part[:, :HEAD_DIM].astype(BF)
+            flat = jnp.transpose(part[:, HEAD_DIM:])[0:PARTS, :].astype(BF)
+            for piece in range(tokens // HEAD_DIM):
+                first = tokens + piece * PARTS
+                out[group, first : first + PARTS, :] = flat[
+                    :, piece * HEAD_DIM : (piece + 1) * HEAD_DIM
+                ]
+            return carry
+
+        lax.fori_loop(0, blocks // rounds, unpack, 0, unroll=4)
+
+
+def tall_parts(ref, group, first, tokens):
+    flat = jnp.concatenate(
+        [
+            ref[group, first + piece * PARTS : first + (piece + 1) * PARTS, :].astype(F32)
+            for piece in range(tokens // HEAD_DIM)
+        ],
+        axis=1,
+    )
+    return jnp.transpose(flat)
+
+
+def put_parts(ref, group, first, column):
+    tokens = column.shape[0]
+    high, mid, low = three_parts(column)
+    lane = lax.broadcasted_iota(jnp.int32, (tokens, PARTS), 1)
+    tall = jnp.where(lane == 0, high, jnp.where(lane == 1, mid, jnp.where(lane == 2, low, 0.0)))
+    flat = jnp.transpose(tall).astype(BF)
+    for piece in range(tokens // HEAD_DIM):
+        at = first + piece * PARTS
+        ref[group, at : at + PARTS, :] = flat[:, piece * HEAD_DIM : (piece + 1) * HEAD_DIM]
+
+
+def combined(refs, group):
+    tokens = refs[0].shape[1] // (HEAD_DIM + PARTS) * HEAD_DIM
+    lse = []
+    for ref in refs:
+        tall = tall_parts(ref, group, tokens, tokens)
+        lse.append(tall[:, 0:1] + tall[:, 1:2] + tall[:, 2:3])
+    top = lse[0]
+    for other in lse[1:]:
+        top = jnp.maximum(top, other)
+    weights = [jnp.exp(one - top) for one in lse]
+    total = sum(weights[1:], weights[0])
+    scale = 1.0 / total
+    rows = [
+        (weight * scale) * ref[group, 0:tokens, :].astype(F32)
+        for weight, ref in zip(weights, refs)
+    ]
+    return sum(rows[1:], rows[0]), top + jnp.log(total)
+
+
+def pair_kernel(a, b, out):
+    tokens = out.shape[1] // (HEAD_DIM + PARTS) * HEAD_DIM
+    for group in range(out.shape[0]):
+        rows, lse = combined((a, b), group)
+        out[group, 0:tokens, :] = rows.astype(BF)
+        put_parts(out, group, tokens, lse)
+
+
+def final_kernel(a, b, c, mixed, total_lse):
+    for group in range(mixed.shape[0]):
+        rows, lse = combined((a, b, c), group)
+        mixed[group] = rows.astype(BF)
+        put_parts(total_lse, group, 0, lse)
+
+
+def backward_kernel(
+    place,
+    g_0,
+    g_1,
+    g_2,
+    g_3,
+    l_0,
+    l_1,
+    l_2,
+    l_3,
+    kept_rows,
+    info,
+    key_ids,
+    out_0,
+    out_1,
+    out_2,
+    out_3,
+    lanes,
+    sums,
+):
     blocks, tokens = info.shape[0], info.shape[2]
     slots = blocks * CAP_ROWS
     width = kept_rows.shape[1]
     spans = tokens // SPAN
 
-    def pack(source, carry):
-        hot = hot_rows(info[source, 3:4, :], slots)
-        flat = jnp.concatenate(
-            [
-                grads[source, tokens + piece * PARTS : tokens + (piece + 1) * PARTS, :].astype(F32)
-                for piece in range(tokens // HEAD_DIM)
-            ],
-            axis=1,
-        )
-        tall = jnp.concatenate([flat, jnp.zeros((HEAD_DIM - PARTS, tokens), F32)], axis=0)
-        rows = jnp.concatenate(
-            [grads[source, 0:tokens, :], jnp.transpose(tall).astype(BF)], axis=1
-        )
-        part = dot_nn(hot, rows).astype(BF)
-        lanes[:, pl.ds(source, 1)] = part.reshape(blocks, 1, CAP_ROWS, width)
-        return carry
-
-    lax.fori_loop(0, blocks, pack, 0, unroll=4)
+    for offset, grads, lse in ((0, g_0, l_0), (1, g_1, l_1), (2, g_2, l_2), (3, g_3, l_3)):
+
+        def pack(group, carry, offset=offset, grads=grads, lse=lse):
+            source = group * ROUNDS + lax.bitwise_xor(place[0], offset)
+            hot = hot_rows(info[source, 3:4, :], slots)
+            tall = [tall_parts(grads, group, tokens, tokens), tall_parts(lse, group, 0, tokens)]
+            tall.append(jnp.zeros((tokens, HEAD_DIM - 2 * PARTS), F32))
+            rows = jnp.concatenate(
+                [grads[group, 0:tokens, :], jnp.concatenate(tall, axis=1).astype(BF)], axis=1
+            )
+            part = dot_nn(hot, rows).astype(BF)
+            lanes[:, pl.ds(source, 1)] = part.reshape(blocks, 1, CAP_ROWS, width)
+            return carry
+
+        lax.fori_loop(0, blocks // ROUNDS, pack, 0, unroll=4)
+
     sums[0:SPAN, :] = jnp.zeros((SPAN, width), F32)
 
     def attend(block, carry):
         cols = jnp.transpose(info[block])
         hot = hot_cols(cols[:, 2:3], slots)
         part_grads = dot_nn(hot, lanes[block].reshape(slots, width))
-        grad_rows = part_grads[:, :HEAD_DIM].astype(BF)
-        grad_lse = (
-            part_grads[:, HEAD_DIM : HEAD_DIM + 1]
-            + part_grads[:, HEAD_DIM + 1 : HEAD_DIM + 2]
-            + part_grads[:, HEAD_DIM + 2 : HEAD_DIM + 3]
-        )
+        grad_rows = part_grads[:, :HEAD_DIM]
+
+        def summed(first):
+            return sum(
+                (part_grads[:, first + at : first + at + 1] for at in (1, 2)),
+                part_grads[:, first : first + 1],
+            )
+
+        pull = summed(HEAD_DIM)
+        total_lse = summed(HEAD_DIM + PARTS)
         first = []
         for part in range(spans):
             span = block * spans + part
@@ -603,29 +698,33 @@
             rows = kept_rows[pl.ds(start, 2 * SPAN), :]
             keys = rows[:, :HEAD_DIM]
             queries = rows[SPAN:, :HEAD_DIM]
-            grad_out = grad_rows[part * SPAN : (part + 1) * SPAN]
             raw = dot_nt(queries, keys)
-            grad_prob = dot_nt(grad_out, rows[:, HEAD_DIM:])
-            first.append((start, keys, queries, grad_out, raw, grad_prob, key_norm(keys)))
-        second = []
-        slopes = []
+            first.append((start, keys, queries, rows[:, HEAD_DIM:], raw, key_norm(keys)))
+        middle = []
         for part in range(spans):
-            start, keys, queries, grad_out, raw, grad_prob, norm = first[part]
+            start, keys, queries, values, raw, norm = first[part]
             here = slice(part * SPAN, (part + 1) * SPAN)
             ids = cols[here]
             factor, kept, weight, top, total = span_softmax(
                 raw, norm, key_ids[pl.ds(block * spans + part, 1), :], ids[:, 0:1], ids[:, 1:2]
             )
-            probs = weight * (1.0 / total)
-            row_dot = jnp.sum(probs * grad_prob, axis=1, keepdims=True)
-            grad_score = jnp.where(kept, probs * (grad_prob - row_dot + grad_lse[here]), 0.0)
+            merge = jnp.exp(top + jnp.log(total) - total_lse[here])
+            grad_out = (merge * grad_rows[here]).astype(BF)
+            middle.append((factor, kept, weight * (1.0 / total), grad_out, merge * pull[here]))
+        back = [dot_nt(middle[part][3], first[part][3]) for part in range(spans)]
+        second = []
+        slopes = []
+        for part in range(spans):
+            raw, norm = first[part][4:]
+            factor, kept, probs, grad_out, pulled = middle[part]
+            grad_score = jnp.where(kept, probs * (back[part] - pulled), 0.0)
             slopes.append(
                 jnp.sum(grad_score * raw, axis=0, keepdims=True) * SCALE * norm * norm * norm
             )
             second.append(((grad_score * factor).astype(BF), probs.astype(BF)))
         held = []
         for part in range(spans):
-            start, keys, queries, grad_out = first[part][:4]
+            start, keys, queries = first[part][:3]
             grad_raw, probs = second[part]
             held.append(
                 (
@@ -633,7 +732,7 @@
                     keys,
                     dot_nn(grad_raw, keys),
                     dot_tn(grad_raw, queries),
-                    dot_tn(probs, grad_out),
+                    dot_tn(probs, middle[part][3]),
                 )
             )
         slopes.append(jnp.zeros((8 - spans, 2 * SPAN), F32))
@@ -680,50 +779,60 @@
     return [pl.BlockSpec(memory_space=pltpu.VMEM)] * count
 
 
+def run_kernel(kernel, name, operands, shapes, scratch, scalar):
+    first = [pl.BlockSpec(memory_space=pltpu.SMEM)] if scalar else []
+    return pl.pallas_call(
+        kernel,
+        out_shape=tuple(jax.ShapeDtypeStruct(shape, BF) for shape in shapes),
+        in_specs=first + in_vmem(len(operands) - len(first)),
+        out_specs=tuple(in_vmem(len(shapes))),
+        scratch_shapes=[pltpu.VMEM(shape, dtype) for shape, dtype in scratch],
+        compiler_params=pltpu.CompilerParams(vmem_limit_bytes=48 << 20),
+        cost_estimate=pl.CostEstimate(
+            flops=20 * 10**9 if scalar else 10**7,
+            bytes_accessed=12 * 10**6 if scalar else 2 * 10**6,
+            transcendentals=10**6 if scalar else 10**4,
+        ),
+        name=name,
+    )(*operands)
+
+
 def run_forward(turn, rows, info, key_ids):
     blocks, _, tokens = info.shape
     width = rows[0].shape[1]
-    positions = blocks * tokens
-    extra = PARTS * tokens // HEAD_DIM
-    return pl.pallas_call(
+    tall = tokens + PARTS * tokens // HEAD_DIM
+    return run_kernel(
         forward_kernel,
-        out_shape=(
-            jax.ShapeDtypeStruct((blocks, tokens + extra, HEAD_DIM), BF),
-            jax.ShapeDtypeStruct((SPAN + positions, width), BF),
-        ),
-        in_specs=[pl.BlockSpec(memory_space=pltpu.SMEM)] + in_vmem(6),
-        out_specs=tuple(in_vmem(2)),
-        scratch_shapes=[
-            pltpu.VMEM((blocks, blocks, CAP_ROWS, width), BF),
-            pltpu.VMEM((blocks, tokens, width), BF),
-        ],
-        compiler_params=pltpu.CompilerParams(vmem_limit_bytes=48 << 20),
-        cost_estimate=pl.CostEstimate(
-            flops=20 * 10**9, bytes_accessed=12 * 10**6, transcendentals=10**6
-        ),
-        name="hash_forward",
-    )(turn, *rows, info, key_ids)
-
-
-def run_backward(turn, grads, kept_rows, info, key_ids):
+        "hash_forward",
+        (turn, *rows, info, key_ids),
+        [(blocks // ROUNDS, tall, HEAD_DIM)] * ROUNDS + [(SPAN + blocks * tokens, width)],
+        [((blocks, blocks, CAP_ROWS, width), BF), ((blocks, tokens, width), BF)],
+        True,
+    )
+
+
+def run_backward(turn, grads, lse, kept_rows, info, key_ids):
     blocks, _, tokens = info.shape
     width = kept_rows.shape[1]
-    positions = blocks * tokens
-    return pl.pallas_call(
+    return run_kernel(
         backward_kernel,
-        out_shape=(jax.ShapeDtypeStruct((positions // ROUNDS, width), BF),) * ROUNDS,
-        in_specs=[pl.BlockSpec(memory_space=pltpu.SMEM)] + in_vmem(4),
-        out_specs=tuple(in_vmem(ROUNDS)),
-        scratch_shapes=[
-            pltpu.VMEM((blocks, blocks, CAP_ROWS, width), BF),
-            pltpu.VMEM((SPAN + positions, width), F32),
-        ],
-        compiler_params=pltpu.CompilerParams(vmem_limit_bytes=48 << 20),
-        cost_estimate=pl.CostEstimate(
-            flops=20 * 10**9, bytes_accessed=12 * 10**6, transcendentals=10**6
-        ),
-        name="hash_backward",
-    )(turn, grads, kept_rows, info, key_ids)
+        "hash_backward",
+        (turn, *grads, *lse, kept_rows, info, key_ids),
+        [(blocks * tokens // ROUNDS, width)] * ROUNDS,
+        [((blocks, blocks, CAP_ROWS, width), BF), ((SPAN + blocks * tokens, width), F32)],
+        True,
+    )
+
+
+def merge_pair(a, b):
+    return run_kernel(pair_kernel, "merge_pair", (a, b), [a.shape], [], False)[0]
+
+
+def merge_final(a, b, c):
+    groups, tall, width = a.shape
+    tokens = tall // (HEAD_DIM + PARTS) * HEAD_DIM
+    shapes = [(groups, tokens, width), (groups, tall - tokens, width)]
+    return run_kernel(final_kernel, "merge_final", (a, b, c), shapes, [], False)
 
 
 def peers(mask):
@@ -845,42 +954,41 @@
         [w_qk.reshape(shard, HEADS, HEAD_DIM), w_value.reshape(shard, HEADS, HEAD_DIM)], axis=2
     ).reshape(shard, 2 * features)
     m_pair = lax.all_gather(pair.astype(BF), "seq", axis=0, tiled=True)
-    m_out = lax.all_gather(w_out.astype(BF), "seq", axis=0, tiled=True)
+    half = HEADS * wide
     up_cols = jnp.transpose(
         w_up.astype(BF).reshape(shard, HEADS, ROUNDS, wide), (2, 0, 1, 3)
-    ).reshape(ROUNDS, shard, HEADS * wide)
-    up_cols = exchange(up_cols, rows_of()).reshape(ROUNDS * shard, HEADS * wide)
+    ).reshape(ROUNDS, shard, half)
+    out_rows = jnp.broadcast_to(w_out.astype(BF), (ROUNDS, shard, features))
+    near_rows = exchange(jnp.concatenate([up_cols, out_rows], axis=2), rows_of())
+    near_rows = near_rows.reshape(ROUNDS * shard, half + features)
+    b_up = lax.dynamic_index_in_dim(
+        b_up.reshape(HEADS, ROUNDS, wide), place % ROUNDS, axis=1, keepdims=False
+    ).reshape(HEADS * wide)
+
+    normed_one, hat_one, inv_one = layer_norm(x_second, gain_one, shift_one)
+    normed_one, near_rows = lax.optimization_barrier((normed_one.astype(BF), near_rows))
+    rows = linear(normed_one, m_pair).astype(BF)
+    rows = jnp.transpose(rows.reshape(tokens, HEADS, 2 * HEAD_DIM), (1, 0, 2))
+    own = exchange(rows, columns()).reshape(HEADS * tokens, 2 * HEAD_DIM)
+    own, near_rows = lax.optimization_barrier((own, near_rows))
     m_ffn = lax.all_gather(
-        jnp.concatenate([up_cols, w_down.astype(BF)], axis=1),
+        jnp.concatenate([near_rows, w_down.astype(BF)], axis=1),
         "seq",
         axis=0,
         tiled=True,
         axis_index_groups=columns(),
     )
-    m_up, m_down = m_ffn[:, : HEADS * wide], m_ffn[:, HEADS * wide :]
-    b_up = lax.dynamic_index_in_dim(
-        b_up.reshape(HEADS, ROUNDS, wide), place % ROUNDS, axis=1, keepdims=False
-    ).reshape(HEADS * wide)
-
-    normed_one, hat_one, inv_one = layer_norm(x_second, gain_one, shift_one)
-    normed_one = normed_one.astype(BF)
-    rows = linear(normed_one, m_pair).astype(BF)
-    rows = jnp.transpose(rows.reshape(tokens, HEADS, 2 * HEAD_DIM), (1, 0, 2))
-    own = exchange(rows, columns()).reshape(HEADS * tokens, 2 * HEAD_DIM)
-    all_rows = gather_group(own)
+    m_up, m_out, m_down = (m_ffn[:, at : at + features] for at in (0, half, half + features))
+    turn = (place % ROUNDS).astype(jnp.int32).reshape(1)
+    *sent, kept_rows = run_forward(turn, gather_group(own), info, key_ids)
+    far = merge_pair(sent[2], swap(sent[3], 1))
+    mixed, total_lse = merge_final(sent[0], swap(sent[1], 1), swap(far, 2))
+    mixed = exchange(mixed, columns())
+    mixed, normed_one = lax.optimization_barrier((mixed, normed_one))
     normed_col = lax.all_gather(
         normed_one, "seq", axis=0, tiled=True, axis_index_groups=columns()
     )
-    turn = (place % ROUNDS).astype(jnp.int32).reshape(1)
-    sent, kept_rows = run_forward(turn, all_rows, info, key_ids)
-    back = exchange(sent).reshape(HEADS, ROUNDS, -1, HEAD_DIM)
-    out_all = jnp.transpose(back[:, :, :tokens], (1, 2, 0, 3)).astype(F32)
-    pieces = back[:, :, tokens:].reshape(HEADS, ROUNDS, -1, PARTS, HEAD_DIM)[:, :, :, :3]
-    lse_all = jnp.sum(pieces.astype(F32), axis=3).reshape(HEADS, ROUNDS, tokens)
-    lse_all = jnp.transpose(lse_all, (1, 2, 0))
-
-    merge = jnp.exp(lse_all - jax.nn.logsumexp(lse_all, axis=0))
-    mixed = jnp.sum(merge[..., None] * out_all, axis=0).reshape(tokens, -1).astype(BF)
+    mixed = jnp.transpose(mixed, (1, 0, 2)).reshape(tokens, features)
     y_first = x_first + linear(mixed, m_out)
     normed_two, hat_two, inv_two = layer_norm(y_first, gain_two, shift_two)
     normed_two = normed_two.astype(BF)
@@ -904,6 +1012,19 @@
     grad_attn = dx_first.astype(BF)
     grad_out = inner_rows(mixed, grad_attn)
     fourth = features // ROUNDS
+    grad_mixed = outer_cols(grad_attn, m_out).astype(BF)
+    pull = jnp.sum(
+        (grad_mixed.astype(F32) * mixed.astype(F32)).reshape(tokens, HEADS, HEAD_DIM), axis=-1
+    )
+    parts = split_three(jnp.transpose(pull))
+    parts = jnp.pad(parts, ((0, PARTS - 3), (0, 0), (0, 0)))
+    parts = jnp.transpose(parts.reshape(PARTS, HEADS, -1, HEAD_DIM), (1, 2, 0, 3))
+    parts = parts.reshape(HEADS, -1, HEAD_DIM).astype(BF)
+    grad_mixed = jnp.transpose(grad_mixed.reshape(tokens, HEADS, HEAD_DIM), (1, 0, 2))
+    grad_mixed = exchange(jnp.concatenate([grad_mixed, parts], axis=1), columns())
+    grad_mixed, grad_up, grad_down, grad_out = lax.optimization_barrier(
+        (grad_mixed, grad_up, grad_down, grad_out)
+    )
     grad_out = sum_group(
         [
             lax.dynamic_slice_in_dim(grad_out, ((place % ROUNDS) ^ near) * fourth, fourth, axis=1)
@@ -914,26 +1035,18 @@
     merged = lax.psum_scatter(
         merged, "seq", scatter_dimension=0, tiled=True, axis_index_groups=columns()
     )
-    half = HEADS * wide
     s_down = merged[:, half + fourth :].astype(F32)
     merged = exchange(merged[:, : half + fourth].reshape(ROUNDS, shard, -1), rows_of())
     s_up = jnp.transpose(merged[:, :, :half].reshape(ROUNDS, shard, HEADS, wide), (1, 2, 0, 3))
     s_up = s_up.reshape(shard, ROUNDS * half).astype(F32)
     s_out = jnp.transpose(merged[:, :, half:], (1, 0, 2)).reshape(shard, features).astype(F32)
-    grad_mixed = outer_cols(grad_attn, m_out).reshape(tokens, HEADS, HEAD_DIM)
-    along = jnp.sum(grad_mixed[None] * out_all, axis=-1)
-    grad_lse_all = merge * (along - jnp.sum(merge * along, axis=0, keepdims=True))
-
-    grad_round = (merge[..., None] * grad_mixed[None]).astype(BF)
-    grad_round = jnp.transpose(grad_round, (2, 0, 1, 3)).reshape(devices, tokens, HEAD_DIM)
-    parts = split_three(jnp.transpose(grad_lse_all, (2, 0, 1)).reshape(devices, tokens))
-    parts = jnp.pad(parts, ((0, PARTS - 3), (0, 0), (0, 0)))
-    parts = jnp.transpose(parts.reshape(PARTS, devices, -1, HEAD_DIM), (1, 2, 0, 3))
-    parts = parts.reshape(devices, -1, HEAD_DIM).astype(BF)
-    got_grads = exchange(jnp.concatenate([grad_round, parts], axis=1))
-    grad_head = run_backward(turn, got_grads, kept_rows, info, key_ids)
+
+    grad_head = run_backward(
+        turn, gather_group(grad_mixed), gather_group(total_lse), kept_rows, info, key_ids
+    )
     grad_head = sum_group([x.astype(F32) for x in grad_head]).astype(BF)
     grad_rows = exchange(grad_head.reshape(HEADS, tokens, 2 * HEAD_DIM), columns())
+    grad_rows, grad_head = lax.optimization_barrier((grad_rows, grad_head))
     grad_rows = jnp.transpose(grad_rows, (1, 0, 2)).reshape(tokens, 2 * features)
 
     s_pair = exchange(
@@ -948,7 +1061,6 @@
     grad_gain_attn = jnp.sum(grad_one * hat_one, axis=0)
     grad_bias_attn = jnp.sum(grad_one, axis=0)
     dx_second = dy_second + norm_back(grad_one, hat_one, inv_one, gain_one)
-
     is_mine = (jnp.arange(ROUNDS) == place % ROUNDS).astype(F32)
     grad_bias_up = grad_bias_up.reshape(HEADS, 1, wide) * is_mine[None, :, None]
     small = jnp.concatenate(

time: 635 us -> 580 us (0.913)
  waiting for transfers between devices: 296 us -> 260 us
  blocking collectives: 30 us -> 0 us
  local copies, waits for them, and re-layouts: 38.6 us -> 22.4 us
  Pallas kernels: 105 us -> 120 us
  starting transfers between devices: 52.3 us -> 64.8 us
  matrix products: 47.8 us -> 58.1 us
  other arithmetic: 41.8 us -> 33.8 us
    all_to_all x8 -> x9, waiting for transfers between devices: 160 us -> 103 us  [exchange(): lax.all_to_all(x, 'seq', split_axis=0, concat_axis=0, tiled=True, axis_in...]
    ppermute x21 -> x30, waiting for transfers between devices: 94.9 us -> 129 us  [swap(): return lax.ppermute(x, 'seq', peers(mask))]
    all_to_all x1 -> x0, blocking collectives: 30 us -> none  [exchange(): lax.all_to_all(x, 'seq', split_axis=0, concat_axis=0, tiled=True, axis_in...]
    pallas_call x2 -> x4, Pallas kernels: 105 us -> 120 us  [run_kernel(): pl.pallas_call(kernel, out_shape=tuple((jax.ShapeDtypeStruct(shape, BF) f...]
    all_gather x1, waiting for transfers between devices: 40.2 us -> 27.6 us  [shards_fast(): m_pair = lax.all_gather(pair.astype(BF), 'seq', axis=0, tiled=True)]
    all_to_all x8 -> x9, starting transfers between devices: 40 us -> 50.1 us  [exchange(): lax.all_to_all(x, 'seq', split_axis=0, concat_axis=0, tiled=True, axis_in...]
    unnamed x90 -> x73, local copies, waits for them, and re-layouts: 12.4 us -> 2.78 us
    dot_general x4, matrix products: 12.9 us -> 20 us  [inner_rows(): lax.dot_general(matrix_a, matrix_b, (((0,), (0,)), ((), ())), preferred_e...]
  transfers between devices with their start and end apart: 34 -> 43, of which waited for: 17 -> 26; matrix products, arithmetic and copies ran while one was open for 17% -> 14% of each run, Pallas kernels for 17% -> 21%
where the time goes in v3:
time: 580 us; the launch traced here: 574 us
  waiting for transfers between devices  260 us (45%)
  Pallas kernels  120 us (21%)
  starting transfers between devices  64.8 us (11%)
  matrix products  58.1 us (10%)
  other arithmetic  33.8 us (6%)
  local copies, waits for them, and re-layouts  22.4 us (4%)
  between operations  14.9 us (3%)
    ppermute x30, waiting for transfers between devices, swap(): return lax.ppermute(x, 'seq', peers(mask))  129 us
    pallas_call x4, Pallas kernels, run_kernel(): pl.pallas_call(kernel, out_shape=tuple((jax.ShapeDtypeStruct(shape, BF) f...  120 us
    all_to_all x9, waiting for transfers between devices, exchange(): lax.all_to_all(x, 'seq', split_axis=0, concat_axis=0, tiled=True, axis_in...  103 us
    all_to_all x9, starting transfers between devices, exchange(): lax.all_to_all(x, 'seq', split_axis=0, concat_axis=0, tiled=True, axis_in...  50.1 us
    all_gather x1, waiting for transfers between devices, shards_fast(): m_pair = lax.all_gather(pair.astype(BF), 'seq', axis=0, tiled=True)  27.6 us
    dot_general x4, matrix products, inner_rows(): lax.dot_general(matrix_a, matrix_b, (((0,), (0,)), ((), ())), preferred_e...  20 us
    dot_general x4, matrix products, outer_cols(): lax.dot_general(matrix_a, matrix_b, (((1,), (1,)), ((), ())), preferred_e...  19.6 us
    dot_general x4, matrix products, linear(): return jnp.dot(matrix_a, matrix_b, preferred_element_type=jnp.float32)  18.5 us
  transfers between devices with their start and end apart: 43, of which 26 were waited for; matrix products, arithmetic and copies ran while one was open for 14% of the time, Pallas kernels for 21%

profile of v3, /device:TPU:0, one launch (start us, length us, event | category | flops | bytes accessed | tf_op | source)
XLA Modules:
  0.0 574.3 jit_solution(8607118141521717)
XLA Ops:
  15.8 7.3 %all-to-all-start = ((f32[32,8,256]{2,1,0:T(8,128)}), f32[32,8,256]{2,1,0:T(8,128)S(1)}, u32[]{:S(2)}, u32[]{:S(2)}) async-start(f32[32,8,256]{2,1,0:T(8,128)} %bitcast.35), calls=%async_computation | async-start | bytes 524288 | tf_op jit(solution)/shard_map/all_to_all | solution.py:867
  26.1 9.8 %all-to-all-done.info = f32[32,8,256]{2,1,0:T(8,128)S(1)} async-done(((f32[32,8,256]{2,1,0:T(8,128)}), f32[32,8,256]{2,1,0:T(8,128)S(1)}, u32[]{:S(2)}, u32[]{:S(2)}) %all-to-all-start) | async-done | bytes 262176 | tf_op jit(solution)/shard_map/all_to_all | solution.py:867
  40.5 11.3 %all-to-all-done.1 = bf16[4,32,2048]{2,1,0:T(8,128)(2,1)S(1)} async-done(((bf16[4,32,2048]{2,1,0:T(8,128)(2,1)}), bf16[4,32,2048]{2,1,0:T(8,128)(2,1)S(1)}, u32[]{:S(2)}, u32[]{:S(2)}) %all-to-all-start.1) | async-done | bytes 524320 | tf_op jit(solution)/shard_map/all_to_all | solution.py:867
  51.9 27.6 %all-gather.4.cloned.1.call-done = bf16[1024,2048]{1,0:T(8,128)(2,1)} async-done(((bf16[32,2048]{1,0:T(8,128)(2,1)}), bf16[1024,2048]{1,0:T(8,128)(2,1)}) %all-gather.4.cloned.1.call-update) | async-done | bytes 4194320 | tf_op jit(solution)/shard_map/all_gather | solution.py:956
  88.1 26.1 %all-to-all-done.2 = bf16[8,256,256]{2,1,0:T(8,128)(2,1)S(1)} async-done(((bf16[8,256,256]{2,1,0:T(8,128)(2,1)}), bf16[8,256,256]{2,1,0:T(8,128)(2,1)S(1)}, u32[]{:S(2)}, u32[]{:S(2)}) %all-to-all-start.2) | async-done | bytes 1048608 | tf_op jit(solution)/shard_map/all_to_all | solution.py:867
  116.2 23.3 %collective-permute-done.1.x_2 = bf16[2048,256]{1,0:T(8,128)(2,1)S(1)} collective-permute-done((bf16[2048,256]{1,0:T(8,128)(2,1)S(1)}, bf16[2048,256]{1,0:T(8,128)(2,1)S(1)}, u32[]{:S(2)}, u32[]{:S(2)}) %collective-permute-start.1) | collective-permute-done | bytes 1048608 | tf_op jit(solution)/shard_map/ppermute | solution.py:844
  142.3 45.3 %hash_forward.1 = (bf16[8,272,128]{2,1,0:T(8,128)(2,1)S(1)}, bf16[8,272,128]{2,1,0:T(8,128)(2,1)S(1)}, bf16[8,272,128]{2,1,0:T(8,128)(2,1)S(1)}, bf16[8,272,128]{2,1,0:T(8,128)(2,1)S(1)}, bf16[8256,256]{1,0:T(8,128)(2,1)}) custom-call(s32[1]{0:T(128)} %bitcast.place, bf16[2048,256]{1,0:T(8,128)(2,1)S(1)} %bitcast.134, ...), custom_call_target="tpu_custom_call" | custom-call | flops 20000000000 | bytes 12000000 | tf_op jit(solution)/shard_map/hash_forward/pallas_call | solution.py:784
  194.5 13.4 %collective-permute-done.5.c = bf16[8,272,128]{2,1,0:T(8,128)(2,1)S(1)} collective-permute-done((bf16[8,272,128]{2,1,0:T(8,128)(2,1)S(1)}, bf16[8,272,128]{2,1,0:T(8,128)(2,1)S(1)}, u32[]{:S(2)}, u32[]{:S(2)}) %collective-permute-start.5) | collective-permute-done | bytes 557088 | tf_op jit(solution)/shard_map/ppermute | solution.py:844
  212.8 16.6 %all-to-all-start.3 = ((bf16[8,256,128]{2,1,0:T(8,128)(2,1)}), bf16[8,256,128]{2,1,0:T(8,128)(2,1)S(1)}, u32[]{:S(2)}, u32[]{:S(2)}) async-start(bf16[8,256,128]{2,1,0:T(8,128)(2,1)} %get-tuple-element.45), calls=%async_computation.3 | async-start | bytes 1048576 | tf_op jit(solution)/shard_map/all_to_all | solution.py:867
  229.6 14.1 %all-to-all-done.3 = bf16[8,256,128]{2,1,0:T(8,128)(2,1)S(1)} async-done(((bf16[8,256,128]{2,1,0:T(8,128)(2,1)}), bf16[8,256,128]{2,1,0:T(8,128)(2,1)S(1)}, u32[]{:S(2)}, u32[]{:S(2)}) %all-to-all-start.3) | async-done | bytes 524320 | tf_op jit(solution)/shard_map/all_to_all | solution.py:867
  250.2 13.0 %collective-permute-done.7 = bf16[256,1024]{1,0:T(8,128)(2,1)} collective-permute-done((bf16[256,1024]{1,0:T(8,128)(2,1)}, bf16[256,1024]{1,0:T(8,128)(2,1)}, u32[]{:S(2)}, u32[]{:S(2)}) %collective-permute-start.7) | collective-permute-done | bytes 524320 | tf_op jit(solution)/shard_map/ppermute | solution.py:844
  264.4 7.4 %collective-permute-done.13 = bf16[256,1024]{1,0:T(8,128)(2,1)} collective-permute-done((bf16[256,1024]{1,0:T(8,128)(2,1)S(1)}, bf16[256,1024]{1,0:T(8,128)(2,1)}, u32[]{:S(2)}, u32[]{:S(2)}) %collective-permute-start.13) | collective-permute-done | bytes 524320 | tf_op jit(solution)/shard_map/ppermute | solution.py:844
  276.6 8.2 %convert_reduce_fusion = (f32[1024]{0:T(1024)}, bf16[1024,1024]{1,0:T(8,128)(2,1)S(1)}) fusion(f32[1024,1024]{1,0:T(8,128)S(1)} %fusion.15, f32[1024]{0:T(1024)S(1)} %bitcast.199, bf16[1024,3072]{1,0:T(8,128)(2,1)S(1)} %bitcast.152, bf16[256,1024]{1,0:T(8,128)(2,1)S(1)} %collective-permute-done.14, bf16[256,1024]{1,0:T(8,128)(2,1)} %collective-permute-done.13, ...), kind=kOutput, calls=%fused_computation.10 | convolution fusion | flops 2179988480 | bytes 10493952 | tf_op jit(solution)/shard_map/dot_general | solution.py:58
  296.0 13.0 %collective-permute-done.17 = bf16[256,1024]{1,0:T(8,128)(2,1)} collective-permute-done((bf16[256,1024]{1,0:T(8,128)(2,1)}, bf16[256,1024]{1,0:T(8,128)(2,1)}, u32[]{:S(2)}, u32[]{:S(2)}) %collective-permute-start.17) | collective-permute-done | bytes 524320 | tf_op jit(solution)/shard_map/ppermute | solution.py:844
  322.6 7.6 %fusion.33 = bf16[1024,1024]{1,0:T(8,128)(2,1)} fusion(bf16[256,1024]{1,0:T(8,128)(2,1)} %copy-done.28, bf16[256,1024]{1,0:T(8,128)(2,1)} %collective-permute-done.13, bf16[256,1024]{1,0:T(8,128)(2,1)} %collective-permute-done.12, bf16[256,1024]{1,0:T(8,128)(2,1)S(1)} %copy-done.10, f32[1024,1024]{1,0:T(8,128)} %copy-done.31, f32[1024]{0:T(1024)S(1)} %bitcast.200), kind=kOutput, calls=%fused_computation.67 | convolution fusion | flops 2166358016 | bytes 8392704 | tf_op jit(solution)/shard_map/dot_general | solution.py:52
  330.2 5.2 fusion.34
  338.2 13.8 %all-to-all-done.4.g_0 = bf16[8,272,128]{2,1,0:T(8,128)(2,1)S(1)} async-done(((bf16[8,272,128]{2,1,0:T(8,128)(2,1)}), bf16[8,272,128]{2,1,0:T(8,128)(2,1)S(1)}, u32[]{:S(2)}, u32[]{:S(2)}) %all-to-all-start.4) | async-done | bytes 557088 | tf_op jit(solution)/shard_map/all_to_all | solution.py:867
  359.7 10.7 %collective-permute-done.19.g_2 = bf16[8,272,128]{2,1,0:T(8,128)(2,1)S(1)} collective-permute-done((bf16[8,272,128]{2,1,0:T(8,128)(2,1)S(1)}, bf16[8,272,128]{2,1,0:T(8,128)(2,1)S(1)}, u32[]{:S(2)}, u32[]{:S(2)}) %collective-permute-start.19) | collective-permute-done | bytes 557088 | tf_op jit(solution)/shard_map/ppermute | solution.py:844
  370.4 10.4 %collective-permute-done.29 = bf16[1024,256]{1,0:T(8,128)(2,1)} collective-permute-done((bf16[1024,256]{1,0:T(8,128)(2,1)S(1)}, bf16[1024,256]{1,0:T(8,128)(2,1)}, u32[]{:S(2)}, u32[]{:S(2)}) %collective-permute-start.29) | collective-permute-done | bytes 524320 | tf_op jit(solution)/shard_map/ppermute | solution.py:844
  391.9 66.3 %hash_backward.1 = (bf16[2048,256]{1,0:T(8,128)(2,1)S(1)}, bf16[2048,256]{1,0:T(8,128)(2,1)S(1)}, bf16[2048,256]{1,0:T(8,128)(2,1)S(1)}, bf16[2048,256]{1,0:T(8,128)(2,1)}) custom-call(s32[1]{0:T(128)} %bitcast.place, bf16[8,272,128]{2,1,0:T(8,128)(2,1)S(1)} %all-to-all-done.4.g_0, bf16[8,272,128]{2,1,0:T(8,128)(2,1)S(1)} %collective-permute-done.18.g_1, ...), custom_call_target="tpu_custom_call" | custom-call | flops 20000000000 | bytes 12000000 | tf_op jit(solution)/shard_map/hash_backward/pallas_call | solution.py:784
  462.6 24.0 %collective-permute-done.26 = bf16[2048,256]{1,0:T(8,128)(2,1)S(1)} collective-permute-done((bf16[2048,256]{1,0:T(8,128)(2,1)S(1)}, bf16[2048,256]{1,0:T(8,128)(2,1)S(1)}, u32[]{:S(2)}, u32[]{:S(2)}) %collective-permute-start.26) | collective-permute-done | bytes 1048608 | tf_op jit(solution)/shard_map/ppermute | solution.py:844
  492.5 7.7 %fusion.77 = (bf16[1024,1024]{1,0:T(8,128)(2,1)S(1)}, f32[1024,1024]{1,0:T(8,128)}) fusion(bf16[1024,3072]{1,0:T(8,128)(2,1)} %all-gather.6.cloned.1.call-done, f32[1024,1024]{1,0:T(8,128)} %copy-done.31, f32[1024]{0:T(1024)S(1)} %bitcast.201), kind=kOutput, calls=%fused_computation.230 | convolution fusion | flops 2159017984 | bytes 12587008 | tf_op jit(solution)/shard_map/dot_general | solution.py:48
  506.6 11.4 %all-to-all-done.5 = bf16[8,256,256]{1,2,0:T(8,128)(2,1)S(1)} async-done(((bf16[8,256,256]{1,2,0:T(8,128)(2,1)}), bf16[8,256,256]{1,2,0:T(8,128)(2,1)S(1)}, u32[]{:S(2)}, u32[]{:S(2)}) %all-to-all-start.5) | async-done | bytes 1048608 | tf_op jit(solution)/shard_map/all_to_all | solution.py:867
  541.6 10.7 %all-to-all-done.6 = bf16[32,32,256]{2,1,0:T(8,128)(2,1)S(1)} async-done(((bf16[32,32,256]{2,1,0:T(8,128)(2,1)}), bf16[32,32,256]{2,1,0:T(8,128)(2,1)S(1)}, u32[]{:S(2)}, u32[]{:S(2)}) %all-to-all-start.6) | async-done | bytes 524320 | tf_op jit(solution)/shard_map/all_to_all | solution.py:867
  (293 shorter events, 155.2 us)
Async XLA Ops:
  7.2 72.2 %all-gather.4.cloned.1.call-start = ((), (), s32[]{:S(2)}) async-start(), calls=%async_computation.10 | async-start | bytes 4325376 | tf_op jit(solution)/shard_map/all_gather | solution.py:956
  15.8 20.1 %all-to-all-start = ((f32[32,8,256]{2,1,0:T(8,128)}), f32[32,8,256]{2,1,0:T(8,128)S(1)}, u32[]{:S(2)}, u32[]{:S(2)}) async-start(f32[32,8,256]{2,1,0:T(8,128)} %bitcast.35), calls=%async_computation | async-start | bytes 524288 | tf_op jit(solution)/shard_map/all_to_all | solution.py:867
  35.9 16.0 %all-to-all-start.1 = ((bf16[4,32,2048]{2,1,0:T(8,128)(2,1)}), bf16[4,32,2048]{2,1,0:T(8,128)(2,1)S(1)}, u32[]{:S(2)}, u32[]{:S(2)}) async-start(bf16[4,32,2048]{2,1,0:T(8,128)(2,1)} %pad_maximum_fusion.5), calls=%async_computation.1 | async-start | bytes 1048576 | tf_op jit(solution)/shard_map/all_to_all | solution.py:867
  84.0 30.3 %all-to-all-start.2 = ((bf16[8,256,256]{2,1,0:T(8,128)(2,1)}), bf16[8,256,256]{2,1,0:T(8,128)(2,1)S(1)}, u32[]{:S(2)}, u32[]{:S(2)}) async-start(bf16[8,256,256]{2,1,0:T(8,128)(2,1)} %bitcast.125), calls=%async_computation.2 | async-start | bytes 2097152 | tf_op jit(solution)/shard_map/all_to_all | solution.py:867
  88.0 155.9 %all-gather.6.cloned.1.call-start = ((), (), s32[]{:S(2)}) async-start(), calls=%async_computation.11 | async-start | bytes 7077888 | tf_op jit(solution)/shard_map/all_gather | solution.py:974
  115.2 24.3 %collective-permute-start.1 = (bf16[2048,256]{1,0:T(8,128)(2,1)S(1)}, bf16[2048,256]{1,0:T(8,128)(2,1)S(1)}, u32[]{:S(2)}, u32[]{:S(2)}) collective-permute-start(bf16[2048,256]{1,0:T(8,128)(2,1)S(1)} %bitcast.132), channel_id=1, source_target_pairs={{0,2},{1,3},{2,0},{3,1},{4,6},{5,7},{6,4},{7,5},{8,10},{9,11},{10,... | collective-permute-start | bytes 3145736 | tf_op jit(solution)/shard_map/ppermute | solution.py:844
  116.2 23.5 %collective-permute-start = (bf16[2048,256]{1,0:T(8,128)(2,1)S(1)}, bf16[2048,256]{1,0:T(8,128)(2,1)S(1)}, u32[]{:S(2)}, u32[]{:S(2)}) collective-permute-start(bf16[2048,256]{1,0:T(8,128)(2,1)S(1)} %bitcast.133), channel_id=1, source_target_pairs={{0,1},{1,0},{2,3},{3,2},{4,5},{5,4},{6,7},{7,6},{8,9},{9,8},{10,11... | collective-permute-start | bytes 3145736 | tf_op jit(solution)/shard_map/ppermute | solution.py:844
  212.8 30.9 %all-to-all-start.3 = ((bf16[8,256,128]{2,1,0:T(8,128)(2,1)}), bf16[8,256,128]{2,1,0:T(8,128)(2,1)S(1)}, u32[]{:S(2)}, u32[]{:S(2)}) async-start(bf16[8,256,128]{2,1,0:T(8,128)(2,1)} %get-tuple-element.45), calls=%async_computation.3 | async-start | bytes 1048576 | tf_op jit(solution)/shard_map/all_to_all | solution.py:867
  229.4 297.1 %all-gather.8.cloned.1.call-start = ((), (), s32[]{:S(2)}) async-start(), calls=%async_computation.12 | async-start | bytes 4718592 | tf_op jit(solution)/shard_map/all_gather | solution.py:988
  248.0 15.2 %collective-permute-start.7 = (bf16[256,1024]{1,0:T(8,128)(2,1)}, bf16[256,1024]{1,0:T(8,128)(2,1)}, u32[]{:S(2)}, u32[]{:S(2)}) collective-permute-start(bf16[256,1024]{1,0:T(8,128)(2,1)} %add_convert_fusion.4), channel_id=1, source_target_pairs={{0,2},{1,3},{2,0},{3,1},{4,6},{5,7},{6,4},{7,5},{8,10},{9,11},{10,... | collective-permute-start | bytes 1572872 | tf_op jit(solution)/shard_map/ppermute | solution.py:844
  249.4 22.5 %collective-permute-start.13 = (bf16[256,1024]{1,0:T(8,128)(2,1)S(1)}, bf16[256,1024]{1,0:T(8,128)(2,1)}, u32[]{:S(2)}, u32[]{:S(2)}) collective-permute-start(bf16[256,1024]{1,0:T(8,128)(2,1)S(1)} %get-tuple-element.74), channel_id=1, source_target_pairs={{0,2},{1,3},{2,0},{3,1},{4,6},{5,7},{6,4},{7,5},{8,10},{9,11},{10,... | collective-permute-start | bytes 1572872 | tf_op jit(solution)/shard_map/ppermute | solution.py:844
  250.2 21.7 %collective-permute-start.6 = (bf16[256,1024]{1,0:T(8,128)(2,1)}, bf16[256,1024]{1,0:T(8,128)(2,1)S(1)}, u32[]{:S(2)}, u32[]{:S(2)}) collective-permute-start(bf16[256,1024]{1,0:T(8,128)(2,1)} %add_convert_fusion.4), channel_id=1, source_target_pairs={{0,1},{1,0},{2,3},{3,2},{4,5},{5,4},{6,7},{7,6},{8,9},{9,8},{10,11... | collective-permute-start | bytes 1572872 | tf_op jit(solution)/shard_map/ppermute | solution.py:844
  317.4 34.5 %all-to-all-start.4 = ((bf16[8,272,128]{2,1,0:T(8,128)(2,1)}), bf16[8,272,128]{2,1,0:T(8,128)(2,1)S(1)}, u32[]{:S(2)}, u32[]{:S(2)}) async-start(bf16[8,272,128]{2,1,0:T(8,128)(2,1)} %pad_maximum_fusion.4), calls=%async_computation.4 | async-start | bytes 1114112 | tf_op jit(solution)/shard_map/all_to_all | solution.py:867
  322.5 231.0 %reduce-scatter.2.cloned.1.call-start = ((), (), s32[]{:S(2)}) async-start(), calls=%async_computation.13 | async-start | bytes 5308416 | tf_op jit(solution)/shard_map/reduce_scatter | solution.py:1035
  354.4 16.0 %collective-permute-start.27 = (bf16[1024,256]{1,0:T(8,128)(2,1)}, bf16[1024,256]{1,0:T(8,128)(2,1)}, u32[]{:S(2)}, u32[]{:S(2)}) collective-permute-start(bf16[1024,256]{1,0:T(8,128)(2,1)} %get-tuple-element.76), channel_id=1, source_target_pairs={{0,1},{1,0},{2,3},{3,2},{4,5},{5,4},{6,7},{7,6},{8,9},{9,8},{10,11... | collective-permute-start | bytes 1572872 | tf_op jit(solution)/shard_map/ppermute | solution.py:844
  354.9 15.5 %collective-permute-start.19 = (bf16[8,272,128]{2,1,0:T(8,128)(2,1)S(1)}, bf16[8,272,128]{2,1,0:T(8,128)(2,1)S(1)}, u32[]{:S(2)}, u32[]{:S(2)}) collective-permute-start(bf16[8,272,128]{2,1,0:T(8,128)(2,1)S(1)} %all-to-all-done.4.g_0), channel_id=1, source_target_pairs={{0,2},{1,3},{2,0},{3,1},{4,6},{5,7},{6,4},{7,5},{8,10},{9,11},{10,... | collective-permute-start | bytes 1671176 | tf_op jit(solution)/shard_map/ppermute | solution.py:844
  358.4 22.4 %collective-permute-start.29 = (bf16[1024,256]{1,0:T(8,128)(2,1)S(1)}, bf16[1024,256]{1,0:T(8,128)(2,1)}, u32[]{:S(2)}, u32[]{:S(2)}) collective-permute-start(bf16[1024,256]{1,0:T(8,128)(2,1)S(1)} %add_convert_fusion.3), channel_id=1, source_target_pairs={{0,2},{1,3},{2,0},{3,1},{4,6},{5,7},{6,4},{7,5},{8,10},{9,11},{10,... | collective-permute-start | bytes 1572872 | tf_op jit(solution)/shard_map/ppermute | solution.py:844
  359.7 32.2 %collective-permute-start.18 = (bf16[8,272,128]{2,1,0:T(8,128)(2,1)S(1)}, bf16[8,272,128]{2,1,0:T(8,128)(2,1)S(1)}, u32[]{:S(2)}, u32[]{:S(2)}) collective-permute-start(bf16[8,272,128]{2,1,0:T(8,128)(2,1)S(1)} %all-to-all-done.4.g_0), channel_id=1, source_target_pairs={{0,1},{1,0},{2,3},{3,2},{4,5},{5,4},{6,7},{7,6},{8,9},{9,8},{10,11... | collective-permute-start | bytes 1671176 | tf_op jit(solution)/shard_map/ppermute | solution.py:844
  370.4 21.5 %collective-permute-start.20 = (bf16[8,272,128]{2,1,0:T(8,128)(2,1)S(1)}, bf16[8,272,128]{2,1,0:T(8,128)(2,1)S(1)}, u32[]{:S(2)}, u32[]{:S(2)}) collective-permute-start(bf16[8,272,128]{2,1,0:T(8,128)(2,1)S(1)} %collective-permute-done.19.g_2), channel_id=1, source_target_pairs={{0,1},{1,0},{2,3},{3,2},{4,5},{5,4},{6,7},{7,6},{8,9},{9,8},{10,11... | collective-permute-start | bytes 1671176 | tf_op jit(solution)/shard_map/ppermute | solution.py:844
  461.3 25.3 %collective-permute-start.26 = (bf16[2048,256]{1,0:T(8,128)(2,1)S(1)}, bf16[2048,256]{1,0:T(8,128)(2,1)S(1)}, u32[]{:S(2)}, u32[]{:S(2)}) collective-permute-start(bf16[2048,256]{1,0:T(8,128)(2,1)S(1)} %add_convert_fusion.1), channel_id=1, source_target_pairs={{0,2},{1,3},{2,0},{3,1},{4,6},{5,7},{6,4},{7,5},{8,10},{9,11},{10,... | collective-permute-start | bytes 3145736 | tf_op jit(solution)/shard_map/ppermute | solution.py:844
  488.3 29.7 %all-to-all-start.5 = ((bf16[8,256,256]{1,2,0:T(8,128)(2,1)}), bf16[8,256,256]{1,2,0:T(8,128)(2,1)S(1)}, u32[]{:S(2)}, u32[]{:S(2)}) async-start(bf16[8,256,256]{1,2,0:T(8,128)(2,1)} %copy.105), calls=%async_computation.5 | async-start | bytes 2097152 | tf_op jit(solution)/shard_map/all_to_all | solution.py:867
  501.5 35.3 %collective-permute-start.9 = (bf16[256,1024]{1,0:T(8,128)(2,1)}, bf16[256,1024]{1,0:T(8,128)(2,1)}, u32[]{:S(2)}, u32[]{:S(2)}) collective-permute-start(bf16[256,1024]{1,0:T(8,128)(2,1)} %get-tuple-element.80), channel_id=1, source_target_pairs={{0,1},{1,0},{2,3},{3,2},{4,5},{5,4},{6,7},{7,6},{8,9},{9,8},{10,11... | collective-permute-start | bytes 1572872 | tf_op jit(solution)/shard_map/ppermute | solution.py:844
  505.8 31.0 %collective-permute-start.11 = (bf16[256,1024]{1,0:T(8,128)(2,1)}, bf16[256,1024]{1,0:T(8,128)(2,1)}, u32[]{:S(2)}, u32[]{:S(2)}) collective-permute-start(bf16[256,1024]{1,0:T(8,128)(2,1)} %fusion.29), channel_id=1, source_target_pairs={{0,2},{1,3},{2,0},{3,1},{4,6},{5,7},{6,4},{7,5},{8,10},{9,11},{10,... | collective-permute-start | bytes 1572872 | tf_op jit(solution)/shard_map/ppermute | solution.py:844
  533.8 18.5 %all-to-all-start.6 = ((bf16[32,32,256]{2,1,0:T(8,128)(2,1)}), bf16[32,32,256]{2,1,0:T(8,128)(2,1)S(1)}, u32[]{:S(2)}, u32[]{:S(2)}) async-start(bf16[32,32,256]{2,1,0:T(8,128)(2,1)} %bitcast.154), calls=%async_computation.6 | async-start | bytes 1048576 | tf_op jit(solution)/shard_map/all_to_all | solution.py:867
  (53 other events, 748.5 us)
Sparse Core Ops, SparseCore 0:
  11.5 67.9 all-gather.3
  115.3 97.5 all-gather.5
  290.7 80.9 all-gather.7
  386.8 94.3 reduce-scatter.1

commit v4 on v3

--- a/solution.py
+++ b/solution.py
@@ -446,25 +446,32 @@
     return jnp.where(ids == slot_col, 1.0, 0.0).astype(BF)
 
 
-def key_norm(keys):
+def key_factor(keys):
     wide = keys.astype(F32)
-    square = wide * wide
-    high = square.astype(BF)
-    low = (square - high.astype(F32)).astype(BF)
-    ones = jnp.ones((8, keys.shape[1]), BF)
-    return lax.rsqrt((dot_nt(ones, high) + dot_nt(ones, low))[0:1])
-
-
-def span_softmax(raw, norm, key_ids, query_ids, query_starts):
-    factor = norm * SCALE
-    kept = (key_ids < query_ids) & (key_ids >= query_starts)
-    score = jnp.where(
-        key_ids == query_ids, -100000.0, jnp.where(kept, raw * factor, -1000000000.0)
-    )
-    top = jnp.max(score, axis=1, keepdims=True)
-    weight = jnp.exp(score - top)
-    total = jnp.sum(weight, axis=1, keepdims=True)
-    return factor, kept, weight, top, total
+    return lax.rsqrt(jnp.sum(wide * wide, axis=1, keepdims=True)) * SCALE
+
+
+def keep_columns(factors, ids, start, keys, id_column):
+    shape = keys.shape
+    factors[pl.ds(start, shape[0]), :] = jnp.broadcast_to(key_factor(keys), shape)
+    ids[pl.ds(start, shape[0]), :] = jnp.broadcast_to(id_column, shape)
+
+
+def pair_scores(raw, factor, key_ids, query_ids, query_starts):
+    lane = lax.broadcasted_iota(jnp.int32, query_ids.shape, 1)
+    first = jnp.where(lane < SPAN, query_ids, -1.0)
+    second = jnp.where(lane >= SPAN, query_ids, -1.0)
+    scores, masks = [], []
+    for chunk, limits in enumerate((first, query_ids, second)):
+        here = slice(chunk * SPAN, (chunk + 1) * SPAN)
+        ids = key_ids[here]
+        kept = (ids < limits) & (ids >= query_starts)
+        score = jnp.where(kept, raw[here] * factor[here], -1000000000.0)
+        if chunk > 0:
+            score = jnp.where(ids == query_ids, -100000.0, score)
+        scores.append(score)
+        masks.append(kept)
+    return scores, masks
 
 
 def three_parts(wide):
@@ -481,7 +488,6 @@
     x_2,
     x_3,
     info,
-    key_ids,
     out_0,
     out_1,
     out_2,
@@ -489,11 +495,13 @@
     kept_rows,
     lanes,
     heads_out,
+    factors,
+    ids,
 ):
     blocks, tokens = info.shape[0], info.shape[2]
     slots = blocks * CAP_ROWS
     width = x_0.shape[1]
-    spans = tokens // SPAN
+    pairs = tokens // (2 * SPAN)
     turn = place[0]
     rounds = ROUNDS
 
@@ -515,38 +523,48 @@
         part = dot_nn(hot, lanes[block].reshape(slots, width)).astype(BF)
         start = pl.multiple_of(SPAN + block * tokens, SPAN)
         kept_rows[pl.ds(start, tokens), :] = part
+        keep_columns(factors, ids, start, part[:, :HEAD_DIM], cols[:, 0:1])
         return carry
 
     lax.fori_loop(0, blocks, place_rows, 0, unroll=4)
-    kept_rows[0:SPAN, :] = kept_rows[blocks * tokens : blocks * tokens + SPAN, :]
+    for held in (kept_rows, factors, ids):
+        held[0:SPAN, :] = held[blocks * tokens : blocks * tokens + SPAN, :]
+    heads_out[:, :, HEAD_DIM:] = jnp.zeros((blocks, tokens, width - HEAD_DIM), BF)
 
     def attend(block, carry):
-        cols = jnp.transpose(info[block])
-        lane = lax.broadcasted_iota(jnp.int32, (SPAN, width - HEAD_DIM), 1)
         first = []
-        for part in range(spans):
-            span = block * spans + part
-            start = pl.multiple_of(span * SPAN, SPAN)
-            rows = kept_rows[pl.ds(start, 2 * SPAN), :]
-            keys = rows[:, :HEAD_DIM]
-            first.append((rows, dot_nt(rows[SPAN:, :HEAD_DIM], keys), key_norm(keys)))
+        for pair in range(pairs):
+            start = pl.multiple_of(block * tokens + pair * 2 * SPAN, SPAN)
+            rows = kept_rows[pl.ds(start, 3 * SPAN), :]
+            raw = dot_nt(rows[:, :HEAD_DIM], rows[SPAN:, :HEAD_DIM])
+            first.append((start, rows[:, HEAD_DIM:], raw))
         second = []
-        for part in range(spans):
-            rows, raw, norm = first[part]
-            ids = cols[part * SPAN : (part + 1) * SPAN]
-            factor, kept, weight, top, total = span_softmax(
-                raw, norm, key_ids[pl.ds(block * spans + part, 1), :], ids[:, 0:1], ids[:, 1:2]
+        lse = []
+        for pair in range(pairs):
+            start, values, raw = first[pair]
+            here = slice(pair * 2 * SPAN, (pair + 1) * 2 * SPAN)
+            scores, _ = pair_scores(
+                raw,
+                factors[pl.ds(start, 3 * SPAN), :],
+                ids[pl.ds(start, 3 * SPAN), :],
+                info[block, 0:1, here],
+                info[block, 1:2, here],
             )
-            high, mid, low = three_parts(top + jnp.log(total))
-            extra = jnp.where(
-                lane == 0, high, jnp.where(lane == 1, mid, jnp.where(lane == 2, low, 0.0))
-            ).astype(BF)
-            second.append(((weight * (1.0 / total)).astype(BF), extra))
-        for part in range(spans):
-            probs, extra = second[part]
-            here = slice(part * SPAN, (part + 1) * SPAN)
-            heads_out[block, here, :HEAD_DIM] = dot_nn(probs, first[part][0][:, HEAD_DIM:]).astype(BF)
-            heads_out[block, here, HEAD_DIM:] = extra
+            top = jnp.max(
+                jnp.maximum(jnp.maximum(scores[0], scores[1]), scores[2]), axis=0, keepdims=True
+            )
+            weights = [jnp.exp(score - top) for score in scores]
+            total = jnp.sum(weights[0] + weights[1] + weights[2], axis=0, keepdims=True)
+            scale = 1.0 / total
+            second.append(jnp.concatenate([weight * scale for weight in weights]).astype(BF))
+            lse.append(top + jnp.log(total))
+        for pair in range(pairs):
+            here = slice(pair * 2 * SPAN, (pair + 1) * 2 * SPAN)
+            heads_out[block, here, :HEAD_DIM] = dot_tn(second[pair], first[pair][1]).astype(BF)
+        high, mid, low = three_parts(jnp.concatenate(lse, axis=1))
+        row = lax.broadcasted_iota(jnp.int32, (PARTS, tokens), 0)
+        flat = jnp.where(row == 0, high, jnp.where(row == 1, mid, jnp.where(row == 2, low, 0.0)))
+        heads_out[block, :, HEAD_DIM : HEAD_DIM + PARTS] = jnp.transpose(flat).astype(BF)
         return carry
 
     lax.fori_loop(0, blocks, attend, 0)
@@ -646,18 +664,21 @@
     l_3,
     kept_rows,
     info,
-    key_ids,
     out_0,
     out_1,
     out_2,
     out_3,
     lanes,
     sums,
+    factors,
+    ids,
+    rows_in,
+    stats,
 ):
     blocks, tokens = info.shape[0], info.shape[2]
     slots = blocks * CAP_ROWS
     width = kept_rows.shape[1]
-    spans = tokens // SPAN
+    pairs = tokens // (2 * SPAN)
 
     for offset, grads, lse in ((0, g_0, l_0), (1, g_1, l_1), (2, g_2, l_2), (3, g_3, l_3)):
 
@@ -677,74 +698,75 @@
 
     sums[0:SPAN, :] = jnp.zeros((SPAN, width), F32)
 
-    def attend(block, carry):
+    def place_rows(block, carry):
         cols = jnp.transpose(info[block])
         hot = hot_cols(cols[:, 2:3], slots)
-        part_grads = dot_nn(hot, lanes[block].reshape(slots, width))
-        grad_rows = part_grads[:, :HEAD_DIM]
-
-        def summed(first):
-            return sum(
-                (part_grads[:, first + at : first + at + 1] for at in (1, 2)),
-                part_grads[:, first : first + 1],
-            )
-
-        pull = summed(HEAD_DIM)
-        total_lse = summed(HEAD_DIM + PARTS)
+        part = dot_nn(hot, lanes[block].reshape(slots, width))
+        rows_in[block] = part[:, :HEAD_DIM].astype(BF)
+        flat = jnp.transpose(part[:, HEAD_DIM:])
+        stats[block, 0:1, :] = flat[0:1] + flat[1:2] + flat[2:3]
+        stats[block, 1:2, :] = flat[PARTS : PARTS + 1] + (
+            flat[PARTS + 1 : PARTS + 2] + flat[PARTS + 2 : PARTS + 3]
+        )
+        start = pl.multiple_of(SPAN + block * tokens, SPAN)
+        keys = kept_rows[pl.ds(start, tokens), :HEAD_DIM]
+        keep_columns(factors, ids, start, keys, cols[:, 0:1])
+        return carry
+
+    lax.fori_loop(0, blocks, place_rows, 0, unroll=4)
+    for held in (factors, ids):
+        held[0:SPAN, :] = held[blocks * tokens : blocks * tokens + SPAN, :]
+
+    def attend(block, carry):
         first = []
-        for part in range(spans):
-            span = block * spans + part
-            start = pl.multiple_of(span * SPAN, SPAN)
-            rows = kept_rows[pl.ds(start, 2 * SPAN), :]
+        for pair in range(pairs):
+            start = pl.multiple_of(block * tokens + pair * 2 * SPAN, SPAN)
+            here = slice(pair * 2 * SPAN, (pair + 1) * 2 * SPAN)
+            rows = kept_rows[pl.ds(start, 3 * SPAN), :]
             keys = rows[:, :HEAD_DIM]
             queries = rows[SPAN:, :HEAD_DIM]
-            raw = dot_nt(queries, keys)
-            first.append((start, keys, queries, rows[:, HEAD_DIM:], raw, key_norm(keys)))
-        middle = []
-        for part in range(spans):
-            start, keys, queries, values, raw, norm = first[part]
-            here = slice(part * SPAN, (part + 1) * SPAN)
-            ids = cols[here]
-            factor, kept, weight, top, total = span_softmax(
-                raw, norm, key_ids[pl.ds(block * spans + part, 1), :], ids[:, 0:1], ids[:, 1:2]
+            grads = rows_in[block, here, :]
+            raw = dot_nt(keys, queries)
+            back = dot_nt(rows[:, HEAD_DIM:], grads)
+            first.append((start, keys, queries, grads, raw, back))
+        second = []
+        for pair in range(pairs):
+            start, keys, queries, grads, raw, back = first[pair]
+            here = slice(pair * 2 * SPAN, (pair + 1) * 2 * SPAN)
+            factor = factors[pl.ds(start, 3 * SPAN), :]
+            scores, masks = pair_scores(
+                raw,
+                factor,
+                ids[pl.ds(start, 3 * SPAN), :],
+                info[block, 0:1, here],
+                info[block, 1:2, here],
             )
-            merge = jnp.exp(top + jnp.log(total) - total_lse[here])
-            grad_out = (merge * grad_rows[here]).astype(BF)
-            middle.append((factor, kept, weight * (1.0 / total), grad_out, merge * pull[here]))
-        back = [dot_nt(middle[part][3], first[part][3]) for part in range(spans)]
-        second = []
-        slopes = []
-        for part in range(spans):
-            raw, norm = first[part][4:]
-            factor, kept, probs, grad_out, pulled = middle[part]
-            grad_score = jnp.where(kept, probs * (back[part] - pulled), 0.0)
-            slopes.append(
-                jnp.sum(grad_score * raw, axis=0, keepdims=True) * SCALE * norm * norm * norm
+            pull = stats[block, 0:1, here]
+            total_lse = stats[block, 1:2, here]
+            weights = [jnp.exp(score - total_lse) for score in scores]
+            weights_all = jnp.concatenate(weights).astype(BF)
+            grad_score = jnp.concatenate(
+                [
+                    jnp.where(
+                        mask, weight * (back[chunk * SPAN : (chunk + 1) * SPAN] - pull), 0.0
+                    )
+                    for chunk, (mask, weight) in enumerate(zip(masks, weights))
+                ]
             )
-            second.append(((grad_score * factor).astype(BF), probs.astype(BF)))
-        held = []
-        for part in range(spans):
-            start, keys, queries = first[part][:3]
-            grad_raw, probs = second[part]
-            held.append(
-                (
-                    start,
-                    keys,
-                    dot_nn(grad_raw, keys),
-                    dot_tn(grad_raw, queries),
-                    dot_tn(probs, middle[part][3]),
-                )
-            )
-        slopes.append(jnp.zeros((8 - spans, 2 * SPAN), F32))
-        slope_cols = jnp.transpose(jnp.concatenate(slopes, axis=0))
-        for part in range(spans):
-            start, keys, grad_query, grad_key, grad_val = held[part]
-            grad_key = grad_key - slope_cols[:, part : part + 1] * keys.astype(F32)
+            slope = jnp.sum(grad_score * raw, axis=1, keepdims=True)
+            drift = slope * (factor * factor * factor * HEAD_DIM) * keys.astype(F32)
+            second.append(((grad_score * factor).astype(BF), weights_all, drift))
+        for pair in range(pairs):
+            start, keys, queries, grads = first[pair][:4]
+            grad_raw, weights_all, drift = second[pair]
+            grad_val = dot_nn(weights_all, grads)
+            grad_key = dot_nn(grad_raw, queries) - drift
+            grad_query = dot_tn(grad_raw, keys)
             sums[pl.ds(start, SPAN), :] += jnp.concatenate(
                 [grad_key[:SPAN], grad_val[:SPAN]], axis=1
             )
             after = pl.multiple_of(start + SPAN, SPAN)
-            sums[pl.ds(after, SPAN), :] = jnp.concatenate(
+            sums[pl.ds(after, 2 * SPAN), :] = jnp.concatenate(
                 [grad_query + grad_key[SPAN:], grad_val[SPAN:]], axis=1
             )
         return carry
@@ -797,29 +819,32 @@
     )(*operands)
 
 
-def run_forward(turn, rows, info, key_ids):
+def run_forward(turn, rows, info):
     blocks, _, tokens = info.shape
     width = rows[0].shape[1]
     tall = tokens + PARTS * tokens // HEAD_DIM
     return run_kernel(
         forward_kernel,
         "hash_forward",
-        (turn, *rows, info, key_ids),
+        (turn, *rows, info),
         [(blocks // ROUNDS, tall, HEAD_DIM)] * ROUNDS + [(SPAN + blocks * tokens, width)],
-        [((blocks, blocks, CAP_ROWS, width), BF), ((blocks, tokens, width), BF)],
+        [((blocks, blocks, CAP_ROWS, width), BF), ((blocks, tokens, width), BF)]
+        + [((SPAN + blocks * tokens, HEAD_DIM), F32)] * 2,
         True,
     )
 
 
-def run_backward(turn, grads, lse, kept_rows, info, key_ids):
+def run_backward(turn, grads, lse, kept_rows, info):
     blocks, _, tokens = info.shape
     width = kept_rows.shape[1]
     return run_kernel(
         backward_kernel,
         "hash_backward",
-        (turn, *grads, *lse, kept_rows, info, key_ids),
+        (turn, *grads, *lse, kept_rows, info),
         [(blocks * tokens // ROUNDS, width)] * ROUNDS,
-        [((blocks, blocks, CAP_ROWS, width), BF), ((SPAN + blocks * tokens, width), F32)],
+        [((blocks, blocks, CAP_ROWS, width), BF), ((SPAN + blocks * tokens, width), F32)]
+        + [((SPAN + blocks * tokens, HEAD_DIM), F32)] * 2
+        + [((blocks, tokens, HEAD_DIM), BF), ((blocks, 8, tokens), F32)],
         True,
     )
 
@@ -947,9 +972,6 @@
     wide = bias_up.shape[0]
     b_up = vector(4 * shard, wide)
     b_down = vector(4 * shard + wide, shard)
-    spans = info[:, 0].reshape(devices * tokens // SPAN, SPAN)
-    key_ids = jnp.concatenate([jnp.roll(spans, 1, axis=0), spans], axis=1)
-
     pair = jnp.stack(
         [w_qk.reshape(shard, HEADS, HEAD_DIM), w_value.reshape(shard, HEADS, HEAD_DIM)], axis=2
     ).reshape(shard, 2 * features)
@@ -966,7 +988,11 @@
     ).reshape(HEADS * wide)
 
     normed_one, hat_one, inv_one = layer_norm(x_second, gain_one, shift_one)
-    normed_one, near_rows = lax.optimization_barrier((normed_one.astype(BF), near_rows))
+    grad_f = dy_second.astype(BF)
+    normed_one, near_rows, grad_f_all = lax.optimization_barrier(
+        (normed_one.astype(BF), near_rows, gather_group(grad_f))
+    )
+    grad_f_all = jnp.concatenate(grad_f_all)
     rows = linear(normed_one, m_pair).astype(BF)
     rows = jnp.transpose(rows.reshape(tokens, HEADS, 2 * HEAD_DIM), (1, 0, 2))
     own = exchange(rows, columns()).reshape(HEADS * tokens, 2 * HEAD_DIM)
@@ -980,11 +1006,12 @@
     )
     m_up, m_out, m_down = (m_ffn[:, at : at + features] for at in (0, half, half + features))
     turn = (place % ROUNDS).astype(jnp.int32).reshape(1)
-    *sent, kept_rows = run_forward(turn, gather_group(own), info, key_ids)
+    *sent, kept_rows = run_forward(turn, gather_group(own), info)
     far = merge_pair(sent[2], swap(sent[3], 1))
     mixed, total_lse = merge_final(sent[0], swap(sent[1], 1), swap(far, 2))
     mixed = exchange(mixed, columns())
-    mixed, normed_one = lax.optimization_barrier((mixed, normed_one))
+    grad_hidden = outer_cols(grad_f_all, m_down)
+    mixed, normed_one, grad_hidden = lax.optimization_barrier((mixed, normed_one, grad_hidden))
     normed_col = lax.all_gather(
         normed_one, "seq", axis=0, tiled=True, axis_index_groups=columns()
     )
@@ -992,8 +1019,6 @@
     y_first = x_first + linear(mixed, m_out)
     normed_two, hat_two, inv_two = layer_norm(y_first, gain_two, shift_two)
     normed_two = normed_two.astype(BF)
-    grad_f = dy_second.astype(BF)
-    grad_f_all = jnp.concatenate(gather_group(grad_f))
     normed_all = jnp.concatenate(gather_group(normed_two))
     pre_up = linear(normed_all, m_up) + b_up
     hidden, gelu_back = jax.vjp(partial(jax.nn.gelu, approximate=True), pre_up)
@@ -1002,7 +1027,7 @@
     y_second = x_second + (branch + b_down)
     grad_down = inner_rows(hidden, grad_f_all)
     grad_bias_down = jnp.sum(grad_f.astype(F32), axis=0)
-    grad_pre = gelu_back(outer_cols(grad_f_all, m_down))[0].astype(BF)
+    grad_pre = gelu_back(grad_hidden)[0].astype(BF)
     grad_up = inner_rows(normed_all, grad_pre)
     grad_bias_up = jnp.sum(grad_pre.astype(F32), axis=0)
     grad_two = sum_group(outer_cols(grad_pre, m_up).reshape(ROUNDS, tokens, features))
@@ -1022,9 +1047,6 @@
     parts = parts.reshape(HEADS, -1, HEAD_DIM).astype(BF)
     grad_mixed = jnp.transpose(grad_mixed.reshape(tokens, HEADS, HEAD_DIM), (1, 0, 2))
     grad_mixed = exchange(jnp.concatenate([grad_mixed, parts], axis=1), columns())
-    grad_mixed, grad_up, grad_down, grad_out = lax.optimization_barrier(
-        (grad_mixed, grad_up, grad_down, grad_out)
-    )
     grad_out = sum_group(
         [
             lax.dynamic_slice_in_dim(grad_out, ((place % ROUNDS) ^ near) * fourth, fourth, axis=1)
@@ -1032,26 +1054,33 @@
         ]
     )
     merged = jnp.concatenate([x.astype(BF) for x in (grad_up, grad_out, grad_down)], axis=1)
+    grad_mixed, merged = lax.optimization_barrier((grad_mixed, merged))
     merged = lax.psum_scatter(
         merged, "seq", scatter_dimension=0, tiled=True, axis_index_groups=columns()
     )
     s_down = merged[:, half + fourth :].astype(F32)
-    merged = exchange(merged[:, : half + fourth].reshape(ROUNDS, shard, -1), rows_of())
-    s_up = jnp.transpose(merged[:, :, :half].reshape(ROUNDS, shard, HEADS, wide), (1, 2, 0, 3))
-    s_up = s_up.reshape(shard, ROUNDS * half).astype(F32)
-    s_out = jnp.transpose(merged[:, :, half:], (1, 0, 2)).reshape(shard, features).astype(F32)
+    merged = merged[:, : half + fourth].reshape(ROUNDS, shard, -1)
+    s_up = jnp.zeros((shard, HEADS, ROUNDS, wide), F32)
+    s_out = jnp.zeros((shard, features), F32)
+    for near in range(ROUNDS):
+        peer = (place % ROUNDS) ^ near
+        piece = lax.dynamic_index_in_dim(merged, peer, axis=0, keepdims=False)
+        piece = (swap(piece, near) if near else piece).astype(F32)
+        s_up = lax.dynamic_update_slice(
+            s_up, piece[:, :half].reshape(shard, HEADS, 1, wide), (0, 0, peer, 0)
+        )
+        s_out = lax.dynamic_update_slice(s_out, piece[:, half:], (0, peer * fourth))
+    s_up = s_up.reshape(shard, ROUNDS * half)
 
     grad_head = run_backward(
-        turn, gather_group(grad_mixed), gather_group(total_lse), kept_rows, info, key_ids
+        turn, gather_group(grad_mixed), gather_group(total_lse), kept_rows, info
     )
     grad_head = sum_group([x.astype(F32) for x in grad_head]).astype(BF)
     grad_rows = exchange(grad_head.reshape(HEADS, tokens, 2 * HEAD_DIM), columns())
-    grad_rows, grad_head = lax.optimization_barrier((grad_rows, grad_head))
+    s_pair = inner_rows(normed_col, grad_head).astype(BF).reshape(devices, shard, 2 * HEAD_DIM)
+    grad_rows, s_pair = lax.optimization_barrier((grad_rows, s_pair))
     grad_rows = jnp.transpose(grad_rows, (1, 0, 2)).reshape(tokens, 2 * features)
-
-    s_pair = exchange(
-        inner_rows(normed_col, grad_head).astype(BF).reshape(devices, shard, 2 * HEAD_DIM)
-    )
+    s_pair = exchange(s_pair)
     s_pair = jnp.sum(
         s_pair.reshape(HEADS, ROUNDS, shard, 2, HEAD_DIM).astype(F32), axis=1
     ).transpose(2, 1, 0, 3)
@@ -1074,6 +1103,7 @@
         ],
         axis=1,
     )
+    small, s_qk, s_value = lax.optimization_barrier((small, s_qk, s_value))
     small = jnp.sum(exchange(small[:, None]), axis=(0, 1))
     s_gattn, s_battn, s_gffn, s_bffn = (small[i * shard : (i + 1) * shard] for i in range(4))
     s_bup = small[4 * shard : 4 * shard + wide]

time: 580 us -> 538 us (0.928)
  waiting for transfers between devices: 260 us -> 207 us
  local copies, waits for them, and re-layouts: 22.4 us -> 56.4 us
  Pallas kernels: 120 us -> 99.8 us
  starting transfers between devices: 64.8 us -> 55.6 us
    all_to_all x9 -> x8, waiting for transfers between devices: 103 us -> 72.6 us  [exchange(): lax.all_to_all(x, 'seq', split_axis=0, concat_axis=0, tiled=True, axis_in...]
    ppermute x30 -> x33, waiting for transfers between devices: 129 us -> 107 us  [swap(): return lax.ppermute(x, 'seq', peers(mask))]
    pallas_call x4, Pallas kernels: 120 us -> 99.8 us  [run_kernel(): pl.pallas_call(kernel, out_shape=tuple((jax.ShapeDtypeStruct(shape, BF) f...]
    unnamed x73 -> x90, local copies, waits for them, and re-layouts: 2.78 us -> 22.8 us
    all_to_all x9 -> x8, starting transfers between devices: 50.1 us -> 36.4 us  [exchange(): lax.all_to_all(x, 'seq', split_axis=0, concat_axis=0, tiled=True, axis_in...]
    dynamic_update_slice x0 -> x8, local copies, waits for them, and re-layouts: none -> 10.8 us  [the longest x4 10.7 us: shards_fast(): lax.dynamic_update_slice(s_up, piece[:, :half].reshape(shard, HEADS, 1, w...]
    ppermute x30 -> x33, starting transfers between devices: 14.6 us -> 18.8 us  [swap(): return lax.ppermute(x, 'seq', peers(mask))]
  transfers between devices with their start and end apart: 43 -> 45, of which waited for: 26 -> 24; matrix products, arithmetic and copies ran while one was open for 14% -> 23% of each run, Pallas kernels for 21% -> 19%
where the time goes in v4:
time: 538 us; the launch traced here: 528 us
  waiting for transfers between devices  207 us (38%)
  Pallas kernels  99.8 us (19%)
  matrix products  60.6 us (11%)
  local copies, waits for them, and re-layouts  56.4 us (10%)
  starting transfers between devices  55.6 us (10%)
  other arithmetic  32.8 us (6%)
  between operations  15.3 us (3%)
    ppermute x33, waiting for transfers between devices, swap(): return lax.ppermute(x, 'seq', peers(mask))  107 us
    pallas_call x4, Pallas kernels, run_kernel(): pl.pallas_call(kernel, out_shape=tuple((jax.ShapeDtypeStruct(shape, BF) f...  99.8 us
    all_to_all x8, waiting for transfers between devices, exchange(): lax.all_to_all(x, 'seq', split_axis=0, concat_axis=0, tiled=True, axis_in...  72.6 us
    all_to_all x8, starting transfers between devices, exchange(): lax.all_to_all(x, 'seq', split_axis=0, concat_axis=0, tiled=True, axis_in...  36.4 us
    all_gather x1, waiting for transfers between devices, shards_fast(): m_pair = lax.all_gather(pair.astype(BF), 'seq', axis=0, tiled=True)  27.8 us
    dot_general x4, matrix products, linear(): return jnp.dot(matrix_a, matrix_b, preferred_element_type=jnp.float32)  23.7 us
    unnamed x90, local copies, waits for them, and re-layouts  22.8 us
    dot_general x4, matrix products, outer_cols(): lax.dot_general(matrix_a, matrix_b, (((1,), (1,)), ((), ())), preferred_e...  20.4 us
  transfers between devices with their start and end apart: 45, of which 24 were waited for; matrix products, arithmetic and copies ran while one was open for 23% of the time, Pallas kernels for 19%

profile of v4, /device:TPU:0, one launch (start us, length us, event | category | flops | bytes accessed | tf_op | source)
XLA Modules:
  0.0 527.9 jit_solution(3226770237254816557)
XLA Ops:
  20.7 5.0 all-to-all-start
  28.7 9.4 %all-to-all-done.info = f32[32,8,256]{2,1,0:T(8,128)S(1)} async-done(((f32[32,8,256]{2,1,0:T(8,128)}), f32[32,8,256]{2,1,0:T(8,128)S(1)}, u32[]{:S(2)}, u32[]{:S(2)}) %all-to-all-start) | async-done | bytes 262176 | tf_op jit(solution)/shard_map/all_to_all | solution.py:892
  43.4 8.4 %all-to-all-done.1 = bf16[4,32,2048]{2,1,0:T(8,128)(2,1)S(1)} async-done(((bf16[4,32,2048]{2,1,0:T(8,128)(2,1)}), bf16[4,32,2048]{2,1,0:T(8,128)(2,1)S(1)}, u32[]{:S(2)}, u32[]{:S(2)}) %all-to-all-start.1) | async-done | bytes 524320 | tf_op jit(solution)/shard_map/all_to_all | solution.py:892
  51.9 27.8 %all-gather.4.cloned.1.call-done = bf16[1024,2048]{1,0:T(8,128)(2,1)} async-done(((bf16[32,2048]{1,0:T(8,128)(2,1)}), bf16[1024,2048]{1,0:T(8,128)(2,1)}) %all-gather.4.cloned.1.call-update) | async-done | bytes 4194320 | tf_op jit(solution)/shard_map/all_gather | solution.py:978
  88.4 26.1 %all-to-all-done.2 = bf16[8,256,256]{2,1,0:T(8,128)(2,1)S(1)} async-done(((bf16[8,256,256]{2,1,0:T(8,128)(2,1)}), bf16[8,256,256]{2,1,0:T(8,128)(2,1)S(1)}, u32[]{:S(2)}, u32[]{:S(2)}) %all-to-all-start.2) | async-done | bytes 1048608 | tf_op jit(solution)/shard_map/all_to_all | solution.py:892
  116.5 23.3 %collective-permute-done.4.x_2 = bf16[2048,256]{1,0:T(8,128)(2,1)S(1)} collective-permute-done((bf16[2048,256]{1,0:T(8,128)(2,1)S(1)}, bf16[2048,256]{1,0:T(8,128)(2,1)S(1)}, u32[]{:S(2)}, u32[]{:S(2)}) %collective-permute-start.4) | collective-permute-done | bytes 1048608 | tf_op jit(solution)/shard_map/ppermute | solution.py:869
  143.4 44.9 %hash_forward.1 = (bf16[8,272,128]{2,1,0:T(8,128)(2,1)S(1)}, bf16[8,272,128]{2,1,0:T(8,128)(2,1)S(1)}, bf16[8,272,128]{2,1,0:T(8,128)(2,1)S(1)}, bf16[8,272,128]{2,1,0:T(8,128)(2,1)S(1)}, bf16[8256,256]{1,0:T(8,128)(2,1)}) custom-call(s32[1]{0:T(128)} %bitcast.place, bf16[2048,256]{1,0:T(8,128)(2,1)S(1)} %bitcast.162, ...), custom_call_target="tpu_custom_call" | custom-call | flops 20000000000 | bytes 12000000 | tf_op jit(solution)/shard_map/hash_forward/pallas_call | solution.py:806
  199.9 8.8 %collective-permute-done.8.c = bf16[8,272,128]{2,1,0:T(8,128)(2,1)S(1)} collective-permute-done((bf16[8,272,128]{2,1,0:T(8,128)(2,1)S(1)}, bf16[8,272,128]{2,1,0:T(8,128)(2,1)S(1)}, u32[]{:S(2)}, u32[]{:S(2)}) %collective-permute-start.8) | collective-permute-done | bytes 557088 | tf_op jit(solution)/shard_map/ppermute | solution.py:869
  223.7 6.7 %fusion.17 = f32[1024,1024]{1,0:T(8,128)} fusion(bf16[1024,1024]{1,0:T(8,128)(2,1)} %constant_dynamic-update-slice_fusion, bf16[1024,3072]{1,0:T(8,128)(2,1)} %all-gather.6.cloned.1.call-done), kind=kOutput, calls=%fused_computation.28 | convolution fusion | flops 2147483648 | bytes 8388608 | tf_op jit(solution)/shard_map/dot_general | solution.py:58
  236.4 11.2 %collective-permute-done.10 = bf16[256,1024]{1,0:T(8,128)(2,1)S(1)} collective-permute-done((bf16[256,1024]{1,0:T(8,128)(2,1)S(1)}, bf16[256,1024]{1,0:T(8,128)(2,1)S(1)}, u32[]{:S(2)}, u32[]{:S(2)}) %collective-permute-start.10) | collective-permute-done | bytes 524320 | tf_op jit(solution)/shard_map/ppermute | solution.py:869
  249.6 10.1 %convert_reduce_fusion = (f32[1024]{0:T(1024)S(1)}, bf16[1024,1024]{1,0:T(8,128)(2,1)S(1)}, f32[1024,1024]{1,0:T(8,128)}) fusion(f32[1024,1024]{1,0:T(8,128)} %fusion.17, f32[1024]{0:T(1024)S(1)} %bitcast.225, bf16[1024,3072]{1,0:T(8,128)(2,1)} %all-gather.6.cloned.1.call-done, bf16[256,1024]{1,0:T(8,128)(2,1)} %collective-permute-done.11, ...), kind=kOutput, calls=%fused_computation.10 | convolution fusion | flops 2179988480 | bytes 14688256 | tf_op jit(solution)/shard_map/dot_general | solution.py:48
  259.7 6.8 %fusion.71 = (bf16[1024,1024]{1,0:T(8,128)(2,1)S(1)}, f32[1024,1024]{1,0:T(8,128)}) fusion(bf16[1024,1024]{1,0:T(8,128)(2,1)S(1)} %get-tuple-element.178, bf16[1024,3072]{1,0:T(8,128)(2,1)} %all-gather.6.cloned.1.call-done), kind=kOutput, calls=%fused_computation.236 | convolution fusion | flops 2148532224 | bytes 10485760 | tf_op jit(solution)/shard_map/dot_general | solution.py:58
  272.2 6.8 %convolution_convert_fusion.1 = bf16[1024,1024]{0,1:T(8,128)(2,1)} fusion(bf16[1024,1024]{1,0:T(8,128)(2,1)} %constant_dynamic-update-slice_fusion, f32[1024,1024]{1,0:T(8,128)} %get-tuple-element.229, f32[1024]{0:T(1024)S(1)} %bitcast.226), kind=kOutput, calls=%fused_computation.16 | convolution fusion | flops 2159017984 | bytes 8392704 | tf_op jit(solution)/shard_map/dot_general | solution.py:52
  279.0 6.2 %collective-permute-done.17 = bf16[256,1024]{1,0:T(8,128)(2,1)S(1)} collective-permute-done((bf16[256,1024]{1,0:T(8,128)(2,1)S(1)}, bf16[256,1024]{1,0:T(8,128)(2,1)S(1)}, u32[]{:S(2)}, u32[]{:S(2)}) %collective-permute-start.17) | collective-permute-done | bytes 524320 | tf_op jit(solution)/shard_map/ppermute | solution.py:869
  309.4 8.1 %collective-permute-done.20 = bf16[1024,256]{0,1:T(8,128)(2,1)S(1)} collective-permute-done((bf16[1024,256]{0,1:T(8,128)(2,1)S(1)}, bf16[1024,256]{0,1:T(8,128)(2,1)S(1)}, u32[]{:S(2)}, u32[]{:S(2)}) %collective-permute-start.20) | collective-permute-done | bytes 524320 | tf_op jit(solution)/shard_map/ppermute | solution.py:869
  321.6 5.9 %all-to-all-done.4.g_0 = bf16[8,272,128]{2,1,0:T(8,128)(2,1)S(1)} async-done(((bf16[8,272,128]{2,1,0:T(8,128)(2,1)}), bf16[8,272,128]{2,1,0:T(8,128)(2,1)S(1)}, u32[]{:S(2)}, u32[]{:S(2)}) %all-to-all-start.4) | async-done | bytes 557088 | tf_op jit(solution)/shard_map/all_to_all | solution.py:892
  328.6 11.3 %collective-permute-done.22.g_2 = bf16[8,272,128]{2,1,0:T(8,128)(2,1)S(1)} collective-permute-done((bf16[8,272,128]{2,1,0:T(8,128)(2,1)S(1)}, bf16[8,272,128]{2,1,0:T(8,128)(2,1)S(1)}, u32[]{:S(2)}, u32[]{:S(2)}) %collective-permute-start.22) | collective-permute-done | bytes 557088 | tf_op jit(solution)/shard_map/ppermute | solution.py:869
  339.9 6.8 %copy.137 = bf16[1024,2304]{1,0:T(8,128)(2,1)} copy(bf16[1024,2304]{0,1:T(8,128)(2,1)} %pad_maximum_fusion) | data formatting | bytes 9437184
  355.6 46.3 %hash_backward.1 = (bf16[2048,256]{1,0:T(8,128)(2,1)S(1)}, bf16[2048,256]{1,0:T(8,128)(2,1)S(1)}, bf16[2048,256]{1,0:T(8,128)(2,1)S(1)}, bf16[2048,256]{1,0:T(8,128)(2,1)}) custom-call(s32[1]{0:T(128)} %bitcast.place, bf16[8,272,128]{2,1,0:T(8,128)(2,1)S(1)} %all-to-all-done.4.g_0, bf16[8,272,128]{2,1,0:T(8,128)(2,1)S(1)} %copy-done.1, ...), custom_call_target="tpu_custom_call" | custom-call | flops 20000000000 | bytes 12000000 | tf_op jit(solution)/shard_map/hash_backward/pallas_call | solution.py:806
  406.5 23.9 %collective-permute-done.29 = bf16[2048,256]{1,0:T(8,128)(2,1)} collective-permute-done((bf16[2048,256]{1,0:T(8,128)(2,1)S(1)}, bf16[2048,256]{1,0:T(8,128)(2,1)}, u32[]{:S(2)}, u32[]{:S(2)}) %collective-permute-start.29) | collective-permute-done | bytes 1048608 | tf_op jit(solution)/shard_map/ppermute | solution.py:869
  433.7 7.3 %all-to-all-start.5 = ((bf16[8,256,256]{1,2,0:T(8,128)(2,1)}), bf16[8,256,256]{1,2,0:T(8,128)(2,1)S(1)}, u32[]{:S(2)}, u32[]{:S(2)}) async-start(bf16[8,256,256]{1,2,0:T(8,128)(2,1)} %copy.128), calls=%async_computation.5 | async-start | bytes 2097152 | tf_op jit(solution)/shard_map/all_to_all | solution.py:892
  441.8 7.8 %fusion.72 = (bf16[1024,1024]{1,0:T(8,128)(2,1)S(1)}, f32[1024,1024]{1,0:T(8,128)}) fusion(bf16[1024,3072]{1,0:T(8,128)(2,1)} %all-gather.6.cloned.1.call-done, f32[1024,1024]{1,0:T(8,128)} %get-tuple-element.229, f32[1024]{0:T(1024)S(1)} %bitcast.227), kind=kOutput, calls=%fused_computation.237 | convolution fusion | flops 2159017984 | bytes 12587008 | tf_op jit(solution)/shard_map/dot_general | solution.py:48
  455.6 11.4 %all-to-all-done.5 = bf16[8,256,256]{1,2,0:T(8,128)(2,1)S(1)} async-done(((bf16[8,256,256]{1,2,0:T(8,128)(2,1)}), bf16[8,256,256]{1,2,0:T(8,128)(2,1)S(1)}, u32[]{:S(2)}, u32[]{:S(2)}) %all-to-all-start.5) | async-done | bytes 1048608 | tf_op jit(solution)/shard_map/all_to_all | solution.py:892
  480.4 5.9 %all-to-all-done.6 = bf16[32,32,256]{2,1,0:T(8,128)(2,1)} async-done(((bf16[32,32,256]{2,1,0:T(8,128)(2,1)}), bf16[32,32,256]{2,1,0:T(8,128)(2,1)}, u32[]{:S(2)}, u32[]{:S(2)}) %all-to-all-start.6) | async-done | bytes 524320 | tf_op jit(solution)/shard_map/all_to_all | solution.py:892
  (320 shorter events, 176.3 us)
Async XLA Ops:
  7.2 72.5 %all-gather.4.cloned.1.call-start = ((), (), s32[]{:S(2)}) async-start(), calls=%async_computation.9 | async-start | bytes 4325376 | tf_op jit(solution)/shard_map/all_gather | solution.py:978
  12.3 15.8 %collective-permute-start.1 = (bf16[256,1024]{1,0:T(8,128)(2,1)S(1)}, bf16[256,1024]{1,0:T(8,128)(2,1)S(1)}, u32[]{:S(2)}, u32[]{:S(2)}) collective-permute-start(bf16[256,1024]{1,0:T(8,128)(2,1)S(1)} %get-tuple-element.52), channel_id=1, source_target_pairs={{0,2},{1,3},{2,0},{3,1},{4,6},{5,7},{6,4},{7,5},{8,10},{9,11},{10,... | collective-permute-start | bytes 1572872 | tf_op jit(solution)/shard_map/ppermute | solution.py:869
  15.3 36.6 %collective-permute-start = (bf16[256,1024]{1,0:T(8,128)(2,1)S(1)}, bf16[256,1024]{1,0:T(8,128)(2,1)}, u32[]{:S(2)}, u32[]{:S(2)}) collective-permute-start(bf16[256,1024]{1,0:T(8,128)(2,1)S(1)} %get-tuple-element.52), channel_id=1, source_target_pairs={{0,1},{1,0},{2,3},{3,2},{4,5},{5,4},{6,7},{7,6},{8,9},{9,8},{10,11... | collective-permute-start | bytes 1572872 | tf_op jit(solution)/shard_map/ppermute | solution.py:869
  20.7 17.5 %all-to-all-start = ((f32[32,8,256]{2,1,0:T(8,128)}), f32[32,8,256]{2,1,0:T(8,128)S(1)}, u32[]{:S(2)}, u32[]{:S(2)}) async-start(f32[32,8,256]{2,1,0:T(8,128)} %bitcast.35), calls=%async_computation | async-start | bytes 524288 | tf_op jit(solution)/shard_map/all_to_all | solution.py:892
  28.1 23.7 %collective-permute-start.2 = (bf16[256,1024]{1,0:T(8,128)(2,1)S(1)}, bf16[256,1024]{1,0:T(8,128)(2,1)}, u32[]{:S(2)}, u32[]{:S(2)}) collective-permute-start(bf16[256,1024]{1,0:T(8,128)(2,1)S(1)} %collective-permute-done.1), channel_id=1, source_target_pairs={{0,1},{1,0},{2,3},{3,2},{4,5},{5,4},{6,7},{7,6},{8,9},{9,8},{10,11... | collective-permute-start | bytes 1572872 | tf_op jit(solution)/shard_map/ppermute | solution.py:869
  38.2 13.7 %all-to-all-start.1 = ((bf16[4,32,2048]{2,1,0:T(8,128)(2,1)}), bf16[4,32,2048]{2,1,0:T(8,128)(2,1)S(1)}, u32[]{:S(2)}, u32[]{:S(2)}) async-start(bf16[4,32,2048]{2,1,0:T(8,128)(2,1)} %pad_maximum_fusion.4), calls=%async_computation.1 | async-start | bytes 1048576 | tf_op jit(solution)/shard_map/all_to_all | solution.py:892
  84.2 30.3 %all-to-all-start.2 = ((bf16[8,256,256]{2,1,0:T(8,128)(2,1)}), bf16[8,256,256]{2,1,0:T(8,128)(2,1)S(1)}, u32[]{:S(2)}, u32[]{:S(2)}) async-start(bf16[8,256,256]{2,1,0:T(8,128)(2,1)} %bitcast.155), calls=%async_computation.2 | async-start | bytes 2097152 | tf_op jit(solution)/shard_map/all_to_all | solution.py:892
  88.3 135.4 %all-gather.6.cloned.1.call-start = ((), (), s32[]{:S(2)}) async-start(), calls=%async_computation.10 | async-start | bytes 7077888 | tf_op jit(solution)/shard_map/all_gather | solution.py:1000
  115.5 24.3 %collective-permute-start.4 = (bf16[2048,256]{1,0:T(8,128)(2,1)S(1)}, bf16[2048,256]{1,0:T(8,128)(2,1)S(1)}, u32[]{:S(2)}, u32[]{:S(2)}) collective-permute-start(bf16[2048,256]{1,0:T(8,128)(2,1)S(1)} %bitcast.160), channel_id=1, source_target_pairs={{0,2},{1,3},{2,0},{3,1},{4,6},{5,7},{6,4},{7,5},{8,10},{9,11},{10,... | collective-permute-start | bytes 3145736 | tf_op jit(solution)/shard_map/ppermute | solution.py:869
  116.5 23.3 %collective-permute-start.3 = (bf16[2048,256]{1,0:T(8,128)(2,1)S(1)}, bf16[2048,256]{1,0:T(8,128)(2,1)}, u32[]{:S(2)}, u32[]{:S(2)}) collective-permute-start(bf16[2048,256]{1,0:T(8,128)(2,1)S(1)} %bitcast.161), channel_id=1, source_target_pairs={{0,1},{1,0},{2,3},{3,2},{4,5},{5,4},{6,7},{7,6},{8,9},{9,8},{10,11... | collective-permute-start | bytes 3145736 | tf_op jit(solution)/shard_map/ppermute | solution.py:869
  194.0 14.7 %collective-permute-start.8 = (bf16[8,272,128]{2,1,0:T(8,128)(2,1)S(1)}, bf16[8,272,128]{2,1,0:T(8,128)(2,1)S(1)}, u32[]{:S(2)}, u32[]{:S(2)}) collective-permute-start(bf16[8,272,128]{2,1,0:T(8,128)(2,1)S(1)} %merge_pair.1), channel_id=1, source_target_pairs={{0,2},{1,3},{2,0},{3,1},{4,6},{5,7},{6,4},{7,5},{8,10},{9,11},{10,... | collective-permute-start | bytes 1671176 | tf_op jit(solution)/shard_map/ppermute | solution.py:869
  213.5 18.6 %all-to-all-start.3 = ((bf16[8,256,128]{2,1,0:T(8,128)(2,1)}), bf16[8,256,128]{2,1,0:T(8,128)(2,1)S(1)}, u32[]{:S(2)}, u32[]{:S(2)}) async-start(bf16[8,256,128]{2,1,0:T(8,128)(2,1)} %get-tuple-element.51), calls=%async_computation.3 | async-start | bytes 1048576 | tf_op jit(solution)/shard_map/all_to_all | solution.py:892
  218.0 233.2 %all-gather.8.cloned.1.call-start = ((), (), s32[]{:S(2)}) async-start(), calls=%async_computation.11 | async-start | bytes 4718592 | tf_op jit(solution)/shard_map/all_gather | solution.py:1015
  271.2 14.0 %collective-permute-start.17 = (bf16[256,1024]{1,0:T(8,128)(2,1)S(1)}, bf16[256,1024]{1,0:T(8,128)(2,1)S(1)}, u32[]{:S(2)}, u32[]{:S(2)}) collective-permute-start(bf16[256,1024]{1,0:T(8,128)(2,1)S(1)} %fusion.25), channel_id=1, source_target_pairs={{0,2},{1,3},{2,0},{3,1},{4,6},{5,7},{6,4},{7,5},{8,10},{9,11},{10,... | collective-permute-start | bytes 1572872 | tf_op jit(solution)/shard_map/ppermute | solution.py:869
  292.0 17.4 %collective-permute-start.18 = (bf16[1024,256]{0,1:T(8,128)(2,1)}, bf16[1024,256]{0,1:T(8,128)(2,1)}, u32[]{:S(2)}, u32[]{:S(2)}) collective-permute-start(bf16[1024,256]{0,1:T(8,128)(2,1)} %get-tuple-element.180), channel_id=1, source_target_pairs={{0,1},{1,0},{2,3},{3,2},{4,5},{5,4},{6,7},{7,6},{8,9},{9,8},{10,11... | collective-permute-start | bytes 1572872 | tf_op jit(solution)/shard_map/ppermute | solution.py:869
  297.3 30.2 %all-to-all-start.4 = ((bf16[8,272,128]{2,1,0:T(8,128)(2,1)}), bf16[8,272,128]{2,1,0:T(8,128)(2,1)S(1)}, u32[]{:S(2)}, u32[]{:S(2)}) async-start(bf16[8,272,128]{2,1,0:T(8,128)(2,1)} %pad_maximum_fusion.3), calls=%async_computation.4 | async-start | bytes 1114112 | tf_op jit(solution)/shard_map/all_to_all | solution.py:892
  302.2 200.6 %reduce-scatter.4.cloned.1.call-start = ((), (), s32[]{:S(2)}) async-start(), calls=%async_computation.12 | async-start | bytes 5308416 | tf_op jit(solution)/shard_map/reduce_scatter | solution.py:1058
  328.6 23.3 %collective-permute-start.21 = (bf16[8,272,128]{2,1,0:T(8,128)(2,1)S(1)}, bf16[8,272,128]{2,1,0:T(8,128)(2,1)S(1)}, u32[]{:S(2)}, u32[]{:S(2)}) collective-permute-start(bf16[8,272,128]{2,1,0:T(8,128)(2,1)S(1)} %all-to-all-done.4.g_0), channel_id=1, source_target_pairs={{0,1},{1,0},{2,3},{3,2},{4,5},{5,4},{6,7},{7,6},{8,9},{9,8},{10,11... | collective-permute-start | bytes 1671176 | tf_op jit(solution)/shard_map/ppermute | solution.py:869
  405.0 25.4 %collective-permute-start.29 = (bf16[2048,256]{1,0:T(8,128)(2,1)S(1)}, bf16[2048,256]{1,0:T(8,128)(2,1)}, u32[]{:S(2)}, u32[]{:S(2)}) collective-permute-start(bf16[2048,256]{1,0:T(8,128)(2,1)S(1)} %add_convert_fusion.1), channel_id=1, source_target_pairs={{0,2},{1,3},{2,0},{3,1},{4,6},{5,7},{6,4},{7,5},{8,10},{9,11},{10,... | collective-permute-start | bytes 3145736 | tf_op jit(solution)/shard_map/ppermute | solution.py:869
  433.7 33.4 %all-to-all-start.5 = ((bf16[8,256,256]{1,2,0:T(8,128)(2,1)}), bf16[8,256,256]{1,2,0:T(8,128)(2,1)S(1)}, u32[]{:S(2)}, u32[]{:S(2)}) async-start(bf16[8,256,256]{1,2,0:T(8,128)(2,1)} %copy.128), calls=%async_computation.5 | async-start | bytes 2097152 | tf_op jit(solution)/shard_map/all_to_all | solution.py:892
  450.6 20.2 %collective-permute-start.13 = (bf16[256,1024]{1,0:T(8,128)(2,1)}, bf16[256,1024]{1,0:T(8,128)(2,1)}, u32[]{:S(2)}, u32[]{:S(2)}) collective-permute-start(bf16[256,1024]{1,0:T(8,128)(2,1)} %get-tuple-element.185), channel_id=1, source_target_pairs={{0,1},{1,0},{2,3},{3,2},{4,5},{5,4},{6,7},{7,6},{8,9},{9,8},{10,11... | collective-permute-start | bytes 1572872 | tf_op jit(solution)/shard_map/ppermute | solution.py:869
  450.6 43.7 %collective-permute-start.12 = (bf16[256,1024]{1,0:T(8,128)(2,1)}, bf16[256,1024]{1,0:T(8,128)(2,1)}, u32[]{:S(2)}, u32[]{:S(2)}) collective-permute-start(bf16[256,1024]{1,0:T(8,128)(2,1)} %get-tuple-element.184), channel_id=1, source_target_pairs={{0,1},{1,0},{2,3},{3,2},{4,5},{5,4},{6,7},{7,6},{8,9},{9,8},{10,11... | collective-permute-start | bytes 1572872 | tf_op jit(solution)/shard_map/ppermute | solution.py:869
  467.0 19.3 %all-to-all-start.6 = ((bf16[32,32,256]{2,1,0:T(8,128)(2,1)}), bf16[32,32,256]{2,1,0:T(8,128)(2,1)}, u32[]{:S(2)}, u32[]{:S(2)}) async-start(bf16[32,32,256]{2,1,0:T(8,128)(2,1)} %bitcast.177), calls=%async_computation.6 | async-start | bytes 1048576 | tf_op jit(solution)/shard_map/all_to_all | solution.py:892
  473.1 21.2 %collective-permute-start.14 = (bf16[256,1024]{1,0:T(8,128)(2,1)}, bf16[256,1024]{1,0:T(8,128)(2,1)}, u32[]{:S(2)}, u32[]{:S(2)}) collective-permute-start(bf16[256,1024]{1,0:T(8,128)(2,1)} %fusion.27), channel_id=1, source_target_pairs={{0,2},{1,3},{2,0},{3,1},{4,6},{5,7},{6,4},{7,5},{8,10},{9,11},{10,... | collective-permute-start | bytes 1572872 | tf_op jit(solution)/shard_map/ppermute | solution.py:869
  (57 other events, 801.2 us)
Sparse Core Ops, SparseCore 0:
  11.5 68.2 all-gather.3
  115.6 97.6 all-gather.5
  247.8 82.9 all-gather.7
  346.8 98.2 reduce-scatter.3

commit v5 on v4

--- a/solution.py
+++ b/solution.py
@@ -5,6 +5,7 @@
 import jax.numpy as jnp
 from jax import lax
 from jax.experimental import pallas as pl
+from jax.experimental.layout import Layout, with_layout_constraint
 from jax.experimental.pallas import tpu as pltpu
 from jax.sharding import PartitionSpec as P
 
@@ -421,6 +422,8 @@
 
 
 CAP_ROWS = 16
+FORWARD_BATCH = 4
+BACKWARD_BATCH = 2
 PARTS = 8
 
 
@@ -446,15 +449,17 @@
     return jnp.where(ids == slot_col, 1.0, 0.0).astype(BF)
 
 
-def key_factor(keys):
+def keep_columns(factors, ids, start, keys, cols):
+    rows = keys.shape[0]
     wide = keys.astype(F32)
-    return lax.rsqrt(jnp.sum(wide * wide, axis=1, keepdims=True)) * SCALE
-
-
-def keep_columns(factors, ids, start, keys, id_column):
-    shape = keys.shape
-    factors[pl.ds(start, shape[0]), :] = jnp.broadcast_to(key_factor(keys), shape)
-    ids[pl.ds(start, shape[0]), :] = jnp.broadcast_to(id_column, shape)
+    square = wide * wide
+    high = square.astype(BF)
+    low = (square - high.astype(F32)).astype(BF)
+    ones = jnp.ones((HEAD_DIM, HEAD_DIM), BF)
+    total = dot_nn(high, ones) + dot_nn(low, ones)
+    factors[pl.ds(start, rows), :] = lax.rsqrt(total) * SCALE
+    pick = lax.broadcasted_iota(jnp.int32, (PARTS, HEAD_DIM), 0) >= 6
+    ids[pl.ds(start, rows), :] = dot_nn(cols.astype(BF), jnp.where(pick, 1.0, 0.0).astype(BF))
 
 
 def pair_scores(raw, factor, key_ids, query_ids, query_starts):
@@ -523,7 +528,7 @@
         part = dot_nn(hot, lanes[block].reshape(slots, width)).astype(BF)
         start = pl.multiple_of(SPAN + block * tokens, SPAN)
         kept_rows[pl.ds(start, tokens), :] = part
-        keep_columns(factors, ids, start, part[:, :HEAD_DIM], cols[:, 0:1])
+        keep_columns(factors, ids, start, part[:, :HEAD_DIM], cols)
         return carry
 
     lax.fori_loop(0, blocks, place_rows, 0, unroll=4)
@@ -531,17 +536,17 @@
         held[0:SPAN, :] = held[blocks * tokens : blocks * tokens + SPAN, :]
     heads_out[:, :, HEAD_DIM:] = jnp.zeros((blocks, tokens, width - HEAD_DIM), BF)
 
-    def attend(block, carry):
+    def attend(step, carry):
+        todo = [(step * FORWARD_BATCH + at // pairs, at % pairs) for at in range(FORWARD_BATCH * pairs)]
         first = []
-        for pair in range(pairs):
+        for block, pair in todo:
             start = pl.multiple_of(block * tokens + pair * 2 * SPAN, SPAN)
             rows = kept_rows[pl.ds(start, 3 * SPAN), :]
             raw = dot_nt(rows[:, :HEAD_DIM], rows[SPAN:, :HEAD_DIM])
             first.append((start, rows[:, HEAD_DIM:], raw))
         second = []
         lse = []
-        for pair in range(pairs):
-            start, values, raw = first[pair]
+        for (block, pair), (start, values, raw) in zip(todo, first):
             here = slice(pair * 2 * SPAN, (pair + 1) * 2 * SPAN)
             scores, _ = pair_scores(
                 raw,
@@ -558,16 +563,22 @@
             scale = 1.0 / total
             second.append(jnp.concatenate([weight * scale for weight in weights]).astype(BF))
             lse.append(top + jnp.log(total))
-        for pair in range(pairs):
+        for (block, pair), (start, values, raw), probs in zip(todo, first, second):
             here = slice(pair * 2 * SPAN, (pair + 1) * 2 * SPAN)
-            heads_out[block, here, :HEAD_DIM] = dot_tn(second[pair], first[pair][1]).astype(BF)
-        high, mid, low = three_parts(jnp.concatenate(lse, axis=1))
+            heads_out[block, here, :HEAD_DIM] = dot_tn(probs, values).astype(BF)
         row = lax.broadcasted_iota(jnp.int32, (PARTS, tokens), 0)
-        flat = jnp.where(row == 0, high, jnp.where(row == 1, mid, jnp.where(row == 2, low, 0.0)))
-        heads_out[block, :, HEAD_DIM : HEAD_DIM + PARTS] = jnp.transpose(flat).astype(BF)
+        for at in range(FORWARD_BATCH):
+            block = step * FORWARD_BATCH + at
+            high, mid, low = three_parts(
+                jnp.concatenate(lse[at * pairs : (at + 1) * pairs], axis=1)
+            )
+            flat = jnp.where(
+                row == 0, high, jnp.where(row == 1, mid, jnp.where(row == 2, low, 0.0))
+            )
+            heads_out[block, :, HEAD_DIM : HEAD_DIM + PARTS] = jnp.transpose(flat).astype(BF)
         return carry
 
-    lax.fori_loop(0, blocks, attend, 0)
+    lax.fori_loop(0, blocks // FORWARD_BATCH, attend, 0)
 
     def unplace(block, carry):
         hot = hot_rows(info[block, 2:3, :], slots)
@@ -710,16 +721,17 @@
         )
         start = pl.multiple_of(SPAN + block * tokens, SPAN)
         keys = kept_rows[pl.ds(start, tokens), :HEAD_DIM]
-        keep_columns(factors, ids, start, keys, cols[:, 0:1])
+        keep_columns(factors, ids, start, keys, cols)
         return carry
 
     lax.fori_loop(0, blocks, place_rows, 0, unroll=4)
     for held in (factors, ids):
         held[0:SPAN, :] = held[blocks * tokens : blocks * tokens + SPAN, :]
 
-    def attend(block, carry):
+    def attend(step, carry):
+        todo = [(step * BACKWARD_BATCH + at // pairs, at % pairs) for at in range(BACKWARD_BATCH * pairs)]
         first = []
-        for pair in range(pairs):
+        for block, pair in todo:
             start = pl.multiple_of(block * tokens + pair * 2 * SPAN, SPAN)
             here = slice(pair * 2 * SPAN, (pair + 1) * 2 * SPAN)
             rows = kept_rows[pl.ds(start, 3 * SPAN), :]
@@ -730,8 +742,7 @@
             back = dot_nt(rows[:, HEAD_DIM:], grads)
             first.append((start, keys, queries, grads, raw, back))
         second = []
-        for pair in range(pairs):
-            start, keys, queries, grads, raw, back = first[pair]
+        for (block, pair), (start, keys, queries, grads, raw, back) in zip(todo, first):
             here = slice(pair * 2 * SPAN, (pair + 1) * 2 * SPAN)
             factor = factors[pl.ds(start, 3 * SPAN), :]
             scores, masks = pair_scores(
@@ -756,9 +767,9 @@
             slope = jnp.sum(grad_score * raw, axis=1, keepdims=True)
             drift = slope * (factor * factor * factor * HEAD_DIM) * keys.astype(F32)
             second.append(((grad_score * factor).astype(BF), weights_all, drift))
-        for pair in range(pairs):
-            start, keys, queries, grads = first[pair][:4]
-            grad_raw, weights_all, drift = second[pair]
+        for (start, keys, queries, grads, _, _), (grad_raw, weights_all, drift) in zip(
+            first, second
+        ):
             grad_val = dot_nn(weights_all, grads)
             grad_key = dot_nn(grad_raw, queries) - drift
             grad_query = dot_tn(grad_raw, keys)
@@ -771,7 +782,7 @@
             )
         return carry
 
-    lax.fori_loop(0, blocks, attend, 0)
+    lax.fori_loop(0, blocks // BACKWARD_BATCH, attend, 0)
     sums[blocks * tokens : blocks * tokens + SPAN, :] += sums[0:SPAN, :]
 
     def unplace(block, carry):
@@ -886,6 +897,10 @@
     near = parts[0] + swap(parts[1].astype(BF), 1).astype(F32)
     far = parts[2] + swap(parts[3].astype(BF), 1).astype(F32)
     return near + swap(far.astype(BF), 2).astype(F32)
+
+
+def row_major(x):
+    return with_layout_constraint(x.astype(BF), Layout(major_to_minor=(0, 1)))
 
 
 def exchange(x, groups=None):
@@ -959,7 +974,8 @@
                 slots_sent(inverse[turn], tokens, capacity),
             ]
         ).astype(F32)
-        per_round.append(jnp.concatenate([rows, vectors, jnp.zeros((2, tokens), F32)]))
+        split = jnp.stack([ids // SPAN * SPAN, ids % SPAN]).astype(F32)
+        per_round.append(jnp.concatenate([rows, vectors, split]))
     info = jnp.tile(jnp.stack(per_round), (HEADS, 1, 1))
     info = exchange(info)
     got = info[:, 4:6].reshape(devices, 2 * tokens)
@@ -1011,7 +1027,9 @@
     mixed, total_lse = merge_final(sent[0], swap(sent[1], 1), swap(far, 2))
     mixed = exchange(mixed, columns())
     grad_hidden = outer_cols(grad_f_all, m_down)
-    mixed, normed_one, grad_hidden = lax.optimization_barrier((mixed, normed_one, grad_hidden))
+    mixed, normed_one, grad_hidden, total_lse = lax.optimization_barrier(
+        (mixed, normed_one, grad_hidden, gather_group(total_lse))
+    )
     normed_col = lax.all_gather(
         normed_one, "seq", axis=0, tiled=True, axis_index_groups=columns()
     )
@@ -1053,32 +1071,46 @@
             for near in range(ROUNDS)
         ]
     )
-    merged = jnp.concatenate([x.astype(BF) for x in (grad_up, grad_out, grad_down)], axis=1)
+    merged = jnp.concatenate([row_major(x) for x in (grad_up, grad_out, grad_down)], axis=1)
     grad_mixed, merged = lax.optimization_barrier((grad_mixed, merged))
+    grad_mixed = list(gather_group(grad_mixed))
+    merged, normed_col, grad_mixed[1] = lax.optimization_barrier(
+        (merged, normed_col, grad_mixed[1])
+    )
     merged = lax.psum_scatter(
         merged, "seq", scatter_dimension=0, tiled=True, axis_index_groups=columns()
     )
     s_down = merged[:, half + fourth :].astype(F32)
     merged = merged[:, : half + fourth].reshape(ROUNDS, shard, -1)
-    s_up = jnp.zeros((shard, HEADS, ROUNDS, wide), F32)
-    s_out = jnp.zeros((shard, features), F32)
-    for near in range(ROUNDS):
-        peer = (place % ROUNDS) ^ near
-        piece = lax.dynamic_index_in_dim(merged, peer, axis=0, keepdims=False)
-        piece = (swap(piece, near) if near else piece).astype(F32)
-        s_up = lax.dynamic_update_slice(
-            s_up, piece[:, :half].reshape(shard, HEADS, 1, wide), (0, 0, peer, 0)
-        )
-        s_out = lax.dynamic_update_slice(s_out, piece[:, half:], (0, peer * fourth))
-    s_up = s_up.reshape(shard, ROUNDS * half)
+    pieces = [
+        lax.dynamic_index_in_dim(merged, (place % ROUNDS) ^ near, axis=0, keepdims=False)
+        for near in range(ROUNDS)
+    ]
+    pieces = [swap(piece, near) if near else piece for near, piece in enumerate(pieces)]
+
+    def in_order(first, last):
+        mine = place % ROUNDS
+        found = []
+        for peer in range(ROUNDS):
+            options = [pieces[peer ^ at][:, first:last] for at in range(ROUNDS)]
+            low = jnp.where(mine == 0, options[0], options[1])
+            high = jnp.where(mine == 2, options[2], options[3])
+            found.append(jnp.where(mine < 2, low, high))
+        return jnp.stack(found, axis=1).astype(F32)
+
+    s_up = in_order(0, half).reshape(shard, ROUNDS, HEADS, wide)
+    s_up = jnp.transpose(s_up, (0, 2, 1, 3)).reshape(shard, ROUNDS * half)
+    s_out = in_order(half, half + fourth).reshape(shard, features)
 
     grad_head = run_backward(
-        turn, gather_group(grad_mixed), gather_group(total_lse), kept_rows, info
+        turn, grad_mixed, total_lse, kept_rows, info
     )
     grad_head = sum_group([x.astype(F32) for x in grad_head]).astype(BF)
     grad_rows = exchange(grad_head.reshape(HEADS, tokens, 2 * HEAD_DIM), columns())
     s_pair = inner_rows(normed_col, grad_head).astype(BF).reshape(devices, shard, 2 * HEAD_DIM)
-    grad_rows, s_pair = lax.optimization_barrier((grad_rows, s_pair))
+    grad_rows, s_pair, s_up, s_out, s_down = lax.optimization_barrier(
+        (grad_rows, s_pair, s_up, s_out, s_down)
+    )
     grad_rows = jnp.transpose(grad_rows, (1, 0, 2)).reshape(tokens, 2 * features)
     s_pair = exchange(s_pair)
     s_pair = jnp.sum(

time: 538 us -> 493 us (0.916)
  local copies, waits for them, and re-layouts: 56.4 us -> 34.1 us
  Pallas kernels: 99.8 us -> 81.2 us
  other arithmetic: 32.8 us -> 39 us
  matrix products: 60.6 us -> 55.2 us
    pallas_call x4, Pallas kernels: 99.8 us -> 81.2 us  [run_kernel(): pl.pallas_call(kernel, out_shape=tuple((jax.ShapeDtypeStruct(shape, BF) f...]
    dynamic_update_slice x8 -> x0, local copies, waits for them, and re-layouts: 10.8 us -> none  [the longest x4 10.7 us: shards_fast(): lax.dynamic_update_slice(s_up, piece[:, :half].reshape(shard, HEADS, 1, w...]
    unnamed x90 -> x93, local copies, waits for them, and re-layouts: 22.8 us -> 12 us
    dot_general x4, matrix products: 23.7 us -> 17.8 us  [linear(): return jnp.dot(matrix_a, matrix_b, preferred_element_type=jnp.float32)]
    ppermute x33, waiting for transfers between devices: 107 us -> 101 us  [swap(): return lax.ppermute(x, 'seq', peers(mask))]
  transfers between devices with their start and end apart: 45 -> 45, of which waited for: 24 -> 28; matrix products, arithmetic and copies ran while one was open for 23% -> 23% of each run, Pallas kernels for 19% -> 17%
where the time goes in v5:
time: 493 us; the launch traced here: 487 us
  waiting for transfers between devices  208 us (42%)
  Pallas kernels  81.2 us (16%)
  matrix products  55.2 us (11%)
  starting transfers between devices  54.7 us (11%)
  other arithmetic  39 us (8%)
  local copies, waits for them, and re-layouts  34.1 us (7%)
  between operations  15.1 us (3%)
    ppermute x33, waiting for transfers between devices, swap(): return lax.ppermute(x, 'seq', peers(mask))  101 us
    pallas_call x4, Pallas kernels, run_kernel(): pl.pallas_call(kernel, out_shape=tuple((jax.ShapeDtypeStruct(shape, BF) f...  81.2 us
    all_to_all x8, waiting for transfers between devices, exchange(): lax.all_to_all(x, 'seq', split_axis=0, concat_axis=0, tiled=True, axis_in...  73.4 us
    all_to_all x8, starting transfers between devices, exchange(): lax.all_to_all(x, 'seq', split_axis=0, concat_axis=0, tiled=True, axis_in...  33.6 us
    all_gather x1, waiting for transfers between devices, shards_fast(): m_pair = lax.all_gather(pair.astype(BF), 'seq', axis=0, tiled=True)  27.9 us
    dot_general x4, matrix products, outer_cols(): lax.dot_general(matrix_a, matrix_b, (((1,), (1,)), ((), ())), preferred_e...  20.5 us
    ppermute x33, starting transfers between devices, swap(): return lax.ppermute(x, 'seq', peers(mask))  20.4 us
    dot_general x4, matrix products, linear(): return jnp.dot(matrix_a, matrix_b, preferred_element_type=jnp.float32)  17.8 us
  transfers between devices with their start and end apart: 45, of which 28 were waited for; matrix products, arithmetic and copies ran while one was open for 23% of the time, Pallas kernels for 17%

profile of v5, /device:TPU:0, one launch (start us, length us, event | category | flops | bytes accessed | tf_op | source)
XLA Modules:
  0.0 487.4 jit_solution(1844585302109005690)
XLA Ops:
  21.4 5.0 %all-to-all-start = ((f32[32,8,256]{2,1,0:T(8,128)}), f32[32,8,256]{2,1,0:T(8,128)S(1)}, u32[]{:S(2)}, u32[]{:S(2)}) async-start(f32[32,8,256]{2,1,0:T(8,128)} %bitcast.35), calls=%async_computation | async-start | bytes 524288 | tf_op jit(solution)/shard_map/all_to_all | solution.py:907
  29.0 9.7 %all-to-all-done.info = f32[32,8,256]{2,1,0:T(8,128)S(1)} async-done(((f32[32,8,256]{2,1,0:T(8,128)}), f32[32,8,256]{2,1,0:T(8,128)S(1)}, u32[]{:S(2)}, u32[]{:S(2)}) %all-to-all-start) | async-done | bytes 262176 | tf_op jit(solution)/shard_map/all_to_all | solution.py:907
  44.0 8.2 %all-to-all-done.1 = bf16[4,32,2048]{2,1,0:T(8,128)(2,1)S(1)} async-done(((bf16[4,32,2048]{2,1,0:T(8,128)(2,1)}), bf16[4,32,2048]{2,1,0:T(8,128)(2,1)S(1)}, u32[]{:S(2)}, u32[]{:S(2)}) %all-to-all-start.1) | async-done | bytes 524320 | tf_op jit(solution)/shard_map/all_to_all | solution.py:907
  52.2 27.9 %all-gather.4.cloned.1.call-done = bf16[1024,2048]{1,0:T(8,128)(2,1)} async-done(((bf16[32,2048]{1,0:T(8,128)(2,1)}), bf16[1024,2048]{1,0:T(8,128)(2,1)}) %all-gather.4.cloned.1.call-update) | async-done | bytes 4194320 | tf_op jit(solution)/shard_map/all_gather | solution.py:994
  89.2 25.6 %all-to-all-done.2 = bf16[8,256,256]{2,1,0:T(8,128)(2,1)S(1)} async-done(((bf16[8,256,256]{2,1,0:T(8,128)(2,1)}), bf16[8,256,256]{2,1,0:T(8,128)(2,1)S(1)}, u32[]{:S(2)}, u32[]{:S(2)}) %all-to-all-start.2) | async-done | bytes 1048608 | tf_op jit(solution)/shard_map/all_to_all | solution.py:907
  116.8 23.3 %collective-permute-done.4.x_2 = bf16[2048,256]{1,0:T(8,128)(2,1)S(1)} collective-permute-done((bf16[2048,256]{1,0:T(8,128)(2,1)S(1)}, bf16[2048,256]{1,0:T(8,128)(2,1)S(1)}, u32[]{:S(2)}, u32[]{:S(2)}) %collective-permute-start.4) | collective-permute-done | bytes 1048608 | tf_op jit(solution)/shard_map/ppermute | solution.py:880
  143.7 35.6 %hash_forward.1 = (bf16[8,272,128]{2,1,0:T(8,128)(2,1)S(1)}, bf16[8,272,128]{2,1,0:T(8,128)(2,1)S(1)}, bf16[8,272,128]{2,1,0:T(8,128)(2,1)S(1)}, bf16[8,272,128]{2,1,0:T(8,128)(2,1)S(1)}, bf16[8256,256]{1,0:T(8,128)(2,1)}) custom-call(s32[1]{0:T(128)} %bitcast.place, bf16[2048,256]{1,0:T(8,128)(2,1)S(1)} %bitcast.165, ...), custom_call_target="tpu_custom_call" | custom-call | flops 20000000000 | bytes 12000000 | tf_op jit(solution)/shard_map/hash_forward/pallas_call | solution.py:817
  190.9 8.8 %collective-permute-done.8.c = bf16[8,272,128]{2,1,0:T(8,128)(2,1)S(1)} collective-permute-done((bf16[8,272,128]{2,1,0:T(8,128)(2,1)S(1)}, bf16[8,272,128]{2,1,0:T(8,128)(2,1)S(1)}, u32[]{:S(2)}, u32[]{:S(2)}) %collective-permute-start.8) | collective-permute-done | bytes 557088 | tf_op jit(solution)/shard_map/ppermute | solution.py:880
  199.7 4.8 merge_final.1
  216.8 6.7 %fusion.17 = f32[1024,1024]{1,0:T(8,128)} fusion(bf16[1024,1024]{1,0:T(8,128)(2,1)} %constant_dynamic-update-slice_fusion, bf16[1024,3072]{1,0:T(8,128)(2,1)} %all-gather.6.cloned.1.call-done), kind=kOutput, calls=%fused_computation.28 | convolution fusion | flops 2147483648 | bytes 8388608 | tf_op jit(solution)/shard_map/dot_general | solution.py:59
  229.1 12.1 %collective-permute-done.13 = bf16[256,1024]{1,0:T(8,128)(2,1)S(1)} collective-permute-done((bf16[256,1024]{1,0:T(8,128)(2,1)S(1)}, bf16[256,1024]{1,0:T(8,128)(2,1)S(1)}, u32[]{:S(2)}, u32[]{:S(2)}) %collective-permute-start.13) | collective-permute-done | bytes 524320 | tf_op jit(solution)/shard_map/ppermute | solution.py:880
  251.7 6.8 %fusion.75 = (bf16[1024,1024]{1,0:T(8,128)(2,1)S(1)}, f32[1024,1024]{1,0:T(8,128)}) fusion(bf16[1024,1024]{1,0:T(8,128)(2,1)S(1)} %get-tuple-element.108, bf16[1024,3072]{1,0:T(8,128)(2,1)} %all-gather.6.cloned.1.call-done), kind=kOutput, calls=%fused_computation.267 | convolution fusion | flops 2148532224 | bytes 10485760 | tf_op jit(solution)/shard_map/dot_general | solution.py:59
  263.8 7.2 %convolution_convert_fusion.1 = bf16[1024,1024]{1,0:T(8,128)(2,1)} fusion(bf16[1024,1024]{1,0:T(8,128)(2,1)} %constant_dynamic-update-slice_fusion, f32[1024,1024]{1,0:T(8,128)} %copy-done.8, f32[1024]{0:T(1024)S(1)} %bitcast.209), kind=kOutput, calls=%fused_computation.16 | convolution fusion | flops 2159017984 | bytes 8392704 | tf_op jit(solution)/shard_map/dot_general | solution.py:53
  271.0 5.3 %collective-permute-done.20 = bf16[256,1024]{1,0:T(8,128)(2,1)S(1)} collective-permute-done((bf16[256,1024]{1,0:T(8,128)(2,1)S(1)}, bf16[256,1024]{1,0:T(8,128)(2,1)S(1)}, u32[]{:S(2)}, u32[]{:S(2)}) %collective-permute-start.20) | collective-permute-done | bytes 524320 | tf_op jit(solution)/shard_map/ppermute | solution.py:880
  288.4 5.9 %all-to-all-start.4 = ((bf16[8,272,128]{2,1,0:T(8,128)(2,1)}), bf16[8,272,128]{2,1,0:T(8,128)(2,1)S(1)}, u32[]{:S(2)}, u32[]{:S(2)}) async-start(bf16[8,272,128]{2,1,0:T(8,128)(2,1)} %pad_maximum_fusion.3), calls=%async_computation.4 | async-start | bytes 1114112 | tf_op jit(solution)/shard_map/all_to_all | solution.py:907
  301.7 7.9 %collective-permute-done.23 = bf16[1024,256]{1,0:T(8,128)(2,1)S(1)} collective-permute-done((bf16[1024,256]{1,0:T(8,128)(2,1)S(1)}, bf16[1024,256]{1,0:T(8,128)(2,1)S(1)}, u32[]{:S(2)}, u32[]{:S(2)}) %collective-permute-start.23) | collective-permute-done | bytes 524320 | tf_op jit(solution)/shard_map/ppermute | solution.py:880
  313.6 8.0 %all-to-all-done.4.g_0 = bf16[8,272,128]{2,1,0:T(8,128)(2,1)S(1)} async-done(((bf16[8,272,128]{2,1,0:T(8,128)(2,1)}), bf16[8,272,128]{2,1,0:T(8,128)(2,1)S(1)}, u32[]{:S(2)}, u32[]{:S(2)}) %all-to-all-start.4) | async-done | bytes 557088 | tf_op jit(solution)/shard_map/all_to_all | solution.py:907
  326.9 13.1 %collective-permute-done.25.g_2 = bf16[8,272,128]{2,1,0:T(8,128)(2,1)S(1)} collective-permute-done((bf16[8,272,128]{2,1,0:T(8,128)(2,1)S(1)}, bf16[8,272,128]{2,1,0:T(8,128)(2,1)S(1)}, u32[]{:S(2)}, u32[]{:S(2)}) %collective-permute-start.25) | collective-permute-done | bytes 557088 | tf_op jit(solution)/shard_map/ppermute | solution.py:880
  343.5 37.1 %hash_backward.1 = (bf16[2048,256]{1,0:T(8,128)(2,1)S(1)}, bf16[2048,256]{1,0:T(8,128)(2,1)S(1)}, bf16[2048,256]{1,0:T(8,128)(2,1)S(1)}, bf16[2048,256]{1,0:T(8,128)(2,1)}) custom-call(s32[1]{0:T(128)} %bitcast.place, bf16[8,272,128]{2,1,0:T(8,128)(2,1)S(1)} %all-to-all-done.4.g_0, bf16[8,272,128]{2,1,0:T(8,128)(2,1)S(1)} %collective-permute-done.24.g_1, ...), custom_call_target="tpu_custom_call" | custom-call | flops 20000000000 | bytes 12000000 | tf_op jit(solution)/shard_map/hash_backward/pallas_call | solution.py:817
  386.4 7.7 %fusion.76 = (bf16[1024,1024]{1,0:T(8,128)(2,1)S(1)}, f32[1024,1024]{1,0:T(8,128)}) fusion(bf16[1024,3072]{1,0:T(8,128)(2,1)} %all-gather.6.cloned.1.call-done, f32[1024,1024]{1,0:T(8,128)} %copy-done.8, f32[1024]{0:T(1024)} %bitcast.210), kind=kOutput, calls=%fused_computation.268 | convolution fusion | flops 2159017984 | bytes 12587008 | tf_op jit(solution)/shard_map/dot_general | solution.py:49
  395.7 13.5 %collective-permute-done.29 = bf16[2048,256]{1,0:T(8,128)(2,1)} collective-permute-done((bf16[2048,256]{1,0:T(8,128)(2,1)S(1)}, bf16[2048,256]{1,0:T(8,128)(2,1)}, u32[]{:S(2)}, u32[]{:S(2)}) %collective-permute-start.29) | collective-permute-done | bytes 1048608 | tf_op jit(solution)/shard_map/ppermute | solution.py:880
  434.1 11.1 %all-to-all-done.5 = bf16[8,256,256]{1,2,0:T(8,128)(2,1)S(1)} async-done(((bf16[8,256,256]{1,2,0:T(8,128)(2,1)}), bf16[8,256,256]{1,2,0:T(8,128)(2,1)S(1)}, u32[]{:S(2)}, u32[]{:S(2)}) %all-to-all-start.5) | async-done | bytes 1048608 | tf_op jit(solution)/shard_map/all_to_all | solution.py:907
  453.1 4.6 multiply_reduce_fusion.1
  458.0 6.5 %all-to-all-done.6 = bf16[32,32,256]{2,1,0:T(8,128)(2,1)} async-done(((bf16[32,32,256]{2,1,0:T(8,128)(2,1)}), bf16[32,32,256]{2,1,0:T(8,128)(2,1)}, u32[]{:S(2)}, u32[]{:S(2)}) %all-to-all-start.6) | async-done | bytes 524320 | tf_op jit(solution)/shard_map/all_to_all | solution.py:907
  (318 shorter events, 170.0 us)
Async XLA Ops:
  7.2 72.9 %all-gather.4.cloned.1.call-start = ((), (), s32[]{:S(2)}) async-start(), calls=%async_computation.9 | async-start | bytes 4325376 | tf_op jit(solution)/shard_map/all_gather | solution.py:994
  12.3 15.9 %collective-permute-start.1 = (bf16[256,1024]{1,0:T(8,128)(2,1)S(1)}, bf16[256,1024]{1,0:T(8,128)(2,1)S(1)}, u32[]{:S(2)}, u32[]{:S(2)}) collective-permute-start(bf16[256,1024]{1,0:T(8,128)(2,1)S(1)} %get-tuple-element.62), channel_id=1, source_target_pairs={{0,2},{1,3},{2,0},{3,1},{4,6},{5,7},{6,4},{7,5},{8,10},{9,11},{10,... | collective-permute-start | bytes 1572872 | tf_op jit(solution)/shard_map/ppermute | solution.py:880
  15.2 36.9 %collective-permute-start = (bf16[256,1024]{1,0:T(8,128)(2,1)S(1)}, bf16[256,1024]{1,0:T(8,128)(2,1)}, u32[]{:S(2)}, u32[]{:S(2)}) collective-permute-start(bf16[256,1024]{1,0:T(8,128)(2,1)S(1)} %get-tuple-element.62), channel_id=1, source_target_pairs={{0,1},{1,0},{2,3},{3,2},{4,5},{5,4},{6,7},{7,6},{8,9},{9,8},{10,11... | collective-permute-start | bytes 1572872 | tf_op jit(solution)/shard_map/ppermute | solution.py:880
  21.4 17.2 %all-to-all-start = ((f32[32,8,256]{2,1,0:T(8,128)}), f32[32,8,256]{2,1,0:T(8,128)S(1)}, u32[]{:S(2)}, u32[]{:S(2)}) async-start(f32[32,8,256]{2,1,0:T(8,128)} %bitcast.35), calls=%async_computation | async-start | bytes 524288 | tf_op jit(solution)/shard_map/all_to_all | solution.py:907
  28.2 24.0 %collective-permute-start.2 = (bf16[256,1024]{1,0:T(8,128)(2,1)S(1)}, bf16[256,1024]{1,0:T(8,128)(2,1)}, u32[]{:S(2)}, u32[]{:S(2)}) collective-permute-start(bf16[256,1024]{1,0:T(8,128)(2,1)S(1)} %collective-permute-done.1), channel_id=1, source_target_pairs={{0,1},{1,0},{2,3},{3,2},{4,5},{5,4},{6,7},{7,6},{8,9},{9,8},{10,11... | collective-permute-start | bytes 1572872 | tf_op jit(solution)/shard_map/ppermute | solution.py:880
  84.6 30.3 %all-to-all-start.2 = ((bf16[8,256,256]{2,1,0:T(8,128)(2,1)}), bf16[8,256,256]{2,1,0:T(8,128)(2,1)S(1)}, u32[]{:S(2)}, u32[]{:S(2)}) async-start(bf16[8,256,256]{2,1,0:T(8,128)(2,1)} %bitcast.158), calls=%async_computation.2 | async-start | bytes 2097152 | tf_op jit(solution)/shard_map/all_to_all | solution.py:907
  88.6 128.2 %all-gather.6.cloned.1.call-start = ((), (), s32[]{:S(2)}) async-start(), calls=%async_computation.10 | async-start | bytes 7077888 | tf_op jit(solution)/shard_map/all_gather | solution.py:1016
  115.8 24.3 %collective-permute-start.4 = (bf16[2048,256]{1,0:T(8,128)(2,1)S(1)}, bf16[2048,256]{1,0:T(8,128)(2,1)S(1)}, u32[]{:S(2)}, u32[]{:S(2)}) collective-permute-start(bf16[2048,256]{1,0:T(8,128)(2,1)S(1)} %bitcast.163), channel_id=1, source_target_pairs={{0,2},{1,3},{2,0},{3,1},{4,6},{5,7},{6,4},{7,5},{8,10},{9,11},{10,... | collective-permute-start | bytes 3145736 | tf_op jit(solution)/shard_map/ppermute | solution.py:880
  116.8 23.3 %collective-permute-start.3 = (bf16[2048,256]{1,0:T(8,128)(2,1)S(1)}, bf16[2048,256]{1,0:T(8,128)(2,1)}, u32[]{:S(2)}, u32[]{:S(2)}) collective-permute-start(bf16[2048,256]{1,0:T(8,128)(2,1)S(1)} %bitcast.164), channel_id=1, source_target_pairs={{0,1},{1,0},{2,3},{3,2},{4,5},{5,4},{6,7},{7,6},{8,9},{9,8},{10,11... | collective-permute-start | bytes 3145736 | tf_op jit(solution)/shard_map/ppermute | solution.py:880
  185.0 14.7 %collective-permute-start.8 = (bf16[8,272,128]{2,1,0:T(8,128)(2,1)S(1)}, bf16[8,272,128]{2,1,0:T(8,128)(2,1)S(1)}, u32[]{:S(2)}, u32[]{:S(2)}) collective-permute-start(bf16[8,272,128]{2,1,0:T(8,128)(2,1)S(1)} %merge_pair.1), channel_id=1, source_target_pairs={{0,2},{1,3},{2,0},{3,1},{4,6},{5,7},{6,4},{7,5},{8,10},{9,11},{10,... | collective-permute-start | bytes 1671176 | tf_op jit(solution)/shard_map/ppermute | solution.py:880
  204.5 19.7 %all-to-all-start.3 = ((bf16[8,256,128]{2,1,0:T(8,128)(2,1)}), bf16[8,256,128]{2,1,0:T(8,128)(2,1)S(1)}, u32[]{:S(2)}, u32[]{:S(2)}) async-start(bf16[8,256,128]{2,1,0:T(8,128)(2,1)} %get-tuple-element.61), calls=%async_computation.3 | async-start | bytes 1048576 | tf_op jit(solution)/shard_map/all_to_all | solution.py:907
  209.0 116.3 %all-gather.8.cloned.1.call-start = ((), (), s32[]{:S(2)}) async-start(), calls=%async_computation.11 | async-start | bytes 4718592 | tf_op jit(solution)/shard_map/all_gather | solution.py:1033
  262.3 14.0 %collective-permute-start.20 = (bf16[256,1024]{1,0:T(8,128)(2,1)S(1)}, bf16[256,1024]{1,0:T(8,128)(2,1)S(1)}, u32[]{:S(2)}, u32[]{:S(2)}) collective-permute-start(bf16[256,1024]{1,0:T(8,128)(2,1)S(1)} %fusion.25), channel_id=1, source_target_pairs={{0,2},{1,3},{2,0},{3,1},{4,6},{5,7},{6,4},{7,5},{8,10},{9,11},{10,... | collective-permute-start | bytes 1572872 | tf_op jit(solution)/shard_map/ppermute | solution.py:880
  283.2 18.5 %collective-permute-start.21 = (bf16[1024,256]{1,0:T(8,128)(2,1)}, bf16[1024,256]{1,0:T(8,128)(2,1)}, u32[]{:S(2)}, u32[]{:S(2)}) collective-permute-start(bf16[1024,256]{1,0:T(8,128)(2,1)} %get-tuple-element.118), channel_id=1, source_target_pairs={{0,1},{1,0},{2,3},{3,2},{4,5},{5,4},{6,7},{7,6},{8,9},{9,8},{10,11... | collective-permute-start | bytes 1572872 | tf_op jit(solution)/shard_map/ppermute | solution.py:880
  288.4 33.2 %all-to-all-start.4 = ((bf16[8,272,128]{2,1,0:T(8,128)(2,1)}), bf16[8,272,128]{2,1,0:T(8,128)(2,1)S(1)}, u32[]{:S(2)}, u32[]{:S(2)}) async-start(bf16[8,272,128]{2,1,0:T(8,128)(2,1)} %pad_maximum_fusion.3), calls=%async_computation.4 | async-start | bytes 1114112 | tf_op jit(solution)/shard_map/all_to_all | solution.py:907
  294.4 130.0 %reduce-scatter.2.cloned.1.call-start = ((), (), s32[]{:S(2)}) async-start(), calls=%async_computation.12 | async-start | bytes 5308416 | tf_op jit(solution)/shard_map/reduce_scatter | solution.py:1080
  325.4 14.7 %collective-permute-start.25 = (bf16[8,272,128]{2,1,0:T(8,128)(2,1)S(1)}, bf16[8,272,128]{2,1,0:T(8,128)(2,1)S(1)}, u32[]{:S(2)}, u32[]{:S(2)}) collective-permute-start(bf16[8,272,128]{2,1,0:T(8,128)(2,1)S(1)} %all-to-all-done.4.g_0), channel_id=1, source_target_pairs={{0,2},{1,3},{2,0},{3,1},{4,6},{5,7},{6,4},{7,5},{8,10},{9,11},{10,... | collective-permute-start | bytes 1671176 | tf_op jit(solution)/shard_map/ppermute | solution.py:880
  380.7 15.0 %collective-permute-start.27 = (bf16[2048,256]{1,0:T(8,128)(2,1)S(1)}, bf16[2048,256]{1,0:T(8,128)(2,1)}, u32[]{:S(2)}, u32[]{:S(2)}) collective-permute-start(bf16[2048,256]{1,0:T(8,128)(2,1)S(1)} %get-tuple-element.80), channel_id=1, source_target_pairs={{0,1},{1,0},{2,3},{3,2},{4,5},{5,4},{6,7},{7,6},{8,9},{9,8},{10,11... | collective-permute-start | bytes 3145736 | tf_op jit(solution)/shard_map/ppermute | solution.py:880
  383.8 25.4 %collective-permute-start.29 = (bf16[2048,256]{1,0:T(8,128)(2,1)S(1)}, bf16[2048,256]{1,0:T(8,128)(2,1)}, u32[]{:S(2)}, u32[]{:S(2)}) collective-permute-start(bf16[2048,256]{1,0:T(8,128)(2,1)S(1)} %add_convert_fusion.1), channel_id=1, source_target_pairs={{0,2},{1,3},{2,0},{3,1},{4,6},{5,7},{6,4},{7,5},{8,10},{9,11},{10,... | collective-permute-start | bytes 3145736 | tf_op jit(solution)/shard_map/ppermute | solution.py:880
  395.2 53.7 %collective-permute-start.16 = (bf16[256,1024]{1,0:T(8,128)(2,1)}, bf16[256,1024]{1,0:T(8,128)(2,1)}, u32[]{:S(2)}, u32[]{:S(2)}) collective-permute-start(bf16[256,1024]{1,0:T(8,128)(2,1)} %get-tuple-element.123), channel_id=1, source_target_pairs={{0,1},{1,0},{2,3},{3,2},{4,5},{5,4},{6,7},{7,6},{8,9},{9,8},{10,11... | collective-permute-start | bytes 1572872 | tf_op jit(solution)/shard_map/ppermute | solution.py:880
  395.2 76.9 %collective-permute-start.15 = (bf16[256,1024]{1,0:T(8,128)(2,1)}, bf16[256,1024]{1,0:T(8,128)(2,1)}, u32[]{:S(2)}, u32[]{:S(2)}) collective-permute-start(bf16[256,1024]{1,0:T(8,128)(2,1)} %get-tuple-element.122), channel_id=1, source_target_pairs={{0,1},{1,0},{2,3},{3,2},{4,5},{5,4},{6,7},{7,6},{8,9},{9,8},{10,11... | collective-permute-start | bytes 1572872 | tf_op jit(solution)/shard_map/ppermute | solution.py:880
  412.4 32.8 %all-to-all-start.5 = ((bf16[8,256,256]{1,2,0:T(8,128)(2,1)}), bf16[8,256,256]{1,2,0:T(8,128)(2,1)S(1)}, u32[]{:S(2)}, u32[]{:S(2)}) async-start(bf16[8,256,256]{1,2,0:T(8,128)(2,1)} %copy.116), calls=%async_computation.5 | async-start | bytes 2097152 | tf_op jit(solution)/shard_map/all_to_all | solution.py:907
  445.2 19.3 %all-to-all-start.6 = ((bf16[32,32,256]{2,1,0:T(8,128)(2,1)}), bf16[32,32,256]{2,1,0:T(8,128)(2,1)}, u32[]{:S(2)}, u32[]{:S(2)}) async-start(bf16[32,32,256]{2,1,0:T(8,128)(2,1)} %bitcast.54), calls=%async_computation.7 | async-start | bytes 1048576 | tf_op jit(solution)/shard_map/all_to_all | solution.py:907
  451.2 20.9 %collective-permute-start.17 = (bf16[256,1024]{1,0:T(8,128)(2,1)}, bf16[256,1024]{1,0:T(8,128)(2,1)}, u32[]{:S(2)}, u32[]{:S(2)}) collective-permute-start(bf16[256,1024]{1,0:T(8,128)(2,1)} %fusion.27), channel_id=1, source_target_pairs={{0,2},{1,3},{2,0},{3,1},{4,6},{5,7},{6,4},{7,5},{8,10},{9,11},{10,... | collective-permute-start | bytes 1572872 | tf_op jit(solution)/shard_map/ppermute | solution.py:880
  (62 other events, 826.1 us)
Sparse Core Ops, SparseCore 0:
  11.5 68.5 all-gather.3
  115.9 98.2 all-gather.5
  241.4 83.9 all-gather.7
  328.8 95.4 reduce-scatter.1

commit v6 on v5

--- a/solution.py
+++ b/solution.py
@@ -988,10 +988,9 @@
     wide = bias_up.shape[0]
     b_up = vector(4 * shard, wide)
     b_down = vector(4 * shard + wide, shard)
-    pair = jnp.stack(
-        [w_qk.reshape(shard, HEADS, HEAD_DIM), w_value.reshape(shard, HEADS, HEAD_DIM)], axis=2
-    ).reshape(shard, 2 * features)
-    m_pair = lax.all_gather(pair.astype(BF), "seq", axis=0, tiled=True)
+    m_pair = lax.all_gather(
+        jnp.concatenate([w_qk.astype(BF), w_value.astype(BF)], axis=1), "seq", axis=0, tiled=True
+    )
     half = HEADS * wide
     up_cols = jnp.transpose(
         w_up.astype(BF).reshape(shard, HEADS, ROUNDS, wide), (2, 0, 1, 3)
@@ -1010,8 +1009,8 @@
     )
     grad_f_all = jnp.concatenate(grad_f_all)
     rows = linear(normed_one, m_pair).astype(BF)
-    rows = jnp.transpose(rows.reshape(tokens, HEADS, 2 * HEAD_DIM), (1, 0, 2))
-    own = exchange(rows, columns()).reshape(HEADS * tokens, 2 * HEAD_DIM)
+    rows = jnp.transpose(rows.reshape(tokens, 2, HEADS, HEAD_DIM), (2, 0, 1, 3))
+    own = exchange(rows.reshape(HEADS, tokens, 2 * HEAD_DIM), columns()).reshape(HEADS * tokens, 2 * HEAD_DIM)
     own, near_rows = lax.optimization_barrier((own, near_rows))
     m_ffn = lax.all_gather(
         jnp.concatenate([near_rows, w_down.astype(BF)], axis=1),
@@ -1020,15 +1019,16 @@
         tiled=True,
         axis_index_groups=columns(),
     )
-    m_up, m_out, m_down = (m_ffn[:, at : at + features] for at in (0, half, half + features))
     turn = (place % ROUNDS).astype(jnp.int32).reshape(1)
     *sent, kept_rows = run_forward(turn, gather_group(own), info)
     far = merge_pair(sent[2], swap(sent[3], 1))
     mixed, total_lse = merge_final(sent[0], swap(sent[1], 1), swap(far, 2))
     mixed = exchange(mixed, columns())
+    m_ffn, normed_one = lax.optimization_barrier((m_ffn, normed_one))
+    m_up, m_out, m_down = (m_ffn[:, at : at + features] for at in (0, half, half + features))
     grad_hidden = outer_cols(grad_f_all, m_down)
-    mixed, normed_one, grad_hidden, total_lse = lax.optimization_barrier(
-        (mixed, normed_one, grad_hidden, gather_group(total_lse))
+    mixed, grad_hidden, total_lse = lax.optimization_barrier(
+        (mixed, grad_hidden, gather_group(total_lse))
     )
     normed_col = lax.all_gather(
         normed_one, "seq", axis=0, tiled=True, axis_index_groups=columns()
@@ -1037,18 +1037,26 @@
     y_first = x_first + linear(mixed, m_out)
     normed_two, hat_two, inv_two = layer_norm(y_first, gain_two, shift_two)
     normed_two = normed_two.astype(BF)
-    normed_all = jnp.concatenate(gather_group(normed_two))
-    pre_up = linear(normed_all, m_up) + b_up
-    hidden, gelu_back = jax.vjp(partial(jax.nn.gelu, approximate=True), pre_up)
-    hidden = hidden.astype(BF)
-    branch = sum_group(linear(hidden, m_down).reshape(ROUNDS, tokens, features))
-    y_second = x_second + (branch + b_down)
+    side = swap(normed_two, 2)
+    halves = (
+        jnp.concatenate([normed_two, swap(normed_two, 1)]),
+        jnp.concatenate([side, swap(side, 1)]),
+    )
+    found = []
+    for at, rows in enumerate(halves):
+        pre_up = linear(rows, m_up) + b_up
+        hidden, gelu_back = jax.vjp(partial(jax.nn.gelu, approximate=True), pre_up)
+        grad_pre = grad_hidden[at * 2 * tokens : (at + 1) * 2 * tokens]
+        grad_pre = gelu_back(grad_pre)[0].astype(BF)
+        grad_two = outer_cols(grad_pre, m_up)
+        found.append((hidden.astype(BF), grad_pre, grad_two[:tokens], grad_two[tokens:]))
+    normed_all = jnp.concatenate(halves)
+    hidden, grad_pre = (jnp.concatenate([found[0][at], found[1][at]]) for at in range(2))
     grad_down = inner_rows(hidden, grad_f_all)
     grad_bias_down = jnp.sum(grad_f.astype(F32), axis=0)
-    grad_pre = gelu_back(grad_hidden)[0].astype(BF)
     grad_up = inner_rows(normed_all, grad_pre)
     grad_bias_up = jnp.sum(grad_pre.astype(F32), axis=0)
-    grad_two = sum_group(outer_cols(grad_pre, m_up).reshape(ROUNDS, tokens, features))
+    grad_two = sum_group([*found[0][2:], *found[1][2:]])
     grad_gain_ffn = jnp.sum(grad_two * hat_two, axis=0)
     grad_bias_ffn = jnp.sum(grad_two, axis=0)
     dx_first = dy_first + norm_back(grad_two, hat_two, inv_two, gain_two)
@@ -1064,7 +1072,10 @@
     parts = jnp.transpose(parts.reshape(PARTS, HEADS, -1, HEAD_DIM), (1, 2, 0, 3))
     parts = parts.reshape(HEADS, -1, HEAD_DIM).astype(BF)
     grad_mixed = jnp.transpose(grad_mixed.reshape(tokens, HEADS, HEAD_DIM), (1, 0, 2))
-    grad_mixed = exchange(jnp.concatenate([grad_mixed, parts], axis=1), columns())
+    grad_mixed, normed_col = lax.optimization_barrier(
+        (jnp.concatenate([grad_mixed, parts], axis=1), normed_col)
+    )
+    grad_mixed = exchange(grad_mixed, columns())
     grad_out = sum_group(
         [
             lax.dynamic_slice_in_dim(grad_out, ((place % ROUNDS) ^ near) * fourth, fourth, axis=1)
@@ -1105,19 +1116,28 @@
     grad_head = run_backward(
         turn, grad_mixed, total_lse, kept_rows, info
     )
-    grad_head = sum_group([x.astype(F32) for x in grad_head]).astype(BF)
+    near_head = grad_head[0].astype(F32) + swap(grad_head[1], 1).astype(F32)
+    far_head = grad_head[2].astype(F32) + swap(grad_head[3], 1).astype(F32)
+    far_head, hidden = lax.optimization_barrier((far_head.astype(BF), hidden))
+    far_head = swap(far_head, 2)
+    branch = linear(hidden, m_down).reshape(ROUNDS, tokens, features)
+    branch_near = branch[0] + swap(branch[1].astype(BF), 1).astype(F32)
+    branch_far = (branch[2] + swap(branch[3].astype(BF), 1).astype(F32)).astype(BF)
+    far_head, near_head, branch_near, branch_far, grad_bias_up, grad_bias_down = (
+        lax.optimization_barrier(
+            (far_head, near_head, branch_near, branch_far, grad_bias_up, grad_bias_down)
+        )
+    )
+    grad_head = (near_head + far_head.astype(F32)).astype(BF)
+    branch = branch_near + swap(branch_far, 2).astype(F32)
+    y_second = x_second + (branch + b_down)
     grad_rows = exchange(grad_head.reshape(HEADS, tokens, 2 * HEAD_DIM), columns())
     s_pair = inner_rows(normed_col, grad_head).astype(BF).reshape(devices, shard, 2 * HEAD_DIM)
-    grad_rows, s_pair, s_up, s_out, s_down = lax.optimization_barrier(
-        (grad_rows, s_pair, s_up, s_out, s_down)
-    )
-    grad_rows = jnp.transpose(grad_rows, (1, 0, 2)).reshape(tokens, 2 * features)
-    s_pair = exchange(s_pair)
-    s_pair = jnp.sum(
-        s_pair.reshape(HEADS, ROUNDS, shard, 2, HEAD_DIM).astype(F32), axis=1
-    ).transpose(2, 1, 0, 3)
-    s_qk = s_pair[0].reshape(shard, features)
-    s_value = s_pair[1].reshape(shard, features)
+    grad_rows, s_pair, s_up, s_out, s_down, y_second = lax.optimization_barrier(
+        (grad_rows, s_pair, s_up, s_out, s_down, y_second)
+    )
+    grad_rows = grad_rows.reshape(HEADS, tokens, 2, HEAD_DIM)
+    grad_rows = jnp.transpose(grad_rows, (1, 2, 0, 3)).reshape(tokens, 2 * features)
     grad_one = outer_cols(grad_rows, m_pair)
     grad_gain_attn = jnp.sum(grad_one * hat_one, axis=0)
     grad_bias_attn = jnp.sum(grad_one, axis=0)
@@ -1135,8 +1155,18 @@
         ],
         axis=1,
     )
-    small, s_qk, s_value = lax.optimization_barrier((small, s_qk, s_value))
-    small = jnp.sum(exchange(small[:, None]), axis=(0, 1))
+    count = small.shape[1]
+    lines = -(-3 * count // (2 * HEAD_DIM))
+    small = jnp.transpose(split_three(small), (1, 0, 2)).reshape(devices, 3 * count)
+    small = jnp.pad(small, ((0, 0), (0, lines * 2 * HEAD_DIM - 3 * count)))
+    small = small.astype(BF).reshape(devices, lines, 2 * HEAD_DIM)
+    both = exchange(jnp.concatenate([s_pair, small], axis=1))
+    small = both[:, shard:].reshape(devices, -1)[:, : 3 * count].astype(F32)
+    small = jnp.sum(small.reshape(devices * 3, count), axis=0)
+    s_pair = both[:, :shard].reshape(HEADS, ROUNDS, shard, 2, HEAD_DIM)
+    s_pair = jnp.sum(s_pair.astype(F32), axis=1).transpose(2, 1, 0, 3)
+    s_qk = s_pair[0].reshape(shard, features)
+    s_value = s_pair[1].reshape(shard, features)
     s_gattn, s_battn, s_gffn, s_bffn = (small[i * shard : (i + 1) * shard] for i in range(4))
     s_bup = small[4 * shard : 4 * shard + wide]
     s_bdown = small[4 * shard + wide :]

time: 493 us -> 479 us (0.972)
  waiting for transfers between devices: 208 us -> 202 us
  starting transfers between devices: 54.7 us -> 49.3 us
    all_to_all x8 -> x7, waiting for transfers between devices: 73.4 us -> 64.9 us  [exchange(): lax.all_to_all(x, 'seq', split_axis=0, concat_axis=0, tiled=True, axis_in...]
    all_to_all x8 -> x7, starting transfers between devices: 33.6 us -> 29.2 us  [exchange(): lax.all_to_all(x, 'seq', split_axis=0, concat_axis=0, tiled=True, axis_in...]
    dot_general x4 -> x5, matrix products: 20.5 us -> 16.7 us  [outer_cols(): lax.dot_general(matrix_a, matrix_b, (((1,), (1,)), ((), ())), preferred_e...]
    dot_general x4 -> x5, matrix products: 17.8 us -> 20.3 us  [linear(): return jnp.dot(matrix_a, matrix_b, preferred_element_type=jnp.float32)]
    unnamed x93 -> x137, local copies, waits for them, and re-layouts: 12 us -> 12.8 us
  transfers between devices with their start and end apart: 45 -> 44, of which waited for: 28 -> 25; matrix products, arithmetic and copies ran while one was open for 23% -> 21% of each run, Pallas kernels for 17% -> 17%
where the time goes in v6:
time: 479 us; the launch traced here: 473 us
  waiting for transfers between devices  202 us (42%)
  Pallas kernels  81.3 us (17%)
  matrix products  52.6 us (11%)
  starting transfers between devices  49.3 us (10%)
  other arithmetic  39.4 us (8%)
  local copies, waits for them, and re-layouts  32.6 us (7%)
  between operations  15.5 us (3%)
    ppermute x33, waiting for transfers between devices, swap(): return lax.ppermute(x, 'seq', peers(mask))  104 us
    pallas_call x4, Pallas kernels, run_kernel(): pl.pallas_call(kernel, out_shape=tuple((jax.ShapeDtypeStruct(shape, BF) f...  81.3 us
    all_to_all x7, waiting for transfers between devices, exchange(): lax.all_to_all(x, 'seq', split_axis=0, concat_axis=0, tiled=True, axis_in...  64.9 us
    all_to_all x7, starting transfers between devices, exchange(): lax.all_to_all(x, 'seq', split_axis=0, concat_axis=0, tiled=True, axis_in...  29.2 us
    all_gather x1, waiting for transfers between devices, shards_fast(): lax.all_gather(jnp.concatenate([w_qk.astype(BF), w_value.astype(BF)], axi...  28.3 us
    dot_general x5, matrix products, linear(): return jnp.dot(matrix_a, matrix_b, preferred_element_type=jnp.float32)  20.3 us
    ppermute x33, starting transfers between devices, swap(): return lax.ppermute(x, 'seq', peers(mask))  19.3 us
    dot_general x5, matrix products, outer_cols(): lax.dot_general(matrix_a, matrix_b, (((1,), (1,)), ((), ())), preferred_e...  16.7 us
  transfers between devices with their start and end apart: 44, of which 25 were waited for; matrix products, arithmetic and copies ran while one was open for 21% of the time, Pallas kernels for 17%

profile of v6, /device:TPU:0, one launch (start us, length us, event | category | flops | bytes accessed | tf_op | source)
XLA Modules:
  0.0 472.7 jit_solution(289654038069103234)
XLA Ops:
  18.1 5.0 %all-to-all-start = ((f32[32,8,256]{2,1,0:T(8,128)}), f32[32,8,256]{2,1,0:T(8,128)S(1)}, u32[]{:S(2)}, u32[]{:S(2)}) async-start(f32[32,8,256]{2,1,0:T(8,128)} %bitcast.35), calls=%async_computation | async-start | bytes 524288 | tf_op jit(solution)/shard_map/all_to_all | solution.py:907
  29.2 5.9 %all-to-all-done.info = f32[32,8,256]{2,1,0:T(8,128)S(1)} async-done(((f32[32,8,256]{2,1,0:T(8,128)}), f32[32,8,256]{2,1,0:T(8,128)S(1)}, u32[]{:S(2)}, u32[]{:S(2)}) %all-to-all-start) | async-done | bytes 262176 | tf_op jit(solution)/shard_map/all_to_all | solution.py:907
  40.5 10.7 %all-to-all-done.1 = bf16[4,32,2048]{2,1,0:T(8,128)(2,1)S(1)} async-done(((bf16[4,32,2048]{2,1,0:T(8,128)(2,1)}), bf16[4,32,2048]{2,1,0:T(8,128)(2,1)S(1)}, u32[]{:S(2)}, u32[]{:S(2)}) %all-to-all-start.1) | async-done | bytes 524320 | tf_op jit(solution)/shard_map/all_to_all | solution.py:907
  51.1 28.3 %all-gather.4.cloned.1.call-done = bf16[1024,2048]{1,0:T(8,128)(2,1)} async-done(((bf16[32,2048]{1,0:T(8,128)(2,1)}), bf16[1024,2048]{1,0:T(8,128)(2,1)}) %all-gather.4.cloned.1.call-update) | async-done | bytes 4194320 | tf_op jit(solution)/shard_map/all_gather | solution.py:991
  90.1 25.6 %all-to-all-done.2 = bf16[8,256,256]{2,1,0:T(8,128)(2,1)S(1)} async-done(((bf16[8,256,256]{2,1,0:T(8,128)(2,1)}), bf16[8,256,256]{2,1,0:T(8,128)(2,1)S(1)}, u32[]{:S(2)}, u32[]{:S(2)}) %all-to-all-start.2) | async-done | bytes 1048608 | tf_op jit(solution)/shard_map/all_to_all | solution.py:907
  117.7 23.3 %collective-permute-done.4.x_2 = bf16[2048,256]{1,0:T(8,128)(2,1)S(1)} collective-permute-done((bf16[2048,256]{1,0:T(8,128)(2,1)S(1)}, bf16[2048,256]{1,0:T(8,128)(2,1)S(1)}, u32[]{:S(2)}, u32[]{:S(2)}) %collective-permute-start.4) | collective-permute-done | bytes 1048608 | tf_op jit(solution)/shard_map/ppermute | solution.py:880
  144.6 35.6 %hash_forward.1 = (bf16[8,272,128]{2,1,0:T(8,128)(2,1)S(1)}, bf16[8,272,128]{2,1,0:T(8,128)(2,1)S(1)}, bf16[8,272,128]{2,1,0:T(8,128)(2,1)S(1)}, bf16[8,272,128]{2,1,0:T(8,128)(2,1)S(1)}, bf16[8256,256]{1,0:T(8,128)(2,1)}) custom-call(s32[1]{0:T(128)} %bitcast.place, bf16[2048,256]{1,0:T(8,128)(2,1)S(1)} %bitcast.172, ...), custom_call_target="tpu_custom_call" | custom-call | flops 20000000000 | bytes 12000000 | tf_op jit(solution)/shard_map/hash_forward/pallas_call | solution.py:817
  191.7 8.8 %collective-permute-done.8.c = bf16[8,272,128]{2,1,0:T(8,128)(2,1)S(1)} collective-permute-done((bf16[8,272,128]{2,1,0:T(8,128)(2,1)S(1)}, bf16[8,272,128]{2,1,0:T(8,128)(2,1)S(1)}, u32[]{:S(2)}, u32[]{:S(2)}) %collective-permute-start.8) | collective-permute-done | bytes 557088 | tf_op jit(solution)/shard_map/ppermute | solution.py:880
  200.5 4.8 %merge_final.1 = (bf16[8,256,128]{2,1,0:T(8,128)(2,1)}, bf16[8,16,128]{2,1,0:T(8,128)(2,1)S(1)}) custom-call(bf16[8,272,128]{2,1,0:T(8,128)(2,1)S(1)} %get-tuple-element.66.a, bf16[8,272,128]{2,1,0:T(8,128)(2,1)S(1)} %collective-permute-done.6.b, bf16[8,272,128]{2,1,0:T(8,128)(2,1)S(1)} %collective-permute-done.8.c), custom_call_target="tpu_custom_call" | custom-call | flops 10000000 | bytes 2000000 | tf_op jit(solution)/shard_map/merge_final/pallas_call | solution.py:817
  205.3 4.5 all-to-all-start.3
  216.8 6.8 %fusion.31 = f32[1024,1024]{1,0:T(8,128)} fusion(bf16[1024,1024]{1,0:T(8,128)(2,1)} %constant_dynamic-update-slice_fusion, bf16[1024,3072]{1,0:T(8,128)(2,1)} %all-gather.6.cloned.1.call-done), kind=kOutput, calls=%fused_computation.44 | convolution fusion | flops 2147483648 | bytes 8388608 | tf_op jit(solution)/shard_map/dot_general | solution.py:59
  230.1 12.0 %collective-permute-done.14 = bf16[256,1024]{1,0:T(8,128)(2,1)S(1)} collective-permute-done((bf16[256,1024]{1,0:T(8,128)(2,1)S(1)}, bf16[256,1024]{1,0:T(8,128)(2,1)S(1)}, u32[]{:S(2)}, u32[]{:S(2)}) %collective-permute-start.14) | collective-permute-done | bytes 524320 | tf_op jit(solution)/shard_map/ppermute | solution.py:880
  245.4 7.2 %fusion.6 = (bf16[512,1024]{1,0:T(8,128)(2,1)S(1)}, bf16[512,1024]{1,0:T(8,128)(2,1)S(1)}, bf16[512,1024]{1,0:T(8,128)(2,1)S(1)}, bf16[512,1024]{1,0:T(8,128)(2,1)}) fusion(f32[1024,1024]{1,0:T(8,128)S(1)} %copy-done.59, f32[512,1024]{1,0:T(8,128)S(1)} %fusion.43, f32[1024]{0:T(1024)S(1)} %bitcast.237, bf16[1024,3072]{1,0:T(8,128)(2,1)} %all-gather.6.cloned.1.call-done, ...), kind=kOutput, calls=%fused_computation.13 | convolution fusion | flops 1099956224 | bytes 13635584 | tf_op jit(solution)/shard_map/dot_general | solution.py:49
  259.5 6.3 %convolution_convert_fusion.1 = bf16[1024,1024]{1,0:T(8,128)(2,1)} fusion(bf16[1024,1024]{1,0:T(8,128)(2,1)} %constant_dynamic-update-slice_fusion, bf16[512,1024]{1,0:T(8,128)(2,1)S(1)} %get-tuple-element.140, bf16[512,1024]{1,0:T(8,128)(2,1)} %get-tuple-element.141), kind=kOutput, calls=%fused_computation.37 | convolution fusion | flops 2152726528 | bytes 6291456 | tf_op jit(solution)/shard_map/dot_general | solution.py:53
  265.8 6.6 %collective-permute-done.17 = bf16[256,1024]{1,0:T(8,128)(2,1)} collective-permute-done((bf16[256,1024]{1,0:T(8,128)(2,1)}, bf16[256,1024]{1,0:T(8,128)(2,1)}, u32[]{:S(2)}, u32[]{:S(2)}) %collective-permute-start.17) | collective-permute-done | bytes 524320 | tf_op jit(solution)/shard_map/ppermute | solution.py:880
  286.9 4.5 all-gather.8.cloned.1.call-done
  303.8 5.8 %all-to-all-done.4.g_0 = bf16[8,272,128]{2,1,0:T(8,128)(2,1)S(1)} async-done(((bf16[8,272,128]{2,1,0:T(8,128)(2,1)}), bf16[8,272,128]{2,1,0:T(8,128)(2,1)S(1)}, u32[]{:S(2)}, u32[]{:S(2)}) %all-to-all-start.4) | async-done | bytes 557088 | tf_op jit(solution)/shard_map/all_to_all | solution.py:907
  313.2 13.2 %collective-permute-done.22.g_2 = bf16[8,272,128]{2,1,0:T(8,128)(2,1)S(1)} collective-permute-done((bf16[8,272,128]{2,1,0:T(8,128)(2,1)S(1)}, bf16[8,272,128]{2,1,0:T(8,128)(2,1)S(1)}, u32[]{:S(2)}, u32[]{:S(2)}) %collective-permute-start.22) | collective-permute-done | bytes 557088 | tf_op jit(solution)/shard_map/ppermute | solution.py:880
  329.8 37.2 %hash_backward.1 = (bf16[2048,256]{1,0:T(8,128)(2,1)S(1)}, bf16[2048,256]{1,0:T(8,128)(2,1)S(1)}, bf16[2048,256]{1,0:T(8,128)(2,1)S(1)}, bf16[2048,256]{1,0:T(8,128)(2,1)}) custom-call(s32[1]{0:T(128)} %bitcast.place, bf16[8,272,128]{2,1,0:T(8,128)(2,1)S(1)} %all-to-all-done.4.g_0, bf16[8,272,128]{2,1,0:T(8,128)(2,1)S(1)} %collective-permute-done.21.g_1, ...), custom_call_target="tpu_custom_call" | custom-call | flops 20000000000 | bytes 12000000 | tf_op jit(solution)/shard_map/hash_backward/pallas_call | solution.py:817
  385.5 15.5 %collective-permute-done.25 = bf16[2048,256]{1,0:T(8,128)(2,1)S(1)} collective-permute-done((bf16[2048,256]{1,0:T(8,128)(2,1)S(1)}, bf16[2048,256]{1,0:T(8,128)(2,1)S(1)}, u32[]{:S(2)}, u32[]{:S(2)}) %collective-permute-start.25) | collective-permute-done | bytes 1048608 | tf_op jit(solution)/shard_map/ppermute | solution.py:880
  412.4 7.6 %collective-permute-done.32 = bf16[256,1024]{1,0:T(8,128)(2,1)} collective-permute-done((bf16[256,1024]{1,0:T(8,128)(2,1)}, bf16[256,1024]{1,0:T(8,128)(2,1)}, u32[]{:S(2)}, u32[]{:S(2)}) %collective-permute-start.32) | collective-permute-done | bytes 524320 | tf_op jit(solution)/shard_map/ppermute | solution.py:880
  432.6 4.7 multiply_reduce_fusion.1
  438.8 4.8 %all-to-all-start.6 = ((bf16[32,36,256]{2,1,0:T(8,128)(2,1)}), bf16[32,36,256]{2,1,0:T(8,128)(2,1)S(1)}, u32[]{:S(2)}, u32[]{:S(2)}) async-start(bf16[32,36,256]{2,1,0:T(8,128)(2,1)} %pad_maximum_fusion.5), calls=%async_computation.7 | async-start | bytes 1310720 | tf_op jit(solution)/shard_map/all_to_all | solution.py:907
  446.2 15.3 %all-to-all-done.6 = bf16[32,36,256]{2,1,0:T(8,128)(2,1)S(1)} async-done(((bf16[32,36,256]{2,1,0:T(8,128)(2,1)}), bf16[32,36,256]{2,1,0:T(8,128)(2,1)S(1)}, u32[]{:S(2)}, u32[]{:S(2)}) %all-to-all-start.6) | async-done | bytes 589856 | tf_op jit(solution)/shard_map/all_to_all | solution.py:907
  (376 shorter events, 157.3 us)
Async XLA Ops:
  7.3 72.1 %all-gather.4.cloned.1.call-start = ((), (), s32[]{:S(2)}) async-start(), calls=%async_computation.8 | async-start | bytes 4325376 | tf_op jit(solution)/shard_map/all_gather | solution.py:991
  11.9 16.8 %collective-permute-start.1 = (bf16[256,1024]{1,0:T(8,128)(2,1)S(1)}, bf16[256,1024]{1,0:T(8,128)(2,1)S(1)}, u32[]{:S(2)}, u32[]{:S(2)}) collective-permute-start(bf16[256,1024]{1,0:T(8,128)(2,1)S(1)} %get-tuple-element.71), channel_id=1, source_target_pairs={{0,2},{1,3},{2,0},{3,1},{4,6},{5,7},{6,4},{7,5},{8,10},{9,11},{10,... | collective-permute-start | bytes 1572872 | tf_op jit(solution)/shard_map/ppermute | solution.py:880
  14.8 36.3 %collective-permute-start = (bf16[256,1024]{1,0:T(8,128)(2,1)S(1)}, bf16[256,1024]{1,0:T(8,128)(2,1)}, u32[]{:S(2)}, u32[]{:S(2)}) collective-permute-start(bf16[256,1024]{1,0:T(8,128)(2,1)S(1)} %get-tuple-element.71), channel_id=1, source_target_pairs={{0,1},{1,0},{2,3},{3,2},{4,5},{5,4},{6,7},{7,6},{8,9},{9,8},{10,11... | collective-permute-start | bytes 1572872 | tf_op jit(solution)/shard_map/ppermute | solution.py:880
  18.1 17.1 %all-to-all-start = ((f32[32,8,256]{2,1,0:T(8,128)}), f32[32,8,256]{2,1,0:T(8,128)S(1)}, u32[]{:S(2)}, u32[]{:S(2)}) async-start(f32[32,8,256]{2,1,0:T(8,128)} %bitcast.35), calls=%async_computation | async-start | bytes 524288 | tf_op jit(solution)/shard_map/all_to_all | solution.py:907
  28.7 22.5 %collective-permute-start.2 = (bf16[256,1024]{1,0:T(8,128)(2,1)S(1)}, bf16[256,1024]{1,0:T(8,128)(2,1)}, u32[]{:S(2)}, u32[]{:S(2)}) collective-permute-start(bf16[256,1024]{1,0:T(8,128)(2,1)S(1)} %collective-permute-done.1), channel_id=1, source_target_pairs={{0,1},{1,0},{2,3},{3,2},{4,5},{5,4},{6,7},{7,6},{8,9},{9,8},{10,11... | collective-permute-start | bytes 1572872 | tf_op jit(solution)/shard_map/ppermute | solution.py:880
  35.1 16.0 %all-to-all-start.1 = ((bf16[4,32,2048]{2,1,0:T(8,128)(2,1)}), bf16[4,32,2048]{2,1,0:T(8,128)(2,1)S(1)}, u32[]{:S(2)}, u32[]{:S(2)}) async-start(bf16[4,32,2048]{2,1,0:T(8,128)(2,1)} %pad_maximum_fusion.7), calls=%async_computation.1 | async-start | bytes 1048576 | tf_op jit(solution)/shard_map/all_to_all | solution.py:907
  85.4 30.3 %all-to-all-start.2 = ((bf16[8,256,256]{2,1,0:T(8,128)(2,1)}), bf16[8,256,256]{2,1,0:T(8,128)(2,1)S(1)}, u32[]{:S(2)}, u32[]{:S(2)}) async-start(bf16[8,256,256]{2,1,0:T(8,128)(2,1)} %reshape.779), calls=%async_computation.2 | async-start | bytes 2097152 | tf_op jit(solution)/shard_map/all_to_all | solution.py:907
  89.5 127.3 %all-gather.6.cloned.1.call-start = ((), (), s32[]{:S(2)}) async-start(), calls=%async_computation.9 | async-start | bytes 7077888 | tf_op jit(solution)/shard_map/all_gather | solution.py:1015
  116.7 24.3 %collective-permute-start.4 = (bf16[2048,256]{1,0:T(8,128)(2,1)S(1)}, bf16[2048,256]{1,0:T(8,128)(2,1)S(1)}, u32[]{:S(2)}, u32[]{:S(2)}) collective-permute-start(bf16[2048,256]{1,0:T(8,128)(2,1)S(1)} %bitcast.170), channel_id=1, source_target_pairs={{0,2},{1,3},{2,0},{3,1},{4,6},{5,7},{6,4},{7,5},{8,10},{9,11},{10,... | collective-permute-start | bytes 3145736 | tf_op jit(solution)/shard_map/ppermute | solution.py:880
  117.7 23.3 %collective-permute-start.3 = (bf16[2048,256]{1,0:T(8,128)(2,1)S(1)}, bf16[2048,256]{1,0:T(8,128)(2,1)}, u32[]{:S(2)}, u32[]{:S(2)}) collective-permute-start(bf16[2048,256]{1,0:T(8,128)(2,1)S(1)} %bitcast.171), channel_id=1, source_target_pairs={{0,1},{1,0},{2,3},{3,2},{4,5},{5,4},{6,7},{7,6},{8,9},{9,8},{10,11... | collective-permute-start | bytes 3145736 | tf_op jit(solution)/shard_map/ppermute | solution.py:880
  185.8 14.7 %collective-permute-start.8 = (bf16[8,272,128]{2,1,0:T(8,128)(2,1)S(1)}, bf16[8,272,128]{2,1,0:T(8,128)(2,1)S(1)}, u32[]{:S(2)}, u32[]{:S(2)}) collective-permute-start(bf16[8,272,128]{2,1,0:T(8,128)(2,1)S(1)} %merge_pair.1), channel_id=1, source_target_pairs={{0,2},{1,3},{2,0},{3,1},{4,6},{5,7},{6,4},{7,5},{8,10},{9,11},{10,... | collective-permute-start | bytes 1671176 | tf_op jit(solution)/shard_map/ppermute | solution.py:880
  205.3 19.9 %all-to-all-start.3 = ((bf16[8,256,128]{2,1,0:T(8,128)(2,1)}), bf16[8,256,128]{2,1,0:T(8,128)(2,1)S(1)}, u32[]{:S(2)}, u32[]{:S(2)}) async-start(bf16[8,256,128]{2,1,0:T(8,128)(2,1)} %get-tuple-element.70), calls=%async_computation.3 | async-start | bytes 1048576 | tf_op jit(solution)/shard_map/all_to_all | solution.py:907
  209.8 81.5 %all-gather.8.cloned.1.call-start = ((), (), s32[]{:S(2)}) async-start(), calls=%async_computation.10 | async-start | bytes 4718592 | tf_op jit(solution)/shard_map/all_gather | solution.py:1033
  228.6 13.4 %collective-permute-start.14 = (bf16[256,1024]{1,0:T(8,128)(2,1)S(1)}, bf16[256,1024]{1,0:T(8,128)(2,1)S(1)}, u32[]{:S(2)}, u32[]{:S(2)}) collective-permute-start(bf16[256,1024]{1,0:T(8,128)(2,1)S(1)} %add_convert_fusion.4), channel_id=1, source_target_pairs={{0,2},{1,3},{2,0},{3,1},{4,6},{5,7},{6,4},{7,5},{8,10},{9,11},{10,... | collective-permute-start | bytes 1572872 | tf_op jit(solution)/shard_map/ppermute | solution.py:880
  257.8 14.6 %collective-permute-start.17 = (bf16[256,1024]{1,0:T(8,128)(2,1)}, bf16[256,1024]{1,0:T(8,128)(2,1)}, u32[]{:S(2)}, u32[]{:S(2)}) collective-permute-start(bf16[256,1024]{1,0:T(8,128)(2,1)} %fusion.49), channel_id=1, source_target_pairs={{0,2},{1,3},{2,0},{3,1},{4,6},{5,7},{6,4},{7,5},{8,10},{9,11},{10,... | collective-permute-start | bytes 1572872 | tf_op jit(solution)/shard_map/ppermute | solution.py:880
  283.1 16.2 %collective-permute-start.18 = (bf16[1024,256]{1,0:T(8,128)(2,1)}, bf16[1024,256]{1,0:T(8,128)(2,1)}, u32[]{:S(2)}, u32[]{:S(2)}) collective-permute-start(bf16[1024,256]{1,0:T(8,128)(2,1)} %get-tuple-element.138), channel_id=1, source_target_pairs={{0,1},{1,0},{2,3},{3,2},{4,5},{5,4},{6,7},{7,6},{8,9},{9,8},{10,11... | collective-permute-start | bytes 1572872 | tf_op jit(solution)/shard_map/ppermute | solution.py:880
  284.6 14.7 %collective-permute-start.20 = (bf16[1024,256]{1,0:T(8,128)(2,1)S(1)}, bf16[1024,256]{1,0:T(8,128)(2,1)S(1)}, u32[]{:S(2)}, u32[]{:S(2)}) collective-permute-start(bf16[1024,256]{1,0:T(8,128)(2,1)S(1)} %add_convert_fusion.3), channel_id=1, source_target_pairs={{0,2},{1,3},{2,0},{3,1},{4,6},{5,7},{6,4},{7,5},{8,10},{9,11},{10,... | collective-permute-start | bytes 1572872 | tf_op jit(solution)/shard_map/ppermute | solution.py:880
  291.4 18.3 %all-to-all-start.4 = ((bf16[8,272,128]{2,1,0:T(8,128)(2,1)}), bf16[8,272,128]{2,1,0:T(8,128)(2,1)S(1)}, u32[]{:S(2)}, u32[]{:S(2)}) async-start(bf16[8,272,128]{2,1,0:T(8,128)(2,1)} %pad_maximum_fusion.6), calls=%async_computation.4 | async-start | bytes 1114112 | tf_op jit(solution)/shard_map/all_to_all | solution.py:907
  294.9 127.7 %reduce-scatter.2.cloned.1.call-start = ((), (), s32[]{:S(2)}) async-start(), calls=%async_computation.11 | async-start | bytes 5308416 | tf_op jit(solution)/shard_map/reduce_scatter | solution.py:1091
  311.6 14.7 %collective-permute-start.22 = (bf16[8,272,128]{2,1,0:T(8,128)(2,1)S(1)}, bf16[8,272,128]{2,1,0:T(8,128)(2,1)S(1)}, u32[]{:S(2)}, u32[]{:S(2)}) collective-permute-start(bf16[8,272,128]{2,1,0:T(8,128)(2,1)S(1)} %all-to-all-done.4.g_0), channel_id=1, source_target_pairs={{0,2},{1,3},{2,0},{3,1},{4,6},{5,7},{6,4},{7,5},{8,10},{9,11},{10,... | collective-permute-start | bytes 1671176 | tf_op jit(solution)/shard_map/ppermute | solution.py:880
  375.7 25.3 %collective-permute-start.25 = (bf16[2048,256]{1,0:T(8,128)(2,1)S(1)}, bf16[2048,256]{1,0:T(8,128)(2,1)S(1)}, u32[]{:S(2)}, u32[]{:S(2)}) collective-permute-start(bf16[2048,256]{1,0:T(8,128)(2,1)S(1)} %add_convert_fusion.1), channel_id=1, source_target_pairs={{0,2},{1,3},{2,0},{3,1},{4,6},{5,7},{6,4},{7,5},{8,10},{9,11},{10,... | collective-permute-start | bytes 3145736 | tf_op jit(solution)/shard_map/ppermute | solution.py:880
  402.6 29.9 %all-to-all-start.5 = ((bf16[8,256,256]{1,2,0:T(8,128)(2,1)}), bf16[8,256,256]{1,2,0:T(8,128)(2,1)S(1)}, u32[]{:S(2)}, u32[]{:S(2)}) async-start(bf16[8,256,256]{1,2,0:T(8,128)(2,1)} %copy.123), calls=%async_computation.5 | async-start | bytes 2097152 | tf_op jit(solution)/shard_map/all_to_all | solution.py:907
  406.4 13.6 %collective-permute-start.32 = (bf16[256,1024]{1,0:T(8,128)(2,1)}, bf16[256,1024]{1,0:T(8,128)(2,1)}, u32[]{:S(2)}, u32[]{:S(2)}) collective-permute-start(bf16[256,1024]{1,0:T(8,128)(2,1)} %get-tuple-element.102), channel_id=1, source_target_pairs={{0,2},{1,3},{2,0},{3,1},{4,6},{5,7},{6,4},{7,5},{8,10},{9,11},{10,... | collective-permute-start | bytes 1572872 | tf_op jit(solution)/shard_map/ppermute | solution.py:880
  438.8 22.7 %all-to-all-start.6 = ((bf16[32,36,256]{2,1,0:T(8,128)(2,1)}), bf16[32,36,256]{2,1,0:T(8,128)(2,1)S(1)}, u32[]{:S(2)}, u32[]{:S(2)}) async-start(bf16[32,36,256]{2,1,0:T(8,128)(2,1)} %pad_maximum_fusion.5), calls=%async_computation.7 | async-start | bytes 1310720 | tf_op jit(solution)/shard_map/all_to_all | solution.py:907
  (82 other events, 688.8 us)
Sparse Core Ops, SparseCore 0:
  11.6 67.8 all-gather.3
  116.8 98.6 all-gather.5
  217.6 73.7 all-gather.7
  311.7 94.2 reduce-scatter.1

commit v7 on v6

--- a/solution.py
+++ b/solution.py
@@ -422,7 +422,7 @@
 
 
 CAP_ROWS = 16
-FORWARD_BATCH = 4
+FORWARD_BATCH = 8
 BACKWARD_BATCH = 2
 PARTS = 8
 
@@ -607,60 +607,71 @@
         lax.fori_loop(0, blocks // rounds, unpack, 0, unroll=4)
 
 
-def tall_parts(ref, group, first, tokens):
-    flat = jnp.concatenate(
+def flat_parts(ref, group, first, tokens):
+    return jnp.concatenate(
         [
             ref[group, first + piece * PARTS : first + (piece + 1) * PARTS, :].astype(F32)
             for piece in range(tokens // HEAD_DIM)
         ],
         axis=1,
     )
-    return jnp.transpose(flat)
-
-
-def put_parts(ref, group, first, column):
-    tokens = column.shape[0]
-    high, mid, low = three_parts(column)
-    lane = lax.broadcasted_iota(jnp.int32, (tokens, PARTS), 1)
-    tall = jnp.where(lane == 0, high, jnp.where(lane == 1, mid, jnp.where(lane == 2, low, 0.0)))
-    flat = jnp.transpose(tall).astype(BF)
+
+
+def tall_parts(ref, group, first, tokens):
+    return jnp.transpose(flat_parts(ref, group, first, tokens))
+
+
+def put_parts(ref, group, first, line):
+    tokens = line.shape[1]
+    high, mid, low = three_parts(line)
+    row = lax.broadcasted_iota(jnp.int32, (PARTS, tokens), 0)
+    flat = jnp.where(row == 0, high, jnp.where(row == 1, mid, jnp.where(row == 2, low, 0.0)))
+    flat = flat.astype(BF)
     for piece in range(tokens // HEAD_DIM):
         at = first + piece * PARTS
         ref[group, at : at + PARTS, :] = flat[:, piece * HEAD_DIM : (piece + 1) * HEAD_DIM]
 
 
-def combined(refs, group):
+def merge_weights(refs, groups):
     tokens = refs[0].shape[1] // (HEAD_DIM + PARTS) * HEAD_DIM
-    lse = []
-    for ref in refs:
-        tall = tall_parts(ref, group, tokens, tokens)
-        lse.append(tall[:, 0:1] + tall[:, 1:2] + tall[:, 2:3])
-    top = lse[0]
-    for other in lse[1:]:
-        top = jnp.maximum(top, other)
-    weights = [jnp.exp(one - top) for one in lse]
-    total = sum(weights[1:], weights[0])
-    scale = 1.0 / total
+    found = []
+    for group in range(groups):
+        flats = [flat_parts(ref, group, tokens, tokens) for ref in refs]
+        lse = [one[0:1] + one[1:2] + one[2:3] for one in flats]
+        top = lse[0]
+        for other in lse[1:]:
+            top = jnp.maximum(top, other)
+        weights = [jnp.exp(one - top) for one in lse]
+        total = sum(weights[1:], weights[0])
+        scale = 1.0 / total
+        lines = [weight * scale for weight in weights]
+        lines.append(jnp.zeros((PARTS - len(lines), tokens), F32))
+        found.append((jnp.transpose(jnp.concatenate(lines, axis=0)), top + jnp.log(total)))
+    return tokens, found
+
+
+def merged_rows(refs, group, tokens, weights):
     rows = [
-        (weight * scale) * ref[group, 0:tokens, :].astype(F32)
-        for weight, ref in zip(weights, refs)
+        weights[:, at : at + 1] * ref[group, 0:tokens, :].astype(F32)
+        for at, ref in enumerate(refs)
     ]
-    return sum(rows[1:], rows[0]), top + jnp.log(total)
+    return sum(rows[1:], rows[0]).astype(BF)
 
 
 def pair_kernel(a, b, out):
-    tokens = out.shape[1] // (HEAD_DIM + PARTS) * HEAD_DIM
-    for group in range(out.shape[0]):
-        rows, lse = combined((a, b), group)
-        out[group, 0:tokens, :] = rows.astype(BF)
+    tokens, found = merge_weights((a, b), out.shape[0])
+    for group, (weights, lse) in enumerate(found):
         put_parts(out, group, tokens, lse)
+    for group, (weights, lse) in enumerate(found):
+        out[group, 0:tokens, :] = merged_rows((a, b), group, tokens, weights)
 
 
 def final_kernel(a, b, c, mixed, total_lse):
-    for group in range(mixed.shape[0]):
-        rows, lse = combined((a, b, c), group)
-        mixed[group] = rows.astype(BF)
+    tokens, found = merge_weights((a, b, c), mixed.shape[0])
+    for group, (weights, lse) in enumerate(found):
         put_parts(total_lse, group, 0, lse)
+    for group, (weights, lse) in enumerate(found):
+        mixed[group] = merged_rows((a, b, c), group, tokens, weights)
 
 
 def backward_kernel(
@@ -989,15 +1000,17 @@
     b_up = vector(4 * shard, wide)
     b_down = vector(4 * shard + wide, shard)
     m_pair = lax.all_gather(
-        jnp.concatenate([w_qk.astype(BF), w_value.astype(BF)], axis=1), "seq", axis=0, tiled=True
-    )
+        jnp.concatenate([w.astype(BF) for w in (w_qk, w_value, w_out)], axis=1),
+        "seq",
+        axis=0,
+        tiled=True,
+    )
+    m_pair, m_out = m_pair[:, : 2 * features], m_pair[:, 2 * features :]
     half = HEADS * wide
     up_cols = jnp.transpose(
         w_up.astype(BF).reshape(shard, HEADS, ROUNDS, wide), (2, 0, 1, 3)
     ).reshape(ROUNDS, shard, half)
-    out_rows = jnp.broadcast_to(w_out.astype(BF), (ROUNDS, shard, features))
-    near_rows = exchange(jnp.concatenate([up_cols, out_rows], axis=2), rows_of())
-    near_rows = near_rows.reshape(ROUNDS * shard, half + features)
+    near_rows = exchange(up_cols, rows_of()).reshape(ROUNDS * shard, half)
     b_up = lax.dynamic_index_in_dim(
         b_up.reshape(HEADS, ROUNDS, wide), place % ROUNDS, axis=1, keepdims=False
     ).reshape(HEADS * wide)
@@ -1025,7 +1038,7 @@
     mixed, total_lse = merge_final(sent[0], swap(sent[1], 1), swap(far, 2))
     mixed = exchange(mixed, columns())
     m_ffn, normed_one = lax.optimization_barrier((m_ffn, normed_one))
-    m_up, m_out, m_down = (m_ffn[:, at : at + features] for at in (0, half, half + features))
+    m_up, m_down = m_ffn[:, :half], m_ffn[:, half:]
     grad_hidden = outer_cols(grad_f_all, m_down)
     mixed, grad_hidden, total_lse = lax.optimization_barrier(
         (mixed, grad_hidden, gather_group(total_lse))
@@ -1054,6 +1067,7 @@
     hidden, grad_pre = (jnp.concatenate([found[0][at], found[1][at]]) for at in range(2))
     grad_down = inner_rows(hidden, grad_f_all)
     grad_bias_down = jnp.sum(grad_f.astype(F32), axis=0)
+    normed_all, normed_col = lax.optimization_barrier((normed_all, normed_col))
     grad_up = inner_rows(normed_all, grad_pre)
     grad_bias_up = jnp.sum(grad_pre.astype(F32), axis=0)
     grad_two = sum_group([*found[0][2:], *found[1][2:]])

time: 479 us -> 495 us (1.033)
  waiting for transfers between devices: 202 us -> 227 us
  Pallas kernels: 81.3 us -> 74 us
    ppermute x33, waiting for transfers between devices: 104 us -> 128 us  [swap(): return lax.ppermute(x, 'seq', peers(mask))]
    all_gather x1, waiting for transfers between devices: 28.3 us -> 36.5 us  [shards_fast(): lax.all_gather(jnp.concatenate([w.astype(BF) for w in (w_qk, w_value, w_o...]
    pallas_call x4, Pallas kernels: 81.3 us -> 74 us  [run_kernel(): pl.pallas_call(kernel, out_shape=tuple((jax.ShapeDtypeStruct(shape, BF) f...]
    unnamed x137 -> x131, local copies, waits for them, and re-layouts: 12.8 us -> 14.4 us
  transfers between devices with their start and end apart: 44 -> 44, of which waited for: 25 -> 26; matrix products, arithmetic and copies ran while one was open for 21% -> 18% of each run, Pallas kernels for 17% -> 15%
where the time goes in v7:
time: 495 us; the launch traced here: 489 us
  waiting for transfers between devices  227 us (46%)
  Pallas kernels  74 us (15%)
  starting transfers between devices  50.8 us (10%)
  matrix products  48.3 us (10%)
  other arithmetic  40.9 us (8%)
  local copies, waits for them, and re-layouts  32.5 us (7%)
  between operations  15.4 us (3%)
    ppermute x33, waiting for transfers between devices, swap(): return lax.ppermute(x, 'seq', peers(mask))  128 us
    pallas_call x4, Pallas kernels, run_kernel(): pl.pallas_call(kernel, out_shape=tuple((jax.ShapeDtypeStruct(shape, BF) f...  74 us
    all_to_all x7, waiting for transfers between devices, exchange(): lax.all_to_all(x, 'seq', split_axis=0, concat_axis=0, tiled=True, axis_in...  62.5 us
    all_gather x1, waiting for transfers between devices, shards_fast(): lax.all_gather(jnp.concatenate([w.astype(BF) for w in (w_qk, w_value, w_o...  36.5 us
    all_to_all x7, starting transfers between devices, exchange(): lax.all_to_all(x, 'seq', split_axis=0, concat_axis=0, tiled=True, axis_in...  31.5 us
    dot_general x5, matrix products, linear(): return jnp.dot(matrix_a, matrix_b, preferred_element_type=jnp.float32)  19.1 us
    ppermute x33, starting transfers between devices, swap(): return lax.ppermute(x, 'seq', peers(mask))  18.4 us
    dot_general x5, matrix products, outer_cols(): lax.dot_general(matrix_a, matrix_b, (((1,), (1,)), ((), ())), preferred_e...  16.3 us
  transfers between devices with their start and end apart: 44, of which 26 were waited for; matrix products, arithmetic and copies ran while one was open for 18% of the time, Pallas kernels for 15%

profile of v7, /device:TPU:0, one launch (start us, length us, event | category | flops | bytes accessed | tf_op | source)
XLA Modules:
  0.0 488.6 jit_solution(5541976347004510120)
XLA Ops:
  19.0 4.9 %all-to-all-start = ((f32[32,8,256]{2,1,0:T(8,128)}), f32[32,8,256]{2,1,0:T(8,128)S(1)}, u32[]{:S(2)}, u32[]{:S(2)}) async-start(f32[32,8,256]{2,1,0:T(8,128)} %bitcast.35), calls=%async_computation | async-start | bytes 524288 | tf_op jit(solution)/shard_map/all_to_all | solution.py:918
  24.4 7.2 %collective-permute-done.1 = bf16[256,1024]{1,0:T(8,128)(2,1)} collective-permute-done((bf16[256,1024]{1,0:T(8,128)(2,1)S(1)}, bf16[256,1024]{1,0:T(8,128)(2,1)}, u32[]{:S(2)}, u32[]{:S(2)}) %collective-permute-start.1) | collective-permute-done | bytes 524320 | tf_op jit(solution)/shard_map/ppermute | solution.py:891
  32.6 5.0 %all-to-all-done.info = f32[32,8,256]{2,1,0:T(8,128)S(1)} async-done(((f32[32,8,256]{2,1,0:T(8,128)}), f32[32,8,256]{2,1,0:T(8,128)S(1)}, u32[]{:S(2)}, u32[]{:S(2)}) %all-to-all-start) | async-done | bytes 262176 | tf_op jit(solution)/shard_map/all_to_all | solution.py:918
  42.0 7.8 %all-to-all-done.1 = bf16[4,32,1024]{2,1,0:T(8,128)(2,1)S(1)} async-done(((bf16[4,32,1024]{2,1,0:T(8,128)(2,1)}), bf16[4,32,1024]{2,1,0:T(8,128)(2,1)S(1)}, u32[]{:S(2)}, u32[]{:S(2)}) %all-to-all-start.1) | async-done | bytes 262176 | tf_op jit(solution)/shard_map/all_to_all | solution.py:918
  49.8 36.5 %all-gather.4.cloned.1.call-done = bf16[1024,3072]{1,0:T(8,128)(2,1)} async-done(((bf16[32,3072]{1,0:T(8,128)(2,1)}), bf16[1024,3072]{1,0:T(8,128)(2,1)}) %all-gather.4.cloned.1.call-update) | async-done | bytes 6291472 | tf_op jit(solution)/shard_map/all_gather | solution.py:1002
  96.7 25.9 %all-to-all-done.2 = bf16[8,256,256]{2,1,0:T(8,128)(2,1)S(1)} async-done(((bf16[8,256,256]{2,1,0:T(8,128)(2,1)}), bf16[8,256,256]{2,1,0:T(8,128)(2,1)S(1)}, u32[]{:S(2)}, u32[]{:S(2)}) %all-to-all-start.2) | async-done | bytes 1048608 | tf_op jit(solution)/shard_map/all_to_all | solution.py:918
  124.7 23.0 %collective-permute-done.4.x_2 = bf16[2048,256]{1,0:T(8,128)(2,1)S(1)} collective-permute-done((bf16[2048,256]{1,0:T(8,128)(2,1)S(1)}, bf16[2048,256]{1,0:T(8,128)(2,1)S(1)}, u32[]{:S(2)}, u32[]{:S(2)}) %collective-permute-start.4) | collective-permute-done | bytes 1048608 | tf_op jit(solution)/shard_map/ppermute | solution.py:891
  151.4 33.8 %hash_forward.1 = (bf16[8,272,128]{2,1,0:T(8,128)(2,1)S(1)}, bf16[8,272,128]{2,1,0:T(8,128)(2,1)S(1)}, bf16[8,272,128]{2,1,0:T(8,128)(2,1)S(1)}, bf16[8,272,128]{2,1,0:T(8,128)(2,1)S(1)}, bf16[8256,256]{1,0:T(8,128)(2,1)}) custom-call(s32[1]{0:T(128)} %bitcast.place, bf16[2048,256]{1,0:T(8,128)(2,1)S(1)} %bitcast.169, ...), custom_call_target="tpu_custom_call" | custom-call | flops 20000000000 | bytes 12000000 | tf_op jit(solution)/shard_map/hash_forward/pallas_call | solution.py:828
  192.8 10.0 %collective-permute-done.8.c = bf16[8,272,128]{2,1,0:T(8,128)(2,1)S(1)} collective-permute-done((bf16[8,272,128]{2,1,0:T(8,128)(2,1)S(1)}, bf16[8,272,128]{2,1,0:T(8,128)(2,1)S(1)}, u32[]{:S(2)}, u32[]{:S(2)}) %collective-permute-start.8) | collective-permute-done | bytes 557088 | tf_op jit(solution)/shard_map/ppermute | solution.py:891
  204.9 4.5 all-to-all-start.3
  216.6 6.7 %fusion.27 = f32[1024,1024]{1,0:T(8,128)} fusion(bf16[1024,1024]{1,0:T(8,128)(2,1)} %constant_dynamic-update-slice_fusion, bf16[1024,2048]{1,0:T(8,128)(2,1)} %all-gather.6.cloned.1.call-done), kind=kOutput, calls=%fused_computation.41 | convolution fusion | flops 2147483648 | bytes 8388608 | tf_op jit(solution)/shard_map/dot_general | solution.py:59
  228.1 12.9 %collective-permute-done.14 = bf16[256,1024]{1,0:T(8,128)(2,1)S(1)} collective-permute-done((bf16[256,1024]{1,0:T(8,128)(2,1)S(1)}, bf16[256,1024]{1,0:T(8,128)(2,1)S(1)}, u32[]{:S(2)}, u32[]{:S(2)}) %collective-permute-start.14) | collective-permute-done | bytes 524320 | tf_op jit(solution)/shard_map/ppermute | solution.py:891
  246.1 6.2 %fusion.13 = (bf16[512,1024]{1,0:T(8,128)(2,1)S(1)}, bf16[512,1024]{1,0:T(8,128)(2,1)S(1)}, bf16[512,1024]{1,0:T(8,128)(2,1)}, bf16[512,1024]{1,0:T(8,128)(2,1)}) fusion(f32[1024,1024]{1,0:T(8,128)S(1)} %copy-done.58, f32[512,1024]{1,0:T(8,128)S(1)} %fusion.41, f32[1024]{0:T(1024)S(1)} %bitcast.232, bf16[1024,2048]{1,0:T(8,128)(2,1)S(1)} %copy-done.55, ...), kind=kOutput, calls=%fused_computation.17 | convolution fusion | flops 1099956224 | bytes 13635584 | tf_op jit(solution)/shard_map/dot_general | solution.py:49
  258.5 12.8 %collective-permute-done.17 = bf16[256,1024]{1,0:T(8,128)(2,1)} collective-permute-done((bf16[256,1024]{1,0:T(8,128)(2,1)}, bf16[256,1024]{1,0:T(8,128)(2,1)}, u32[]{:S(2)}, u32[]{:S(2)}) %collective-permute-start.17) | collective-permute-done | bytes 524320 | tf_op jit(solution)/shard_map/ppermute | solution.py:891
  292.1 11.1 %collective-permute-done.20 = bf16[1024,256]{1,0:T(8,128)(2,1)} collective-permute-done((bf16[1024,256]{1,0:T(8,128)(2,1)}, bf16[1024,256]{1,0:T(8,128)(2,1)}, u32[]{:S(2)}, u32[]{:S(2)}) %collective-permute-start.20) | collective-permute-done | bytes 524320 | tf_op jit(solution)/shard_map/ppermute | solution.py:891
  304.9 5.9 %all-to-all-start.4 = ((bf16[8,272,128]{2,1,0:T(8,128)(2,1)}), bf16[8,272,128]{2,1,0:T(8,128)(2,1)S(1)}, u32[]{:S(2)}, u32[]{:S(2)}) async-start(bf16[8,272,128]{2,1,0:T(8,128)(2,1)} %pad_maximum_fusion.6), calls=%async_computation.4 | async-start | bytes 1114112 | tf_op jit(solution)/shard_map/all_to_all | solution.py:918
  317.5 8.4 %all-to-all-done.4.g_0 = bf16[8,272,128]{2,1,0:T(8,128)(2,1)S(1)} async-done(((bf16[8,272,128]{2,1,0:T(8,128)(2,1)}), bf16[8,272,128]{2,1,0:T(8,128)(2,1)S(1)}, u32[]{:S(2)}, u32[]{:S(2)}) %all-to-all-start.4) | async-done | bytes 557088 | tf_op jit(solution)/shard_map/all_to_all | solution.py:918
  329.2 13.5 %collective-permute-done.22.g_2 = bf16[8,272,128]{2,1,0:T(8,128)(2,1)S(1)} collective-permute-done((bf16[8,272,128]{2,1,0:T(8,128)(2,1)S(1)}, bf16[8,272,128]{2,1,0:T(8,128)(2,1)S(1)}, u32[]{:S(2)}, u32[]{:S(2)}) %collective-permute-start.22) | collective-permute-done | bytes 557088 | tf_op jit(solution)/shard_map/ppermute | solution.py:891
  346.1 37.2 %hash_backward.1 = (bf16[2048,256]{1,0:T(8,128)(2,1)S(1)}, bf16[2048,256]{1,0:T(8,128)(2,1)S(1)}, bf16[2048,256]{1,0:T(8,128)(2,1)S(1)}, bf16[2048,256]{1,0:T(8,128)(2,1)}) custom-call(s32[1]{0:T(128)} %bitcast.place, bf16[8,272,128]{2,1,0:T(8,128)(2,1)S(1)} %all-to-all-done.4.g_0, bf16[8,272,128]{2,1,0:T(8,128)(2,1)S(1)} %collective-permute-done.21.g_1, ...), custom_call_target="tpu_custom_call" | custom-call | flops 20000000000 | bytes 12000000 | tf_op jit(solution)/shard_map/hash_backward/pallas_call | solution.py:828
  401.5 15.8 %collective-permute-done.25 = bf16[2048,256]{1,0:T(8,128)(2,1)S(1)} collective-permute-done((bf16[2048,256]{1,0:T(8,128)(2,1)S(1)}, bf16[2048,256]{1,0:T(8,128)(2,1)S(1)}, u32[]{:S(2)}, u32[]{:S(2)}) %collective-permute-start.25) | collective-permute-done | bytes 1048608 | tf_op jit(solution)/shard_map/ppermute | solution.py:891
  428.4 7.8 %collective-permute-done.32 = bf16[256,1024]{1,0:T(8,128)(2,1)} collective-permute-done((bf16[256,1024]{1,0:T(8,128)(2,1)}, bf16[256,1024]{1,0:T(8,128)(2,1)}, u32[]{:S(2)}, u32[]{:S(2)}) %collective-permute-start.32) | collective-permute-done | bytes 524320 | tf_op jit(solution)/shard_map/ppermute | solution.py:891
  448.5 4.7 multiply_reduce_fusion.1
  454.6 4.8 all-to-all-start.6
  462.0 15.3 %all-to-all-done.6 = bf16[32,36,256]{2,1,0:T(8,128)(2,1)S(1)} async-done(((bf16[32,36,256]{2,1,0:T(8,128)(2,1)}), bf16[32,36,256]{2,1,0:T(8,128)(2,1)S(1)}, u32[]{:S(2)}, u32[]{:S(2)}) %all-to-all-start.6) | async-done | bytes 589856 | tf_op jit(solution)/shard_map/all_to_all | solution.py:918
  (368 shorter events, 151.4 us)
Async XLA Ops:
  7.3 79.1 %all-gather.4.cloned.1.call-start = ((), (), s32[]{:S(2)}) async-start(), calls=%async_computation.8 | async-start | bytes 6488064 | tf_op jit(solution)/shard_map/all_gather | solution.py:1002
  12.9 36.9 %collective-permute-start = (bf16[256,1024]{1,0:T(8,128)(2,1)S(1)}, bf16[256,1024]{1,0:T(8,128)(2,1)S(1)}, u32[]{:S(2)}, u32[]{:S(2)}) collective-permute-start(bf16[256,1024]{1,0:T(8,128)(2,1)S(1)} %get-tuple-element.73), channel_id=1, source_target_pairs={{0,1},{1,0},{2,3},{3,2},{4,5},{5,4},{6,7},{7,6},{8,9},{9,8},{10,11... | collective-permute-start | bytes 1572872 | tf_op jit(solution)/shard_map/ppermute | solution.py:891
  13.3 18.2 %collective-permute-start.1 = (bf16[256,1024]{1,0:T(8,128)(2,1)S(1)}, bf16[256,1024]{1,0:T(8,128)(2,1)}, u32[]{:S(2)}, u32[]{:S(2)}) collective-permute-start(bf16[256,1024]{1,0:T(8,128)(2,1)S(1)} %get-tuple-element.73), channel_id=1, source_target_pairs={{0,2},{1,3},{2,0},{3,1},{4,6},{5,7},{6,4},{7,5},{8,10},{9,11},{10,... | collective-permute-start | bytes 1572872 | tf_op jit(solution)/shard_map/ppermute | solution.py:891
  19.0 18.6 %all-to-all-start = ((f32[32,8,256]{2,1,0:T(8,128)}), f32[32,8,256]{2,1,0:T(8,128)S(1)}, u32[]{:S(2)}, u32[]{:S(2)}) async-start(f32[32,8,256]{2,1,0:T(8,128)} %bitcast.35), calls=%async_computation | async-start | bytes 524288 | tf_op jit(solution)/shard_map/all_to_all | solution.py:918
  31.5 18.3 %collective-permute-start.2 = (bf16[256,1024]{1,0:T(8,128)(2,1)}, bf16[256,1024]{1,0:T(8,128)(2,1)}, u32[]{:S(2)}, u32[]{:S(2)}) collective-permute-start(bf16[256,1024]{1,0:T(8,128)(2,1)} %collective-permute-done.1), channel_id=1, source_target_pairs={{0,1},{1,0},{2,3},{3,2},{4,5},{5,4},{6,7},{7,6},{8,9},{9,8},{10,11... | collective-permute-start | bytes 1572872 | tf_op jit(solution)/shard_map/ppermute | solution.py:891
  37.6 12.2 %all-to-all-start.1 = ((bf16[4,32,1024]{2,1,0:T(8,128)(2,1)}), bf16[4,32,1024]{2,1,0:T(8,128)(2,1)S(1)}, u32[]{:S(2)}, u32[]{:S(2)}) async-start(bf16[4,32,1024]{2,1,0:T(8,128)(2,1)} %reshape.776), calls=%async_computation.1 | async-start | bytes 524288 | tf_op jit(solution)/shard_map/all_to_all | solution.py:918
  92.4 30.2 %all-to-all-start.2 = ((bf16[8,256,256]{2,1,0:T(8,128)(2,1)}), bf16[8,256,256]{2,1,0:T(8,128)(2,1)S(1)}, u32[]{:S(2)}, u32[]{:S(2)}) async-start(bf16[8,256,256]{2,1,0:T(8,128)(2,1)} %reshape.779), calls=%async_computation.2 | async-start | bytes 2097152 | tf_op jit(solution)/shard_map/all_to_all | solution.py:918
  96.4 120.2 %all-gather.6.cloned.1.call-start = ((), (), s32[]{:S(2)}) async-start(), calls=%async_computation.9 | async-start | bytes 4718592 | tf_op jit(solution)/shard_map/all_gather | solution.py:1028
  123.4 24.3 %collective-permute-start.4 = (bf16[2048,256]{1,0:T(8,128)(2,1)S(1)}, bf16[2048,256]{1,0:T(8,128)(2,1)S(1)}, u32[]{:S(2)}, u32[]{:S(2)}) collective-permute-start(bf16[2048,256]{1,0:T(8,128)(2,1)S(1)} %bitcast.167), channel_id=1, source_target_pairs={{0,2},{1,3},{2,0},{3,1},{4,6},{5,7},{6,4},{7,5},{8,10},{9,11},{10,... | collective-permute-start | bytes 3145736 | tf_op jit(solution)/shard_map/ppermute | solution.py:891
  124.7 23.1 %collective-permute-start.3 = (bf16[2048,256]{1,0:T(8,128)(2,1)S(1)}, bf16[2048,256]{1,0:T(8,128)(2,1)}, u32[]{:S(2)}, u32[]{:S(2)}) collective-permute-start(bf16[2048,256]{1,0:T(8,128)(2,1)S(1)} %bitcast.168), channel_id=1, source_target_pairs={{0,1},{1,0},{2,3},{3,2},{4,5},{5,4},{6,7},{7,6},{8,9},{9,8},{10,11... | collective-permute-start | bytes 3145736 | tf_op jit(solution)/shard_map/ppermute | solution.py:891
  188.1 14.7 %collective-permute-start.8 = (bf16[8,272,128]{2,1,0:T(8,128)(2,1)S(1)}, bf16[8,272,128]{2,1,0:T(8,128)(2,1)S(1)}, u32[]{:S(2)}, u32[]{:S(2)}) collective-permute-start(bf16[8,272,128]{2,1,0:T(8,128)(2,1)S(1)} %merge_pair.1), channel_id=1, source_target_pairs={{0,2},{1,3},{2,0},{3,1},{4,6},{5,7},{6,4},{7,5},{8,10},{9,11},{10,... | collective-permute-start | bytes 1671176 | tf_op jit(solution)/shard_map/ppermute | solution.py:891
  204.9 18.5 %all-to-all-start.3 = ((bf16[8,256,128]{2,1,0:T(8,128)(2,1)}), bf16[8,256,128]{2,1,0:T(8,128)(2,1)S(1)}, u32[]{:S(2)}, u32[]{:S(2)}) async-start(bf16[8,256,128]{2,1,0:T(8,128)(2,1)} %get-tuple-element.72), calls=%async_computation.3 | async-start | bytes 1048576 | tf_op jit(solution)/shard_map/all_to_all | solution.py:918
  209.4 95.5 %all-gather.8.cloned.1.call-start = ((), (), s32[]{:S(2)}) async-start(), calls=%async_computation.10 | async-start | bytes 4718592 | tf_op jit(solution)/shard_map/all_gather | solution.py:1046
  226.7 14.3 %collective-permute-start.14 = (bf16[256,1024]{1,0:T(8,128)(2,1)S(1)}, bf16[256,1024]{1,0:T(8,128)(2,1)S(1)}, u32[]{:S(2)}, u32[]{:S(2)}) collective-permute-start(bf16[256,1024]{1,0:T(8,128)(2,1)S(1)} %add_convert_fusion.4), channel_id=1, source_target_pairs={{0,2},{1,3},{2,0},{3,1},{4,6},{5,7},{6,4},{7,5},{8,10},{9,11},{10,... | collective-permute-start | bytes 1572872 | tf_op jit(solution)/shard_map/ppermute | solution.py:891
  227.9 13.8 %collective-permute-start.12 = (bf16[256,1024]{1,0:T(8,128)(2,1)S(1)}, bf16[256,1024]{1,0:T(8,128)(2,1)S(1)}, u32[]{:S(2)}, u32[]{:S(2)}) collective-permute-start(bf16[256,1024]{1,0:T(8,128)(2,1)S(1)} %add_convert_fusion.4), channel_id=1, source_target_pairs={{0,1},{1,0},{2,3},{3,2},{4,5},{5,4},{6,7},{7,6},{8,9},{9,8},{10,11... | collective-permute-start | bytes 1572872 | tf_op jit(solution)/shard_map/ppermute | solution.py:891
  257.1 14.2 %collective-permute-start.17 = (bf16[256,1024]{1,0:T(8,128)(2,1)}, bf16[256,1024]{1,0:T(8,128)(2,1)}, u32[]{:S(2)}, u32[]{:S(2)}) collective-permute-start(bf16[256,1024]{1,0:T(8,128)(2,1)} %fusion.47), channel_id=1, source_target_pairs={{0,2},{1,3},{2,0},{3,1},{4,6},{5,7},{6,4},{7,5},{8,10},{9,11},{10,... | collective-permute-start | bytes 1572872 | tf_op jit(solution)/shard_map/ppermute | solution.py:891
  288.5 14.7 %collective-permute-start.20 = (bf16[1024,256]{1,0:T(8,128)(2,1)}, bf16[1024,256]{1,0:T(8,128)(2,1)}, u32[]{:S(2)}, u32[]{:S(2)}) collective-permute-start(bf16[1024,256]{1,0:T(8,128)(2,1)} %add_convert_fusion.3), channel_id=1, source_target_pairs={{0,2},{1,3},{2,0},{3,1},{4,6},{5,7},{6,4},{7,5},{8,10},{9,11},{10,... | collective-permute-start | bytes 1572872 | tf_op jit(solution)/shard_map/ppermute | solution.py:891
  304.9 21.1 %all-to-all-start.4 = ((bf16[8,272,128]{2,1,0:T(8,128)(2,1)}), bf16[8,272,128]{2,1,0:T(8,128)(2,1)S(1)}, u32[]{:S(2)}, u32[]{:S(2)}) async-start(bf16[8,272,128]{2,1,0:T(8,128)(2,1)} %pad_maximum_fusion.6), calls=%async_computation.4 | async-start | bytes 1114112 | tf_op jit(solution)/shard_map/all_to_all | solution.py:918
  310.8 128.0 %reduce-scatter.2.cloned.1.call-start = ((), (), s32[]{:S(2)}) async-start(), calls=%async_computation.11 | async-start | bytes 5308416 | tf_op jit(solution)/shard_map/reduce_scatter | solution.py:1105
  327.9 14.7 %collective-permute-start.22 = (bf16[8,272,128]{2,1,0:T(8,128)(2,1)S(1)}, bf16[8,272,128]{2,1,0:T(8,128)(2,1)S(1)}, u32[]{:S(2)}, u32[]{:S(2)}) collective-permute-start(bf16[8,272,128]{2,1,0:T(8,128)(2,1)S(1)} %all-to-all-done.4.g_0), channel_id=1, source_target_pairs={{0,2},{1,3},{2,0},{3,1},{4,6},{5,7},{6,4},{7,5},{8,10},{9,11},{10,... | collective-permute-start | bytes 1671176 | tf_op jit(solution)/shard_map/ppermute | solution.py:891
  392.0 25.2 %collective-permute-start.25 = (bf16[2048,256]{1,0:T(8,128)(2,1)S(1)}, bf16[2048,256]{1,0:T(8,128)(2,1)S(1)}, u32[]{:S(2)}, u32[]{:S(2)}) collective-permute-start(bf16[2048,256]{1,0:T(8,128)(2,1)S(1)} %add_convert_fusion.1), channel_id=1, source_target_pairs={{0,2},{1,3},{2,0},{3,1},{4,6},{5,7},{6,4},{7,5},{8,10},{9,11},{10,... | collective-permute-start | bytes 3145736 | tf_op jit(solution)/shard_map/ppermute | solution.py:891
  418.8 29.5 %all-to-all-start.5 = ((bf16[8,256,256]{1,2,0:T(8,128)(2,1)}), bf16[8,256,256]{1,2,0:T(8,128)(2,1)S(1)}, u32[]{:S(2)}, u32[]{:S(2)}) async-start(bf16[8,256,256]{1,2,0:T(8,128)(2,1)} %copy.124), calls=%async_computation.5 | async-start | bytes 2097152 | tf_op jit(solution)/shard_map/all_to_all | solution.py:918
  422.7 13.5 %collective-permute-start.32 = (bf16[256,1024]{1,0:T(8,128)(2,1)}, bf16[256,1024]{1,0:T(8,128)(2,1)}, u32[]{:S(2)}, u32[]{:S(2)}) collective-permute-start(bf16[256,1024]{1,0:T(8,128)(2,1)} %get-tuple-element.106), channel_id=1, source_target_pairs={{0,2},{1,3},{2,0},{3,1},{4,6},{5,7},{6,4},{7,5},{8,10},{9,11},{10,... | collective-permute-start | bytes 1572872 | tf_op jit(solution)/shard_map/ppermute | solution.py:891
  454.6 22.8 %all-to-all-start.6 = ((bf16[32,36,256]{2,1,0:T(8,128)(2,1)}), bf16[32,36,256]{2,1,0:T(8,128)(2,1)S(1)}, u32[]{:S(2)}, u32[]{:S(2)}) async-start(bf16[32,36,256]{2,1,0:T(8,128)(2,1)} %pad_maximum_fusion.5), calls=%async_computation.7 | async-start | bytes 1310720 | tf_op jit(solution)/shard_map/all_to_all | solution.py:918
  (79 other events, 650.7 us)
Sparse Core Ops, SparseCore 0:
  11.6 74.7 all-gather.3
  123.6 72.2 all-gather.5
  228.2 74.0 all-gather.7
  328.0 93.9 reduce-scatter.1
